TPU v7x, 32 devices: a whole 2x2x4 slice. The times are simulated.
32 devices in a mesh: dp: 8 (over z, y), row: 4 (over x, core).
Axes of the slice: x: 2, y: 2, z: 4, core: 2. Of those that a mesh axis runs over, the one named last changes fastest.
Arguments:
- images: bfloat16 [16, 24, 24, 1024], P('dp', 'row'), may hold values from -6 to 6
- first_weight: bfloat16 [1024, 1024], P(('dp', 'row')), may hold values from -0.1875 to 0.1875
- conv_weight: bfloat16 [3, 3, 1024, 1024], P(None, None, ('dp', 'row')), may hold values from -0.0625 to 0.0625
- last_weight: bfloat16 [1024, 1024], P(('dp', 'row')), may hold values from -0.1875 to 0.1875
- norm_rows: bfloat16 [6, 1024], P(None, ('dp', 'row')), may hold values from -2 to 2, as said below
- read_weight: bfloat16 [1024, 4096], P(None, ('dp', 'row')), may hold values from -0.1875 to 0.1875
- read_bias: bfloat16 [4096], P(('dp', 'row')), may hold values from -3 to 3
- cotangent: bfloat16 [16, 12, 12, 4096], P('dp', 'row'), may hold values from -6 to 6
- live_count: int32 [8], P('dp'), may hold values from 1 to 2, as said below
Outputs:
- readout_out: bfloat16 [16, 12, 12, 4096], P('dp', 'row')
- image_grad: bfloat16 [16, 24, 24, 1024], P('dp', 'row')
- first_grad: float32 [1024, 1024], P(('dp', 'row'))
- conv_grad: float32 [3, 3, 1024, 1024], P(None, None, ('dp', 'row'))
- last_grad: float32 [1024, 1024], P(('dp', 'row'))
- norm_grad: float32 [6, 1024], P(None, ('dp', 'row'))
- read_grad: float32 [1024, 4096], P(None, ('dp', 'row'))
- bias_grad: float32 [4096], P(('dp', 'row'))
Inputs may be any that keep to these rules, and one draw needn't show every extreme that they name: The first live_count[g] of the 2 slots of dp group g hold images; in every draw some group has all 2 live and some group one. `norm_rows`: rows 0, 2, 4 lie in 0.5 to 1.5.
All inputs are finite; a program needn't handle non-finite values.
Results may differ from a plain program's by a relative error of at most 0.012.
Values may be sent and summed in bfloat16 or wider, within the bound.
No kernel may reach another device: no remote copies, remote signals or barrier semaphores. Data moves between devices by JAX's collectives and lax.ppermute only.
A program may use at most 192 MiB of HBM per device.

v0:
```python
import functools

import jax
import jax.numpy as jnp
from jax import lax
from jax.experimental import pallas as pl
from jax.experimental.pallas import tpu as pltpu

from jax.sharding import PartitionSpec as P

eps = 1e-06
F32 = jnp.float32
BF16 = jnp.bfloat16
RING = 8


def ring_order(n):
    return list(range(0, n, 2)) + list(range(n - 1, 0, -2))


def ring_pairs(n):
    order = ring_order(n)
    right = [(order[i], order[(i + 1) % n]) for i in range(n)]
    left = [(b, a) for a, b in right]
    return right, left


def ring_index(n, step):
    me = lax.axis_index("dp")
    place = jnp.where(me % 2 == 0, me // 2, n - 1 - me // 2)
    place = (place + step) % n
    return jnp.where(place < n // 2, 2 * place, 2 * (n - 1 - place) + 1)


def gather_dp(x, n):
    return lax.all_gather(x, "dp", axis=0, tiled=False)


def scatter_dp(parts, n):
    return lax.psum_scatter(parts.astype(F32), "dp", scatter_dimension=0, tiled=False)


def swap_row(x, q):
    return lax.ppermute(x, "row", [(i, i ^ q) for i in range(4)])


def gather_row(x):
    two = swap_row(x, 2)
    one = swap_row(x, 1)
    return [x, one, two, swap_row(two, 1)]


def exchange_row(pieces):
    return [pieces[0]] + [swap_row(pieces[q], q) for q in (1, 2, 3)]


def scatter_row(pieces):
    near = swap_row(jnp.stack([pieces[1], pieces[3]]).astype(BF16), 1).astype(F32)
    mine = pieces[0].astype(F32) + near[0]
    other = (pieces[2].astype(F32) + near[1]).astype(BF16)
    return mine + swap_row(other, 2).astype(F32)


def pick(choices, index):
    value = choices[0]
    for i in range(1, len(choices)):
        value = jnp.where(index == i, choices[i], value)
    return value


def dot(left, right):
    return jnp.dot(left, right, preferred_element_type=F32)


def dot_t(left, right):
    return lax.dot_general(left, right, (((1,), (1,)), ((), ())), preferred_element_type=F32)


def t_dot(left, right):
    return lax.dot_general(left, right, (((0,), (0,)), ((), ())), preferred_element_type=F32)


def normalize(value):
    centred = value - jnp.mean(value, axis=-1, keepdims=True)
    scale = lax.rsqrt(jnp.mean(centred * centred, axis=-1, keepdims=True) + eps)
    return centred * scale, scale


def norm_backward(grad_out, normed, scale, gain):
    weighted = grad_out * gain
    return scale * (
        weighted
        - jnp.mean(weighted, axis=-1, keepdims=True)
        - normed * jnp.mean(weighted * normed, axis=-1, keepdims=True)
    )


def silu_slope(value):
    gate = jax.nn.sigmoid(value)
    return gate * (1.0 + value * (1.0 - gate))


def gelu_slope(value):
    return (
        0.5 * (1.0 + lax.erf(value * 0.7071067811865476))
        + value * jnp.exp(-0.5 * value * value) * 0.3989422804014327
    )


def columns(value):
    cols = value.shape[2]
    wide = jnp.pad(value, ((0, 0), (1, 1), (1, 1), (0, 0)))
    return jnp.concatenate([wide[:, :, v : v + cols] for v in range(3)], axis=3)


def generic(
    images,
    first_weight,
    conv_weight,
    last_weight,
    norm_rows,
    read_weight,
    read_bias,
    cotangent,
    live_count,
):
    n, ranks = lax.axis_size("dp"), lax.axis_size("row")
    row = lax.axis_index("row")
    slots, band, cols, width = images.shape
    patches = slots * band * cols
    high = ranks * band
    own = first_weight.shape[0]
    group = n * own
    outs = read_weight.shape[1]
    rows_at = [row ^ q for q in range(ranks)]

    first_mine = first_weight.reshape(own, n, ranks, own).transpose(0, 2, 1, 3).reshape(own, width)
    small = jnp.concatenate([norm_rows.reshape(-1), read_bias])
    small = jnp.pad(small, (0, 8 * width - small.shape[0])).reshape(8, width)
    first_ring = gather_dp(jnp.concatenate([first_mine, small], axis=0), n)
    first_parts = gather_row(first_ring)

    def interleave(parts):
        whole = jnp.zeros((n, ranks) + parts[0].shape[1:], parts[0].dtype)
        for q in range(ranks):
            whole = lax.dynamic_update_slice(whole, parts[q][:, None], (0, rows_at[q], 0, 0))
        return whole

    first_all = interleave(first_parts)
    first_full = first_all[:, :, :own].reshape(width, width)
    norms = first_all[:, :, own].reshape(n, ranks, width)[:, :, : 6 * own]
    norms = norms.reshape(n, ranks, 6, own).astype(F32)
    norm_vals = norms.transpose(2, 0, 1, 3).reshape(6, width)
    norm_swap = norms.transpose(2, 1, 0, 3).reshape(6, width)
    bias_mine = first_ring[:, own, 6 * own : 6 * own + outs].reshape(n * outs).astype(F32)

    conv_taps = [gather_dp(conv_weight[u].reshape(3 * own, width), n) for u in range(3)]
    conv_taps = [
        tap.reshape(n, 3, own, width).transpose(1, 0, 2, 3).reshape(3 * group, width) for tap in conv_taps
    ]
    last_full = interleave(gather_row(gather_dp(last_weight, n))).reshape(width, width)
    read_mine = gather_dp(read_weight.T, n).reshape(n * outs, width)

    cot = cotangent.reshape(-1, n, ranks, outs)
    cot = exchange_row([pick([cot[:, :, i] for i in range(ranks)], rows_at[q]) for q in range(ranks)])
    cot = jnp.concatenate(cot, axis=0).reshape(-1, n * outs)

    flat_in = images.reshape(patches, width)
    hat_one, scale_one = normalize(dot(flat_in, first_full))
    pre_one = hat_one * norm_swap[0] + norm_swap[1]
    low_one = jax.nn.silu(pre_one).astype(BF16)
    split = [low_one[:, i * group : (i + 1) * group] for i in range(ranks)]
    bands = exchange_row([pick(split, rows_at[q]) for q in range(ranks)])

    def stack_bands(pieces):
        whole = jnp.zeros((slots, ranks, band, cols, pieces[0].shape[-1]), pieces[0].dtype)
        for q in range(ranks):
            piece = pieces[q].reshape(slots, 1, band, cols, -1)
            whole = lax.dynamic_update_slice(whole, piece, (0, rows_at[q], 0, 0, 0))
        return whole.reshape(slots, high, cols, -1)

    def take_bands(value):
        value = value.reshape(slots, ranks, band * cols, -1)
        return [
            lax.dynamic_index_in_dim(value, rows_at[q], 1, keepdims=False).reshape(patches, -1)
            for q in range(ranks)
        ]

    wide_one = columns(stack_bands(bands))
    slabs = [wide_one[:, u : u + high].reshape(slots * high * cols, 3 * group) for u in range(3)]
    act_two = dot(slabs[0], conv_taps[0]) + dot(slabs[1], conv_taps[1]) + dot(slabs[2], conv_taps[2])
    hat_two, scale_two = normalize(scatter_row(take_bands(act_two)))
    pre_two = hat_two * norm_vals[2] + norm_vals[3]
    low_two = jax.nn.silu(pre_two).astype(BF16)
    hat_three, scale_three = normalize(dot(low_two, last_full))
    summed = flat_in.astype(F32) + (hat_three * norm_vals[4] + norm_vals[5])
    pooled = jnp.mean(summed.reshape(slots, band // 2, 2, cols // 2, 2, width), axis=(2, 4)).astype(BF16)
    pooled = pooled.reshape(-1, width)
    pools = jnp.concatenate(gather_row(pooled), axis=0)
    logits = dot_t(pools, read_mine) + bias_mine
    mask = (jnp.arange(slots, dtype=jnp.int32) < live_count[0]).astype(F32)
    mask = jnp.broadcast_to(mask[None, :, None], (ranks, slots, pooled.shape[0] // slots)).reshape(-1, 1)
    shown = (jax.nn.gelu(logits, approximate=False) * mask).astype(BF16)
    shown = exchange_row(jnp.split(shown, ranks, axis=0))
    readout = jnp.zeros((pooled.shape[0], n, ranks, outs), BF16)
    for q in range(ranks):
        readout = lax.dynamic_update_slice(
            readout, shown[q].reshape(-1, n, 1, outs), (0, 0, rows_at[q], 0)
        )
    readout_out = readout.reshape(slots, band // 2, cols // 2, n * ranks * outs)

    grad_low = (cot.astype(F32) * mask * gelu_slope(logits)).astype(BF16)
    read_terms = t_dot(grad_low, pools).reshape(n, outs, width)
    bias_terms = jnp.sum(grad_low.astype(F32), axis=0).reshape(n, 1, outs)
    bias_terms = jnp.pad(bias_terms, ((0, 0), (0, 7), (0, width - outs)))
    read_sum = scatter_dp(jnp.concatenate([read_terms, bias_terms], axis=1), n)
    read_grad, bias_grad = read_sum[:outs].T, read_sum[outs, :outs]
    grad_pool = scatter_row(jnp.split(dot(grad_low, read_mine), ranks, axis=0))
    grad_sum = (
        jnp.broadcast_to(
            grad_pool.reshape(slots, band // 2, 1, cols // 2, 1, width),
            (slots, band // 2, 2, cols // 2, 2, width),
        )
        * 0.25
    ).reshape(-1, width)
    gain_three = jnp.sum(grad_sum * hat_three, axis=0)
    shift_three = jnp.sum(grad_sum, axis=0)
    grad_three = norm_backward(grad_sum, hat_three, scale_three, norm_vals[4]).astype(BF16)
    grad_pre_two = dot_t(grad_three, last_full) * silu_slope(pre_two)
    gain_two = jnp.sum(grad_pre_two * hat_two, axis=0)
    shift_two = jnp.sum(grad_pre_two, axis=0)
    grad_two = norm_backward(grad_pre_two, hat_two, scale_two, norm_vals[2]).astype(BF16)
    grad_full = stack_bands(gather_row(grad_two))
    grad_flat = grad_full.reshape(-1, width)

    def row_sums(terms):
        terms = terms.reshape(n, ranks, -1, width)
        return scatter_row(
            [lax.dynamic_index_in_dim(terms, rows_at[q], 1, keepdims=False) for q in range(ranks)]
        )

    conv_grad = []
    for u in range(3):
        terms = t_dot(slabs[u], grad_flat).reshape(3, n, own, width).transpose(1, 0, 2, 3)
        conv_grad.append(scatter_dp(terms.reshape(n, 3 * own, width), n).reshape(3, own, width))
    conv_grad = jnp.stack(conv_grad)
    wide_grad = jnp.pad(grad_full, ((0, 0), (1, 1), (1, 1), (0, 0)))
    grad_mid = jnp.zeros((slots * high * cols, group), F32)
    for u in range(3):
        for v in range(3):
            slab = wide_grad[:, 2 - u : 2 - u + high, 2 - v : 2 - v + cols].reshape(-1, width)
            grad_mid = grad_mid + dot_t(slab, conv_taps[u][v * group : (v + 1) * group])
    pieces = exchange_row(take_bands(grad_mid.astype(BF16)))
    grad_low_one = jnp.concatenate(
        [pick([pieces[i ^ q] for i in range(ranks)], row) for q in range(ranks)], axis=1
    ).astype(F32)
    last_sum = scatter_dp(row_sums(t_dot(low_two, grad_three)), n)

    grad_pre_one = grad_low_one * silu_slope(pre_one)
    gain_one = jnp.sum(grad_pre_one * hat_one, axis=0)
    shift_one = jnp.sum(grad_pre_one, axis=0)
    grad_one = norm_backward(grad_pre_one, hat_one, scale_one, norm_swap[0]).astype(BF16)
    image_grad = (grad_sum + dot_t(grad_one, first_full)).astype(BF16)
    image_grad = image_grad.reshape(slots, band, cols, width)

    swapped = jnp.stack([gain_one, shift_one]).reshape(2, ranks, n, own).transpose(2, 1, 0, 3)
    plain = jnp.stack([gain_two, shift_two, gain_three, shift_three])
    plain = plain.reshape(4, n, ranks, own).transpose(1, 2, 0, 3)
    norm_terms = jnp.concatenate([swapped, plain], axis=2).reshape(n, ranks, 1, 6 * own)
    norm_terms = jnp.pad(norm_terms, ((0, 0), (0, 0), (0, 7), (0, width - 6 * own)))
    first_terms = t_dot(flat_in, grad_one).reshape(n, ranks, own, width)
    first_sum = scatter_dp(row_sums(jnp.concatenate([first_terms, norm_terms], axis=2)), n)
    norm_grad = first_sum[own, : 6 * own].reshape(6, own)
    first_grad = first_sum[:own].reshape(own, ranks, n, own).transpose(0, 2, 1, 3).reshape(own, width)
    return (
        readout_out,
        image_grad,
        first_grad,
        conv_grad,
        last_sum,
        norm_grad,
        read_grad,
        bias_grad,
    )


VM = pl.BlockSpec(memory_space=pltpu.VMEM)
SM = pl.BlockSpec(memory_space=pltpu.SMEM)
HB = pl.BlockSpec(memory_space=pltpu.HBM)


def shape(dims, dtype):
    return jax.ShapeDtypeStruct(dims, dtype)


def kernel(body, outs, ins, scratch, flops, moved, *arrays, specs=None, room=24):
    return pl.pallas_call(
        body,
        out_shape=outs,
        in_specs=ins,
        out_specs=jax.tree.map(lambda _: VM, outs) if specs is None else specs,
        scratch_shapes=scratch,
        cost_estimate=pl.CostEstimate(flops=flops // 64, bytes_accessed=moved // 64, transcendentals=0),
        compiler_params=pltpu.CompilerParams(vmem_limit_bytes=room << 20),
    )(*arrays)


def at_row(where, q):
    return where[0] ^ q


def start_all(copies):
    for copy in copies:
        copy.start()


def wait_all(copies):
    for copy in copies:
        copy.wait()


def copies_of(pairs, sems):
    return [pltpu.make_async_copy(a, b, sems.at[i]) for i, (a, b) in enumerate(pairs)]


def hop(x, turn):
    right, left = ring_pairs(RING)
    return lax.ppermute(x, "dp", right if turn else left)


def gather_step(state, step, low=None, high=None):
    pieces, a, b = state
    pieces = list(pieces)
    if step < RING // 2:
        a, b = hop(a, True), hop(b, False)
        pieces[RING - step], pieces[step] = a, b
    else:
        pieces[step] = (hop(low(a), True), hop(high(b), False))
    return pieces, a, b


def gather_state(x):
    return [x] * RING, x, x


def scatter_step(low, high, terms, a, b, step):
    half = RING // 2
    if step == half:
        return hop(low, True), hop(high, False)
    right, left = terms[step].astype(F32), terms[RING - step].astype(F32)
    if step == half - 1:
        cut = low.shape[0]
        right = jnp.concatenate([right[:cut] + a.astype(F32), right[cut:]], axis=0)
        left = jnp.concatenate([left[:cut], left[cut:] + b.astype(F32)], axis=0)
    else:
        right, left = right + a.astype(F32), left + b.astype(F32)
    return hop(right.astype(BF16), True), hop(left.astype(BF16), False)


def scatter_end(terms, a, b):
    return terms[0].astype(F32) + a.astype(F32) + b.astype(F32)


def fence(*values):
    return lax.optimization_barrier(values)


def line_up(where, *refs):
    pieces, (first, last) = refs[: RING + 1], refs[RING + 1 :]
    rows = last.shape[1]
    for k in range(RING):
        if k == RING // 2:
            last[where[2 + k]] = pieces[k][...]
            first[where[2 + k]] = pieces[RING][...]
        else:
            last[where[2 + k]] = pieces[k][:rows]
            first[where[2 + k]] = pieces[k][rows:]


def fill(where, weight, parts):
    rows = weight.shape[2]
    for q, part in enumerate(parts):
        weight[:, at_row(where, q)] = part[:, :rows, :]


def center(value):
    mean = jnp.mean(value, axis=-1, keepdims=True)
    gap = value - mean
    scale = lax.rsqrt(jnp.mean(gap * gap, axis=-1, keepdims=True) + eps)
    return gap * scale, scale


def flat_pieces(pieces):
    half = RING // 2
    return [p[0] if k == half else p for k, p in enumerate(pieces)] + [pieces[half][1]]


def stage_one(where, x, f0, f1, f2, f3, hat, scale, s0, s1, s2, s3, norms, weight, low):
    firsts = (f0, f1, f2, f3)
    fill(where, weight, firsts)
    width, rows = x.shape[1], weight.shape[2]
    total = jnp.zeros((8, width), F32)
    bias = total
    for q, first in enumerate(firsts):
        for k in range(RING):
            block = first[k, rows:, :].astype(F32)
            total = total + block
            if q == 0:
                bias = bias + block
    line = lax.broadcasted_iota(jnp.int32, (8, width), 0)
    table = jnp.where(line == 6, bias, total)
    norms[...] = table
    act = dot(x[...], weight[...].reshape(width, width))
    normed, root = center(act)
    hat[...] = normed
    scale[...] = root
    pre = normed * norms[0:1, :] + norms[1:2, :]
    low[...] = (pre * jax.nn.sigmoid(pre)).astype(BF16)
    part = width // 4
    for q, out in enumerate((s0, s1, s2, s3)):
        out[...] = low[:, pl.ds(pl.multiple_of(at_row(where, q) * part, part), part)]


def conv_copies(where, pieces, weight, sems):
    far = RING // 2
    pairs = []
    for k in range(RING):
        if k == far:
            number = pieces[far].shape[0]
            pairs.append((pieces[far], weight.at[pl.ds(0, number), where[2 + k]]))
            pairs.append((pieces[RING], weight.at[pl.ds(number, pieces[RING].shape[0]), where[2 + k]]))
        else:
            pairs.append((pieces[k], weight.at[:, where[2 + k]]))
    return copies_of(pairs, sems)


def conv_forward(dims, first, where, s0, s1, s2, s3, *refs):
    slots, rows, cols = dims
    if first:
        own, near, spans, weight, pad, moved, wide, sems, done = refs[RING + 1 :]
        copies = conv_copies(where, refs[: RING + 1], weight, sems)
        start_all(copies)
    else:
        weight, own, near, spans, pad, moved, wide, done = refs
    group = s0.shape[1]
    patches = rows * cols
    band = patches // 4
    pad[...] = jnp.zeros_like(pad)
    for q, piece in enumerate((s0, s1, s2, s3)):
        for i in range(slots):
            at = pl.multiple_of(cols + 8 + at_row(where, q) * band, 8)
            pad[i, pl.ds(at, band), :] = piece[i * band : (i + 1) * band, :].astype(F32)
    for v in range(3):
        for i in range(slots):
            shifted = pad[i, 8 + v - 1 : 8 + v - 1 + patches + 2 * cols, :]
            if v != 1:
                col = lax.broadcasted_iota(jnp.int32, shifted.shape, 0) % cols
                shifted = jnp.where(col == (0 if v == 0 else cols - 1), 0.0, shifted)
            moved[i] = shifted

        @pl.loop(0, 2 * slots)
        def _(j):
            q, i = j // slots, j % slots
            here = pl.ds(pl.multiple_of(j * band, 16), band)
            for u in range(3):
                at = pl.multiple_of(at_row(where, first + q) * band + u * cols, 8)
                t = u * 3 + v
                wide[here, t * group : (t + 1) * group] = moved[i, pl.ds(at, band), :].astype(BF16)

    keep = pltpu.make_async_copy(wide, spans, done)
    keep.start()
    if first:
        wait_all(copies)
    width = own.shape[1]
    chunk = 256
    patches = slots * band

    @pl.loop(0, width // chunk)
    def _(j):
        lanes = pl.ds(pl.multiple_of(j * chunk, chunk), chunk)
        terms = dot(wide[...], weight[:, :, :, lanes].reshape(-1, chunk))
        own[:, lanes] = terms[:patches]
        near[:, lanes] = terms[patches:].astype(BF16)

    keep.wait()


def stage_two(dims, where, own, near, cross, x, norms, l0, l1, l2, l3, hat_two, scale_two, low, hat, scale, pooled, weight, pairs):
    slots, rows, cols = dims
    fill(where, weight, (l0, l1, l2, l3))
    width = x.shape[1]
    act = own[...] + near[...].astype(F32) + cross[...].astype(F32)
    normed, root = center(act)
    hat_two[...] = normed
    scale_two[...] = root
    pre = normed * norms[2:3, :] + norms[3:4, :]
    low[...] = (pre * jax.nn.sigmoid(pre)).astype(BF16)
    normed, root = center(dot(low[...], weight[...].reshape(width, width)))
    hat[...] = normed
    scale[...] = root
    y = x[...].astype(F32) + (normed * norms[4:5, :] + norms[5:6, :])
    y = jnp.sum(y.reshape(slots * rows // 2, 2, cols, width), axis=1).reshape(-1, width)
    count = pooled.shape[0]
    for g in range(pairs.shape[0]):
        lanes = slice(g * 128, (g + 1) * 128)
        pairs[g] = y[:, lanes]
        pooled[:, lanes] = (
            0.25 * (pairs[g, pl.ds(0, count, stride=2), :] + pairs[g, pl.ds(1, count, stride=2), :])
        ).astype(BF16)


def read_copies(where, pieces, weight, sems):
    half = RING // 2
    pairs = []
    for k in range(RING):
        if k == half:
            rows = pieces[half].shape[0]
            pairs.append((pieces[half], weight.at[where[2 + k], pl.ds(0, rows)]))
            pairs.append((pieces[RING], weight.at[where[2 + k], pl.ds(rows, rows)]))
        else:
            pairs.append((pieces[k], weight.at[where[2 + k]]))
    return copies_of(pairs, sems)


def readout(slots, where, p0, p1, p2, p3, c0, c1, c2, c3, norms, *refs):
    pieces = refs[: RING + 1]
    o0, o1, o2, o3, low, own, near, far, weight, sems = refs[RING + 1 :]
    copies = read_copies(where, pieces, weight, sems)
    start_all(copies)
    count, width = p0.shape
    table = jnp.concatenate([p[...] for p in (p0, p1, p2, p3)], axis=0)
    line = lax.broadcasted_iota(jnp.int32, (count, width), 0)
    mask = jnp.where(line // (count // slots) < where[1], 1.0, 0.0)
    wait_all(copies)
    whole = weight[...].reshape(-1, width)
    logits = dot_t(table, whole) + norms[6:7, :]
    for q, (cot, out) in enumerate(((c0, o0), (c1, o1), (c2, o2), (c3, o3))):
        z = logits[q * count : (q + 1) * count]
        phi = 0.5 * (1.0 + lax.erf(z * 0.7071067811865476))
        out[...] = (z * phi * mask).astype(BF16)
        slope = phi + z * jnp.exp(-0.5 * z * z) * 0.3989422804014327
        low[q * count : (q + 1) * count, :] = (cot[...].astype(F32) * mask * slope).astype(BF16)
    back = dot(low[...], whole)
    own[...] = back[:count]
    near[0] = back[count : 2 * count].astype(BF16)
    far[...] = back[2 * count : 3 * count]
    near[1] = back[3 * count :].astype(BF16)


def readout_terms(where, low, p0, p1, p2, p3, upper, lower, out, terms):
    width = p0.shape[1]
    table = jnp.concatenate([p[...] for p in (p0, p1, p2, p3)], axis=0)
    terms[...] = t_dot(low[...], table).reshape(terms.shape)
    bias = jnp.sum(low[...].astype(F32), axis=0, keepdims=True)
    rows = terms.shape[1]
    for k in range(RING):
        out[k, :rows, :] = terms[where[2 + k]].astype(BF16)
        out[k, rows:, :] = jnp.broadcast_to(bias, (out.shape[1] - rows, width)).astype(BF16)
    upper[...] = out[RING // 2, : upper.shape[0]]
    lower[...] = out[RING // 2, upper.shape[0] :]


def spread(pairs, grad, dims):
    slots, rows, cols = dims
    count, width = grad.shape
    for g in range(pairs.shape[0]):
        lanes = slice(g * 128, (g + 1) * 128)
        pairs[g, pl.ds(0, count, stride=2), :] = grad[:, lanes]
        pairs[g, pl.ds(1, count, stride=2), :] = grad[:, lanes]
    half = slots * rows // 2
    both = jnp.concatenate([pairs[g] for g in range(pairs.shape[0])], axis=1)
    both = jnp.broadcast_to(both.reshape(half, 1, cols, width), (half, 2, cols, width))
    return both.reshape(-1, width) * 0.25


def back_norm(grad, normed, root, gain):
    weighted = grad * gain
    return root * (
        weighted
        - jnp.mean(weighted, axis=-1, keepdims=True)
        - normed * jnp.mean(weighted * normed, axis=-1, keepdims=True)
    )


def total_rows(value):
    return jnp.sum(value, axis=0, keepdims=True)


def stage_two_back(dims, where, own, near, cross, hat, scale, hat_two, scale_two, norms, weight, grad_three, grad_two, pool_sum, sums, pairs):
    width = hat.shape[1]
    grad = own[...] + near[...].astype(F32) + cross[...].astype(F32)
    pool_sum[...] = grad
    gy = spread(pairs, grad, dims)
    sums[...] = jnp.zeros_like(sums)
    sums[4:5, :] = total_rows(gy * hat[...])
    sums[5:6, :] = total_rows(gy)
    grad_three[...] = back_norm(gy, hat[...], scale[...], norms[4:5, :]).astype(BF16)
    gs = dot_t(grad_three[...], weight[...].reshape(width, width))
    pre = hat_two[...] * norms[2:3, :] + norms[3:4, :]
    gn = gs * silu_slope(pre)
    sums[2:3, :] = total_rows(gn * hat_two[...])
    sums[3:4, :] = total_rows(gn)
    grad_two[...] = back_norm(gn, hat_two[...], scale_two[...], norms[2:3, :]).astype(BF16)


def last_terms(where, low, grad, own, near, far, terms):
    terms[...] = t_dot(low[...], grad[...]).reshape(terms.shape)
    for k in range(RING):
        own[k] = terms[where[2 + k], at_row(where, 0)]
        near[0, k] = terms[where[2 + k], at_row(where, 1)].astype(BF16)
        far[k] = terms[where[2 + k], at_row(where, 2)]
        near[1, k] = terms[where[2 + k], at_row(where, 3)].astype(BF16)


def stack_grad(dims, where, pieces, whole):
    slots, rows, cols = dims
    band = rows * cols // 4
    for q, piece in enumerate(pieces):
        for i in range(slots):
            at = pl.multiple_of(i * rows * cols + at_row(where, q) * band, 16)
            whole[pl.ds(at, band), :] = piece[i * band : (i + 1) * band, :]


def conv_half_terms(where, here, g0, g1, out, one):
    count = g0.shape[0]
    one[:count], one[count:] = g0[...], g1[...]
    group = out.shape[1]

    @pl.loop(0, out.shape[0])
    def _(t):
        lanes = pl.ds(pl.multiple_of(t * group, group), group)
        out[t] = t_dot(here[:, lanes], one[...])


def conv_terms(first, number, next_to, where, half, there, g2, g3, *refs):
    parts, (far, side, out, two) = refs[:-4], refs[-4:]
    count = g2.shape[0]
    two[:count], two[count:] = g2[...], g3[...]
    rows, width = out.shape[2:]
    group = RING * rows

    @pl.loop(0, number)
    def _(t):
        lanes = pl.ds(pl.multiple_of((first + t) * group, group), group)
        terms = half[first + t] + t_dot(there[:, lanes], two[...])
        terms = terms.astype(BF16).reshape(RING, rows, width)
        for k in range(RING):
            out[where[2 + RING + k], t] = terms[k]

    if parts:
        own, near, low, high = parts
        half_way = RING // 2
        for a, b, cross in ((0, half_way, low), (half_way, RING, high)):
            out[a:b, number] = (own[a:b] + near[0, a:b].astype(F32) + cross[...].astype(F32)).astype(BF16)
    far[...] = out[RING // 2]
    side[...] = out[next_to]


def conv_back(dims, where, g0, g1, g2, g3, weight, o0, o1, o2, o3, whole, held, low):
    slots, rows, cols = dims
    stack_grad(dims, where, (g0, g1, g2, g3), whole)
    patches = rows * cols
    band = patches // 4
    group = o0.shape[1]
    width = whole.shape[1]
    held[...] = jnp.zeros_like(held)
    @pl.loop(0, 3)
    def _(u):
        at = pl.ds(pl.multiple_of(8 + u * cols, 8), patches)
        for v in range(3):
            part = dot_t(whole[...], weight[u * 3 + v].reshape(group, width))
            for i in range(slots):
                held[v, i, at, :] += part[i * patches : (i + 1) * patches]

    col = lax.broadcasted_iota(jnp.int32, (patches, group), 0) % cols
    for i in range(slots):
        value = held[1, i, 8 + cols : 8 + cols + patches, :]
        value += jnp.where(col == cols - 1, 0.0, held[0, i, 9 + cols : 9 + cols + patches, :])
        value += jnp.where(col == 0, 0.0, held[2, i, 7 + cols : 7 + cols + patches, :])
        low[i * patches : (i + 1) * patches, :] = value.astype(BF16)
    for q, out in enumerate((o0, o1, o2, o3)):
        for i in range(slots):
            at = pl.multiple_of(i * patches + at_row(where, q) * band, 16)
            out[i * band : (i + 1) * band, :] = low[pl.ds(at, band), :]


def stage_one_back(where, b0, b1, b2, b3, hat, scale, norms, x, sums, grad_one, own, near, far, low, terms):
    width = hat.shape[1]
    part = width // 4
    for q, piece in enumerate((b0, b1, b2, b3)):
        low[:, pl.ds(pl.multiple_of(at_row(where, q) * part, part), part)] = piece[...]
    pre = hat[...] * norms[0:1, :] + norms[1:2, :]
    gn = low[...].astype(F32) * silu_slope(pre)
    line = lax.broadcasted_iota(jnp.int32, (8, width), 0)
    tail = jnp.where(line == 0, total_rows(gn * hat[...]), jnp.where(line == 1, total_rows(gn), sums[...]))
    grad_one[...] = back_norm(gn, hat[...], scale[...], norms[0:1, :]).astype(BF16)
    terms[...] = t_dot(x[...], grad_one[...]).reshape(terms.shape)
    rows = terms.shape[2]
    for k in range(RING):
        own[k, :rows] = terms[where[2 + k], at_row(where, 0)]
        near[0, k, :rows] = terms[where[2 + k], at_row(where, 1)].astype(BF16)
        far[k, :rows] = terms[where[2 + k], at_row(where, 2)]
        near[1, k, :rows] = terms[where[2 + k], at_row(where, 3)].astype(BF16)
        own[k, rows:] = tail
        near[0, k, rows:] = tail.astype(BF16)
        far[k, rows:] = tail
        near[1, k, rows:] = tail.astype(BF16)


def image_back(dims, where, grad_one, pool_sum, weight, out, pairs):
    width = grad_one.shape[1]
    gy = spread(pairs, pool_sum[...], dims)
    out[...] = (gy + dot_t(grad_one[...], weight[...].reshape(width, width))).astype(BF16)


def split_columns(where, x, o0, o1, o2, o3):
    lanes = x.shape[1] // (4 * RING)
    for q, out in enumerate((o0, o1, o2, o3)):
        for g in range(RING):
            at = pl.multiple_of((g * 4 + at_row(where, q)) * lanes, lanes)
            out[:, g * lanes : (g + 1) * lanes] = x[:, pl.ds(at, lanes)]


def join_columns(where, i0, i1, i2, i3, out):
    lanes = out.shape[1] // (4 * RING)
    for q, piece in enumerate((i0, i1, i2, i3)):
        for g in range(RING):
            at = pl.multiple_of((g * 4 + at_row(where, q)) * lanes, lanes)
            out[:, pl.ds(at, lanes)] = piece[:, g * lanes : (g + 1) * lanes]


def ringed(
    images,
    first_weight,
    conv_weight,
    last_weight,
    norm_rows,
    read_weight,
    read_bias,
    cotangent,
    live_count,
):
    dp, row = lax.axis_index("dp"), lax.axis_index("row")
    slots, band, cols, width = images.shape
    dims = (slots, band, cols)
    full = (slots, 4 * band, cols)
    patches = slots * band * cols
    count = patches // 4
    own = first_weight.shape[0]
    group = RING * own
    outs = read_weight.shape[1]
    taps = 9
    DMA = pltpu.SemaphoreType.DMA
    index = jnp.arange(18, dtype=jnp.int32)
    place_of = lambda d: jnp.where(d % 2 == 0, d // 2, RING - 1 - d // 2)
    place = (place_of(dp) + index - 2) % RING
    ahead = jnp.where(place < RING // 2, 2 * place, 2 * (RING - 1 - place) + 1)
    steps = (place_of(index - 10) - place_of(dp)) % RING
    where = jnp.where(index == 0, row, jnp.where(index == 1, live_count[0], jnp.where(index < 10, ahead, steps)))
    where = where.astype(jnp.int32)

    first_mine = first_weight.reshape(own, RING, 4, own).transpose(0, 2, 1, 3).reshape(own, width)
    lane = jnp.arange(width, dtype=jnp.int32)[None, :]
    tiled = jnp.tile(norm_rows, (1, width // own))
    at = jnp.where(jnp.arange(6)[:, None] < 2, row * RING + dp, dp * 4 + row)
    small = jnp.where(lane // own == at, tiled, 0).astype(BF16)
    bias = jnp.where(lane // outs == dp, jnp.tile(read_bias, width // outs)[None, :], 0).astype(BF16)
    small = jnp.concatenate([small, bias, jnp.zeros((1, width), BF16)], axis=0)
    first_mine = jnp.concatenate([first_mine, small], axis=0)
    conv = conv_weight.reshape(taps, own, width)
    quarter = shape((count, width), BF16)
    wide_f32, thin_f32, wide_bf16 = (
        shape((patches, width), F32),
        shape((patches, 1), F32),
        shape((patches, width), BF16),
    )
    quarter_f32, near_quarter = shape((count, width), F32), shape((2, count, width), BF16)
    piece = shape((patches, group), BF16)
    block = (RING, own, width)
    matmul = 2 * patches * width * width
    square = 2 * width * width
    square_of = shape((RING, 4, own, width), BF16)
    total = 4 * patches
    pad_rows = full[1] * cols + 2 * cols + 16
    pair_scratch = pltpu.VMEM((width // 128, patches // 2, 128), F32)
    x = images.reshape(patches, width)

    far = RING // 2
    cut = own + 8
    low, high = lambda v: v[:own], lambda v: v[own:]
    more = gather_step(gather_state(conv), 1)
    ring = gather_step(gather_state(jnp.concatenate([last_weight, first_mine], axis=0)), 1)
    read = read_weight.T
    cots = cotangent.reshape(count, -1)
    more, ring, where, read, cots, x = fence(more, ring, where, read, cots, x)
    ring = gather_step(ring, 2)
    cots = kernel(split_columns, [quarter] * 4, [SM, VM], [], 0, 2 * count * 4 * width * 2, where, cots)
    ring, cots = fence(ring, cots)
    ring = gather_step(ring, 3)
    ring = fence(ring)[0]
    ring = gather_step(ring, 4, low, high)
    more, ring = fence(more, ring)
    ring = ring[0]
    firsts, lasts = kernel(
        line_up,
        [shape((RING, cut, width), BF16), shape((RING, own, width), BF16)],
        [SM] + [VM] * (RING + 1),
        [],
        0,
        4 * RING * (cut + own) * width,
        where,
        *flat_pieces(ring),
    )
    more = gather_step(more, 2)
    first_two, first_one = swap_row(firsts, 2), swap_row(firsts, 1)
    more, firsts, first_two, first_one, lasts = fence(more, firsts, first_two, first_one, lasts)
    more = gather_step(more, 3)
    firsts = [firsts, first_one, first_two, swap_row(first_two, 1)]
    last_two, last_one = swap_row(lasts, 2), swap_row(lasts, 1)
    hat_one, scale_one, *lows, norms, first_full = kernel(
        stage_one,
        [wide_f32, thin_f32] + [piece] * 4 + [shape((8, width), F32), square_of],
        [SM] + [VM] * 5,
        [pltpu.VMEM((patches, width), BF16)],
        matmul,
        square + 8 * patches * width,
        where,
        x,
        *firsts,
    )
    more, lows, lasts, last_two, last_one = fence(more, lows, lasts, last_two, last_one)
    taps_half = (taps + 1) // 2
    more = gather_step(more, 4, lambda v: v[:taps_half], lambda v: v[taps_half:])
    lows = exchange_row(lows)
    lasts = [lasts, last_one, last_two, swap_row(last_two, 1)]
    weights = flat_pieces(more[0])
    weights, lows, lasts, read, cots = fence(weights, lows, lasts, read, cots)

    conv_whole = (taps, RING, own, width)

    def conv_half(first, weights):
        return kernel(
            functools.partial(conv_forward, full, first),
            [wide_f32, wide_bf16, shape((2 * patches, taps * group), BF16)]
            + ([shape(conv_whole, BF16)] if first else []),
            [SM] + [VM] * 4 + ([HB] * (RING + 1) if first else [VM]),
            [
                pltpu.VMEM((slots, pad_rows, group), F32),
                pltpu.VMEM((slots, pad_rows - 16, group), F32),
                pltpu.VMEM((2 * patches, taps * group), BF16),
            ]
            + ([DMA((RING + 1,))] if first else [])
            + [DMA],
            9 * matmul // 2,
            9 * square + 6 * patches * width + 4 * patches * taps * group,
            where,
            *lows,
            *weights,
            specs=[VM, VM, HB] + ([VM] if first else []),
        )

    read = gather_step(gather_state(read), 1)
    cots = exchange_row(cots)
    away, near, spans_far, conv_full = conv_half(2, weights)
    away, near, read, cots = fence(away, near, read, cots)
    other = (away + swap_row(near, 1).astype(F32)).astype(BF16)
    other, lows, read = fence(other, lows, read)
    cross = swap_row(other, 2)
    read = gather_step(read, 2)
    mine, near, spans_near = conv_half(0, (conv_full,))
    near = fence(near, mine)[0]
    near = swap_row(near, 1)
    mine, near, cross = fence(mine, near, cross)
    read = gather_step(read, 3)
    hat_two, scale_two, low_two, hat_three, scale_three, pooled, last_full = kernel(
        functools.partial(stage_two, dims),
        [wide_f32, thin_f32, wide_bf16, wide_f32, thin_f32, quarter, square_of],
        [SM] + [VM] * 9,
        [pair_scratch],
        matmul,
        square + 24 * patches * width,
        where,
        mine,
        near,
        cross,
        x,
        norms,
        *lasts,
    )
    read = gather_step(read, 4, lambda v: v[: outs // 2], lambda v: v[outs // 2 :])
    pool_two, pool_one = swap_row(pooled, 2), swap_row(pooled, 1)
    pooled, pool_two, pool_one = fence(pooled, pool_two, pool_one)
    pools = [pooled, pool_one, pool_two, swap_row(pool_two, 1)]
    *shown, grad_low, mine, near, away = kernel(
        functools.partial(readout, slots),
        [quarter] * 4 + [wide_bf16, quarter_f32, near_quarter, quarter_f32],
        [SM] + [VM] * 9 + [HB] * (RING + 1),
        [pltpu.VMEM((RING, outs, width), BF16), DMA((RING + 1,))],
        2 * matmul,
        square + 12 * patches * width,
        where,
        *pools,
        *cots,
        norms,
        *flat_pieces(read[0]),
    )

    near = swap_row(near, 1)
    other = (away + near[1].astype(F32)).astype(BF16)
    other, grad_low, near = fence(other, grad_low, near)
    cross = swap_row(other, 2)
    half_read = shape(((outs + 16) // 2, width), BF16)
    *read_far, read_terms = kernel(
        readout_terms,
        [half_read, half_read, shape((RING, outs + 16, width), BF16)],
        [SM] + [VM] * 5,
        [pltpu.VMEM((RING, outs, width), F32)],
        matmul,
        2 * square,
        where,
        grad_low,
        *pools,
    )
    cross, read_far, read_terms, near = fence(cross, read_far, read_terms, near)
    read_a, read_b = scatter_step(*read_far, read_terms, None, None, 4)
    grad_three, grad_two, pool_sum, sums = kernel(
        functools.partial(stage_two_back, dims),
        [wide_bf16, wide_bf16, quarter_f32, shape((8, width), F32)],
        [SM] + [VM] * 9,
        [pair_scratch],
        matmul,
        square + 14 * patches * width,
        where,
        mine,
        near[0],
        cross,
        hat_three,
        scale_three,
        hat_two,
        scale_two,
        norms,
        last_full,
    )
    grad_three, grad_two, read_a, read_b = fence(grad_three, grad_two, read_a, read_b)
    grad_far, grad_next = swap_row(grad_two, 2), swap_row(grad_two, 1)
    read_a, read_b = scatter_step(*read_far, read_terms, read_a, read_b, 3)
    read_a, read_b = scatter_step(*read_far, read_terms, read_a, read_b, 2)
    here = kernel(
        conv_half_terms,
        shape((taps, group, width), F32),
        [SM] + [VM] * 3,
        [pltpu.VMEM((2 * patches, width), BF16)],
        9 * matmul // 2,
        18 * square,
        where,
        spans_near,
        grad_two,
        grad_next,
    )
    last_own, last_near, last_far = kernel(
        last_terms,
        [shape(block, F32), shape((2,) + block, BF16), shape(block, F32)],
        [SM, VM, VM],
        [pltpu.VMEM((RING, 4, own, width), F32)],
        matmul,
        3 * square,
        where,
        low_two,
        grad_three,
    )
    grad_two, grad_far, grad_next, last_near, last_far, read_a, read_b, here = fence(
        grad_two, grad_far, grad_next, last_near, last_far, read_a, read_b, here
    )
    grads = [grad_two, grad_next, grad_far, swap_row(grad_far, 1)]
    last_near = swap_row(last_near, 1)
    last_low = (last_far[:far] + last_near[1, :far].astype(F32)).astype(BF16)
    last_high = (last_far[far:] + last_near[1, far:].astype(F32)).astype(BF16)
    grads, last_near, last_low, last_high = fence(grads, last_near, last_low, last_high)
    last_low = swap_row(last_low, 2)
    read_a, read_b = scatter_step(*read_far, read_terms, read_a, read_b, 1)

    def weight_terms(first, number, next_to, parts):
        held = number + len(parts) // 4
        some = shape((held, own, width), BF16)
        return kernel(
            functools.partial(conv_terms, first, number, next_to),
            [some, some, shape((RING, held, own, width), BF16)],
            [SM] + [VM] * (4 + len(parts)),
            [pltpu.VMEM((2 * patches, width), BF16)],
            matmul * number,
            2 * square * number,
            where,
            here,
            spans_far,
            *grads[2:],
            *parts,
        )

    def add_to(terms, k, value):
        return (terms[k % RING].astype(F32) + value.astype(F32)).astype(BF16)

    one_far, one_side, one = weight_terms(0, 5, 5, ())
    one_far, one_side, one, grads, last_low, last_high, read_a, read_b = fence(
        one_far, one_side, one, grads, last_low, last_high, read_a, read_b
    )
    last_high = swap_row(last_high, 2)
    one_a, one_b = hop(one_far, True), hop(one_side, False)
    backs = kernel(
        functools.partial(conv_back, full),
        [piece] * 4,
        [SM] + [VM] * 5,
        [
            pltpu.VMEM((total, width), BF16),
            pltpu.VMEM((3, slots, pad_rows, group), F32),
            pltpu.VMEM((total, group), BF16),
        ],
        9 * matmul,
        9 * square + 12 * patches * width,
        where,
        *grads,
        conv_full,
    )
    one_a, one_b, backs, grads, last_high = fence(one_a, one_b, backs, grads, last_high)
    one_a, one_b = hop(add_to(one, 3, one_a), True), hop(add_to(one, -2, one_b), False)
    backs = exchange_row(backs)
    two_far, two_side, two = weight_terms(5, 4, 3, (last_own, last_near, last_low, last_high))
    one_a, one_b, two_far, two_side, two, backs = fence(one_a, one_b, two_far, two_side, two, backs)
    two_a, two_b = hop(two_side, True), hop(two_far, False)
    one_a, one_b = add_to(one, 2, one_a), add_to(one, -1, one_b)
    block = (RING, own + 8, width)
    grad_one, first_own, first_near, first_far = kernel(
        stage_one_back,
        [wide_bf16, shape(block, F32), shape((2,) + block, BF16), shape(block, F32)],
        [SM] + [VM] * 9,
        [pltpu.VMEM((patches, width), BF16), pltpu.VMEM((RING, 4, own, width), F32)],
        matmul,
        3 * square + 8 * patches * width,
        where,
        *backs,
        hat_one,
        scale_one,
        norms,
        x,
        sums,
    )
    one_a, one_b, two_a, two_b, grad_one, first_own, first_near, first_far, shown = fence(
        one_a, one_b, two_a, two_b, grad_one, first_own, first_near, first_far, shown
    )
    one_a, one_b = hop(one_a, True), hop(one_b, False)
    two_a, two_b = add_to(two, 2, two_a), add_to(two, -3, two_b)
    first_near = swap_row(first_near, 1)
    shown = exchange_row(shown)
    first_low = (first_far[:far] + first_near[1, :far].astype(F32)).astype(BF16)
    first_high = (first_far[far:] + first_near[1, far:].astype(F32)).astype(BF16)
    one_a, one_b_end, two_a, two_b, first_near, first_low, first_high, shown = fence(
        one_a, one_b, two_a, two_b, first_near, first_low, first_high, shown
    )
    two_a, two_b = hop(two_a, True), hop(two_b, False)
    one_a = add_to(one, 1, one_a)
    first_high = swap_row(first_high, 2)
    image_grad = kernel(
        functools.partial(image_back, dims),
        wide_bf16,
        [SM, VM, VM, VM],
        [pair_scratch],
        matmul,
        square + 8 * patches * width,
        where,
        grad_one,
        pool_sum,
        first_full,
    ).reshape(slots, band, cols, width)
    one_a, two_a, two_b, first_low, first_high, image_grad = fence(
        one_a, two_a, two_b, first_low, first_high, image_grad
    )
    one_a, two_b = hop(one_a, True), hop(add_to(two, -2, two_b), False)
    first_low = swap_row(first_low, 2)
    first_high = (first_own[far:] + first_near[0, far:].astype(F32) + first_high.astype(F32)).astype(BF16)
    two_a = add_to(two, 1, fence(two_a, first_high)[0])
    one_a, two_a, two_b, first_low, first_high, shown = fence(one_a, two_a, two_b, first_low, first_high, shown)
    first_a, first_b = hop(first_high[0], True), hop(first_high[1], False)
    two_a, two_b = hop(two_a, True), hop(add_to(two, -1, two_b), False)
    first_low = (first_own[:far] + first_near[0, :far].astype(F32) + first_low.astype(F32)).astype(BF16)
    readout_out = kernel(
        join_columns,
        shape((count, 4 * width), BF16),
        [SM] + [VM] * 4,
        [],
        0,
        16 * count * width,
        where,
        *shown,
    ).reshape(slots, band // 2, cols // 2, 4 * width)
    read_sum = scatter_end(read_terms, read_a, read_b)
    two_a, two_b, first_a, first_b, first_low, readout_out, read_sum = fence(
        two_a, two_b, first_a, first_b, first_low, readout_out, read_sum
    )
    first_a, first_b = hop(add_to(first_low, 3, first_a), True), hop(add_to(first_high[far - 2 :], 0, first_b), False)
    read_grad, bias_row = read_sum[:outs].T, read_sum[outs]
    bias_grad = lax.dynamic_slice_in_dim(bias_row, dp * outs, outs)
    first_a, first_b, read_grad = fence(first_a, first_b, read_grad)
    first_a, first_b = hop(add_to(first_low, 2, first_a), True), hop(add_to(first_high[far - 1 :], 0, first_b), False)
    two_sum = scatter_end(two, two_a, two_b)
    conv_grad = jnp.concatenate([scatter_end(one, one_a, one_b_end), two_sum[:4]], axis=0)
    conv_grad = conv_grad.reshape(3, 3, own, width)
    first_a, first_b, conv_grad = fence(first_a, first_b, conv_grad)
    first_a = hop(add_to(first_low, 1, first_a), True)
    tail = first_low[0].astype(F32) + first_a.astype(F32) + first_b.astype(F32)
    first_grad = tail[:own].reshape(own, 4, RING, own).transpose(0, 2, 1, 3).reshape(own, width)
    last_grad = two_sum[4]
    swapped = lax.dynamic_slice(tail, (own, (row * RING + dp) * own), (2, own))
    plain = lax.dynamic_slice(tail, (own + 2, (dp * 4 + row) * own), (4, own))
    norm_grad = jnp.concatenate([swapped, plain], axis=0)
    return (
        readout_out,
        image_grad,
        first_grad,
        conv_grad,
        last_grad,
        norm_grad,
        read_grad,
        bias_grad,
    )


def per_device(*arrays):
    if lax.axis_size("dp") == RING and lax.axis_size("row") == 4:
        return ringed(*arrays)
    return generic(*arrays)


def solution(mesh):
    return jax.shard_map(
        per_device,
        mesh=mesh,
        in_specs=(
            P("dp", "row", None, None),
            P(("dp", "row"), None),
            P(None, None, ("dp", "row"), None),
            P(("dp", "row"), None),
            P(None, ("dp", "row")),
            P(None, ("dp", "row")),
            P(("dp", "row")),
            P("dp", "row", None, None),
            P("dp"),
        ),
        out_specs=(
            P("dp", "row", None, None),
            P("dp", "row", None, None),
            P(("dp", "row"), None),
            P(None, None, ("dp", "row"), None),
            P(("dp", "row"), None),
            P(None, ("dp", "row")),
            P(None, ("dp", "row")),
            P(("dp", "row")),
        ),
        check_vma=False,
    )
```

profile of v0, /device:TPU:0, one launch (start us, length us, event | category | flops | bytes accessed | tf_op | source)
XLA Modules:
  0.0 276.6 jit_solution(16738548308374224661)
XLA Ops:
  0.7 3.1 %collective-permute-start.1 = (bf16[9,32,1024]{2,1,0:T(8,128)(2,1)}, bf16[9,32,1024]{2,1,0:T(8,128)(2,1)S(1)}, u32[]{:S(2)}, u32[]{:S(2)}) collective-permute-start(bf16[9,32,1024]{2,1,0:T(8,128)(2,1)} %bitcast.146), channel_id=1, source_target_pairs={{0,8},{8,16},{16,24},{24,28},{28,20},{20,12},{12,4},{4,0},{1,9},{9... | collective-permute-start | bytes 1769480 | tf_op jit(solution)/shard_map/ppermute | solution.py:328
  7.0 2.1 collective-permute-start.3
  13.3 7.0 %collective-permute-done.3.refs_7_ = bf16[72,1024]{1,0:T(8,128)(2,1)S(1)} collective-permute-done((bf16[72,1024]{1,0:T(8,128)(2,1)S(1)}, bf16[72,1024]{1,0:T(8,128)(2,1)S(1)}, u32[]{:S(2)}, u32[]{:S(2)}) %collective-permute-start.3) | collective-permute-done | bytes 147488 | tf_op jit(solution)/shard_map/ppermute | solution.py:328
  22.2 1.7 collective-permute-start.5
  24.6 2.4 collective-permute-done.4.refs_2_
  27.4 1.7 collective-permute-start.6
  29.4 3.1 %collective-permute-done.6.refs_3_ = bf16[72,1024]{1,0:T(8,128)(2,1)S(1)} collective-permute-done((bf16[72,1024]{1,0:T(8,128)(2,1)S(1)}, bf16[72,1024]{1,0:T(8,128)(2,1)S(1)}, u32[]{:S(2)}, u32[]{:S(2)}) %collective-permute-start.6) | collective-permute-done | bytes 147488 | tf_op jit(solution)/shard_map/ppermute | solution.py:328
  32.5 1.7 collective-permute-done.7.refs_5_
  34.2 1.6 collective-permute-start.9
  36.2 3.8 %collective-permute-done.8.refs_4_ = bf16[32,1024]{1,0:T(8,128)(2,1)S(1)} collective-permute-done((bf16[32,1024]{1,0:T(8,128)(2,1)S(1)}, bf16[32,1024]{1,0:T(8,128)(2,1)S(1)}, u32[]{:S(2)}, u32[]{:S(2)}) %collective-permute-start.8) | collective-permute-done | bytes 65568 | tf_op jit(solution)/shard_map/ppermute | solution.py:328
  42.3 1.8 collective-permute-start.10
  44.3 13.4 %collective-permute-done.10.refs_2_ = bf16[9,32,1024]{2,1,0:T(8,128)(2,1)S(1)} collective-permute-done((bf16[9,32,1024]{2,1,0:T(8,128)(2,1)S(1)}, bf16[9,32,1024]{2,1,0:T(8,128)(2,1)S(1)}, u32[]{:S(2)}, u32[]{:S(2)}) %collective-permute-start.10) | collective-permute-done | bytes 589856 | tf_op jit(solution)/shard_map/ppermute | solution.py:328
  57.7 1.8 collective-permute-done.11.refs_6_
  59.6 1.8 collective-permute-start.14
  62.2 2.0 shard_map.154
  64.3 11.7 %collective-permute-done.17.l2 = bf16[8,32,1024]{2,1,0:T(8,128)(2,1)S(1)} collective-permute-done((bf16[8,32,1024]{2,1,0:T(8,128)(2,1)S(1)}, bf16[8,32,1024]{2,1,0:T(8,128)(2,1)S(1)}, u32[]{:S(2)}, u32[]{:S(2)}) %collective-permute-start.17) | collective-permute-done | bytes 524320 | tf_op jit(solution)/shard_map/ppermute | solution.py:44
  77.5 1.7 collective-permute-start.20
  80.6 5.4 %collective-permute-done.22.s2 = bf16[288,256]{1,0:T(8,128)(2,1)S(1)} collective-permute-done((bf16[288,256]{1,0:T(8,128)(2,1)S(1)}, bf16[288,256]{1,0:T(8,128)(2,1)S(1)}, u32[]{:S(2)}, u32[]{:S(2)}) %collective-permute-start.22) | collective-permute-done | bytes 147488 | tf_op jit(solution)/shard_map/ppermute | solution.py:44
  87.4 1.8 collective-permute-start.25
  91.1 5.9 %shard_map.155 = (f32[288,1024]{1,0:T(8,128)S(1)}, bf16[288,1024]{1,0:T(8,128)(2,1)S(1)}, bf16[576,2304]{1,0:T(8,128)(2,1)S(1)}, bf16[9,8,32,1024]{3,2,1,0:T(8,128)(2,1)S(1)}) custom-call(s32[18]{0:T(128)S(1)} %compare_select_fusion.10.where, bf16[288,256]{1,0:T(8,128)(2,1)S(1)} %get-tuple-element.413.s0, bf16[288,256]{1,0:T(8,128)(2,1)S(1)} %collective-permute-done.21.s1, ...), custom_call_target="tpu_custom_call" | custom-call | flops 42467328 | bytes 364032 | tf_op jit(solution)/shard_map/pallas_call | solution.py:297
  98.5 1.6 collective-permute-done.30
  100.9 5.4 %shard_map.156 = (f32[288,1024]{1,0:T(8,128)S(1)}, bf16[288,1024]{1,0:T(8,128)(2,1)S(1)}, bf16[576,2304]{1,0:T(8,128)(2,1)S(1)}) custom-call(s32[18]{0:T(128)S(1)} %compare_select_fusion.10.where, bf16[288,256]{1,0:T(8,128)(2,1)S(1)} %get-tuple-element.413.s0, bf16[288,256]{1,0:T(8,128)(2,1)S(1)} %collective-permute-done.21.s1, ...), custom_call_target="tpu_custom_call" | custom-call | flops 42467328 | bytes 364032 | tf_op jit(solution)/shard_map/pallas_call | solution.py:297
  108.6 6.6 %collective-permute-done.36.refs_2_ = bf16[128,1024]{1,0:T(8,128)(2,1)S(1)} collective-permute-done((bf16[128,1024]{1,0:T(8,128)(2,1)S(1)}, bf16[128,1024]{1,0:T(8,128)(2,1)S(1)}, u32[]{:S(2)}, u32[]{:S(2)}) %collective-permute-start.36) | collective-permute-done | bytes 262176 | tf_op jit(solution)/shard_map/ppermute | solution.py:328
  117.2 2.3 shard_map.157
  119.6 1.6 collective-permute-start.33
  121.2 4.7 %collective-permute-done.33.p2 = bf16[72,1024]{1,0:T(8,128)(2,1)S(1)} collective-permute-done((bf16[72,1024]{1,0:T(8,128)(2,1)S(1)}, bf16[72,1024]{1,0:T(8,128)(2,1)S(1)}, u32[]{:S(2)}, u32[]{:S(2)}) %collective-permute-start.33) | collective-permute-done | bytes 147488 | tf_op jit(solution)/shard_map/ppermute | solution.py:44
  128.0 3.8 %collective-permute-done.41.refs_8_ = bf16[64,1024]{1,0:T(8,128)(2,1)S(1)} collective-permute-done((bf16[64,1024]{1,0:T(8,128)(2,1)S(1)}, bf16[64,1024]{1,0:T(8,128)(2,1)S(1)}, u32[]{:S(2)}, u32[]{:S(2)}) %collective-permute-start.41) | collective-permute-done | bytes 131104 | tf_op jit(solution)/shard_map/ppermute | solution.py:328
  133.0 3.1 %shard_map.158 = (bf16[72,1024]{1,0:T(8,128)(2,1)S(1)}, bf16[72,1024]{1,0:T(8,128)(2,1)S(1)}, bf16[72,1024]{1,0:T(8,128)(2,1)S(1)}, bf16[72,1024]{1,0:T(8,128)(2...) custom-call(s32[18]{0:T(128)S(1)} %compare_select_fusion.10.where, ...), custom_call_target="tpu_custom_call" | custom-call | flops 18874368 | bytes 88064 | tf_op jit(solution)/shard_map/pallas_call | solution.py:297
  136.2 1.6 collective-permute-done.42
  139.0 2.2 shard_map.159
  141.2 2.6 collective-permute-done.43.cross
  145.8 2.6 shard_map.160
  150.1 1.8 collective-permute-start.50
  153.4 3.5 %collective-permute-done.48 = bf16[144,1024]{1,0:T(8,128)(2,1)S(1)} collective-permute-done((bf16[144,1024]{1,0:T(8,128)(2,1)S(1)}, bf16[144,1024]{1,0:T(8,128)(2,1)S(1)}, u32[]{:S(2)}, u32[]{:S(2)}) %collective-permute-start.48) | collective-permute-done | bytes 294944 | tf_op jit(solution)/shard_map/ppermute | solution.py:328
  157.2 1.9 collective-permute-start.51
  159.2 2.1 shard_map.161
  161.3 6.0 %shard_map.162.half = f32[9,256,1024]{2,1,0:T(8,128)S(1)} custom-call(s32[18]{0:T(128)S(1)} %compare_select_fusion.10.where, bf16[576,2304]{1,0:T(8,128)(2,1)S(1)} %get-tuple-element.472.here, bf16[288,1024]{1,0:T(8,128)(2,1)S(1)} %get-tuple-element.494.g0, bf16[288,1024]{1,0:T(8,128)(2,1)S(1)} %collective-permute-done.47.g1), custom_call_target="tpu_custom_call" | custom-call | flops 42467328 | bytes 589824 | tf_op jit(solution)/shard_map/pallas_call | solution.py:297
  168.3 1.7 collective-permute-start.56
  172.6 3.7 %shard_map.163 = (bf16[5,32,1024]{2,1,0:T(8,128)(2,1)S(1)}, bf16[5,32,1024]{2,1,0:T(8,128)(2,1)S(1)}, bf16[8,5,32,1024]{3,2,1,0:T(8,128)(2,1)S(1)}) custom-call(s32[18]{0:T(128)S(1)} %compare_select_fusion.10.where, f32[9,256,1024]{2,1,0:T(8,128)S(1)} %shard_map.162.half, bf16[576,2304]{1,0:T(8,128)(2,1)S(1)} %get-tuple-element.474.there, ...), custom_call_target="tpu_custom_call" | custom-call | flops 47185920 | bytes 327680 | tf_op jit(solution)/shard_map/pallas_call | solution.py:297
  179.8 1.7 collective-permute-start.58
  183.0 8.0 %shard_map.164 = (bf16[288,256]{1,0:T(8,128)(2,1)S(1)}, bf16[288,256]{1,0:T(8,128)(2,1)S(1)}, bf16[288,256]{1,0:T(8,128)(2,1)S(1)}, bf16[288,256]{1,0:T(8,128)(2,1)S(1)}) custom-call(s32[18]{0:T(128)S(1)} %compare_select_fusion.10.where, bf16[288,1024]{1,0:T(8,128)(2,1)S(1)} %get-tuple-element.494.g0, bf16[288,1024]{1,0:T(8,128)(2,1)S(1)} %collective-permute-done.47.g1, ...), custom_call_target="tpu_custom_call" | custom-call | flops 84934656 | bytes 350208 | tf_op jit(solution)/shard_map/pallas_call | solution.py:297
  191.3 1.7 collective-permute-start.61
  195.3 3.3 %shard_map.165 = (bf16[5,32,1024]{2,1,0:T(8,128)(2,1)S(1)}, bf16[5,32,1024]{2,1,0:T(8,128)(2,1)S(1)}, bf16[8,5,32,1024]{3,2,1,0:T(8,128)(2,1)S(1)}) custom-call(s32[18]{0:T(128)S(1)} %compare_select_fusion.10.where, f32[9,256,1024]{2,1,0:T(8,128)S(1)} %shard_map.162.half, bf16[576,2304]{1,0:T(8,128)(2,1)S(1)} %get-tuple-element.474.there, ...), custom_call_target="tpu_custom_call" | custom-call | flops 37748736 | bytes 262144 | tf_op jit(solution)/shard_map/pallas_call | solution.py:297
  200.1 2.4 collective-permute-done.64.b3
  202.8 1.7 collective-permute-start.66
  204.5 3.2 %shard_map.166 = (bf16[288,1024]{1,0:T(8,128)(2,1)S(1)}, f32[8,40,1024]{2,1,0:T(8,128)S(1)}, bf16[2,8,40,1024]{3,2,1,0:T(8,128)(2,1)S(1)}, f32[8,40,1024]{2,1,0:T(8,128)S(1)}) custom-call(s32[18]{0:T(128)S(1)} %compare_select_fusion.10.where, bf16[288,256]{1,0:T(8,128)(2,1)S(1)} %get-tuple-element.522.b0, bf16[288,256]{1,0:T(8,128)(2,1)S(1)} %collective-permute-done.62.b1, ...), custom_call_target="tpu_custom_call" | custom-call | flops 9437184 | bytes 135168 | tf_op jit(solution)/shard_map/pallas_call | solution.py:297
  207.9 4.4 %collective-permute-done.65 = bf16[5,32,1024]{2,1,0:T(8,128)(2,1)S(1)} collective-permute-done((bf16[5,32,1024]{2,1,0:T(8,128)(2,1)S(1)}, bf16[5,32,1024]{2,1,0:T(8,128)(2,1)S(1)}, u32[]{:S(2)}, u32[]{:S(2)}) %collective-permute-start.65) | collective-permute-done | bytes 327712 | tf_op jit(solution)/shard_map/ppermute | solution.py:328
  217.0 1.7 collective-permute-done.71.i2
  218.6 3.2 %collective-permute-done.72.i3 = bf16[72,1024]{1,0:T(8,128)(2,1)S(1)} collective-permute-done((bf16[72,1024]{1,0:T(8,128)(2,1)S(1)}, bf16[72,1024]{1,0:T(8,128)(2,1)S(1)}, u32[]{:S(2)}, u32[]{:S(2)}) %collective-permute-start.72) | collective-permute-done | bytes 147488 | tf_op jit(solution)/shard_map/ppermute | solution.py:44
  223.4 1.6 collective-permute-start.73
  226.3 2.2 shard_map.167
  229.3 2.3 collective-permute-done.73
  234.4 1.7 collective-permute-start.77
  237.4 2.1 fusion.18
  239.5 2.2 collective-permute-done.77
  241.8 1.7 collective-permute-done.76
  243.8 1.7 collective-permute-start.82
  245.9 1.9 fusion.4
  247.8 1.7 collective-permute-start.80
  253.2 2.0 collective-permute-done.80
  255.2 1.7 collective-permute-done.79
  257.8 1.7 collective-permute-start.84
  265.4 1.6 collective-permute-start.86
  272.7 1.7 collective-permute-done.87
  (226 shorter events, 81.5 us)
Async XLA Ops:
  0.7 21.2 %collective-permute-start.1 = (bf16[9,32,1024]{2,1,0:T(8,128)(2,1)}, bf16[9,32,1024]{2,1,0:T(8,128)(2,1)S(1)}, u32[]{:S(2)}, u32[]{:S(2)}) collective-permute-start(bf16[9,32,1024]{2,1,0:T(8,128)(2,1)} %bitcast.146), channel_id=1, source_target_pairs={{0,8},{8,16},{16,24},{24,28},{28,20},{20,12},{12,4},{4,0},{1,9},{9... | collective-permute-start | bytes 1769480 | tf_op jit(solution)/shard_map/ppermute | solution.py:328
  3.7 18.2 %collective-permute-start = (bf16[9,32,1024]{2,1,0:T(8,128)(2,1)}, bf16[9,32,1024]{2,1,0:T(8,128)(2,1)S(1)}, u32[]{:S(2)}, u32[]{:S(2)}) collective-permute-start(bf16[9,32,1024]{2,1,0:T(8,128)(2,1)} %bitcast.147), channel_id=1, source_target_pairs={{8,0},{16,8},{24,16},{28,24},{20,28},{12,20},{4,12},{0,4},{9,1},{1... | collective-permute-start | bytes 1769480 | tf_op jit(solution)/shard_map/ppermute | solution.py:328
  7.0 13.4 %collective-permute-start.3 = (bf16[72,1024]{1,0:T(8,128)(2,1)S(1)}, bf16[72,1024]{1,0:T(8,128)(2,1)S(1)}, u32[]{:S(2)}, u32[]{:S(2)}) collective-permute-start(bf16[72,1024]{1,0:T(8,128)(2,1)S(1)} %concatenate.17.refs_0_), channel_id=1, source_target_pairs={{0,8},{8,16},{16,24},{24,28},{28,20},{20,12},{12,4},{4,0},{1,9},{9... | collective-permute-start | bytes 442376 | tf_op jit(solution)/shard_map/ppermute | solution.py:328
  9.0 12.9 %collective-permute-start.2 = (bf16[72,1024]{1,0:T(8,128)(2,1)S(1)}, bf16[72,1024]{1,0:T(8,128)(2,1)S(1)}, u32[]{:S(2)}, u32[]{:S(2)}) collective-permute-start(bf16[72,1024]{1,0:T(8,128)(2,1)S(1)} %concatenate.17.refs_0_), channel_id=1, source_target_pairs={{8,0},{16,8},{24,16},{28,24},{20,28},{12,20},{4,12},{0,4},{9,1},{1... | collective-permute-start | bytes 442376 | tf_op jit(solution)/shard_map/ppermute | solution.py:328
  34.2 5.9 %collective-permute-start.9 = (bf16[40,1024]{1,0:T(8,128)(2,1)S(1)}, bf16[40,1024]{1,0:T(8,128)(2,1)S(1)}, u32[]{:S(2)}, u32[]{:S(2)}) collective-permute-start(bf16[40,1024]{1,0:T(8,128)(2,1)S(1)} %slice.191), channel_id=1, source_target_pairs={{8,0},{16,8},{24,16},{28,24},{20,28},{12,20},{4,12},{0,4},{9,1},{1... | collective-permute-start | bytes 245768 | tf_op jit(solution)/shard_map/ppermute | solution.py:328
  40.6 18.9 %collective-permute-start.13 = (bf16[8,40,1024]{2,1,0:T(8,128)(2,1)S(1)}, bf16[8,40,1024]{2,1,0:T(8,128)(2,1)S(1)}, u32[]{:S(2)}, u32[]{:S(2)}) collective-permute-start(bf16[8,40,1024]{2,1,0:T(8,128)(2,1)S(1)} %get-tuple-element.357.f0), channel_id=1, source_target_pairs={{0,1},{1,0},{2,3},{3,2},{4,5},{5,4},{6,7},{7,6},{8,9},{9,8},{10,11... | collective-permute-start | bytes 1966088 | tf_op jit(solution)/shard_map/ppermute | solution.py:44
  40.7 18.8 %collective-permute-start.12 = (bf16[8,40,1024]{2,1,0:T(8,128)(2,1)S(1)}, bf16[8,40,1024]{2,1,0:T(8,128)(2,1)S(1)}, u32[]{:S(2)}, u32[]{:S(2)}) collective-permute-start(bf16[8,40,1024]{2,1,0:T(8,128)(2,1)S(1)} %get-tuple-element.357.f0), channel_id=1, source_target_pairs={{0,2},{1,3},{2,0},{3,1},{4,6},{5,7},{6,4},{7,5},{8,10},{9,11},{10,... | collective-permute-start | bytes 1966088 | tf_op jit(solution)/shard_map/ppermute | solution.py:44
  42.3 15.4 %collective-permute-start.10 = (bf16[9,32,1024]{2,1,0:T(8,128)(2,1)S(1)}, bf16[9,32,1024]{2,1,0:T(8,128)(2,1)S(1)}, u32[]{:S(2)}, u32[]{:S(2)}) collective-permute-start(bf16[9,32,1024]{2,1,0:T(8,128)(2,1)S(1)} %collective-permute-done.refs_1_), channel_id=1, source_target_pairs={{8,0},{16,8},{24,16},{28,24},{20,28},{12,20},{4,12},{0,4},{9,1},{1... | collective-permute-start | bytes 1769480 | tf_op jit(solution)/shard_map/ppermute | solution.py:328
  44.1 15.4 %collective-permute-start.11 = (bf16[9,32,1024]{2,1,0:T(8,128)(2,1)S(1)}, bf16[9,32,1024]{2,1,0:T(8,128)(2,1)S(1)}, u32[]{:S(2)}, u32[]{:S(2)}) collective-permute-start(bf16[9,32,1024]{2,1,0:T(8,128)(2,1)S(1)} %collective-permute-done.1.refs_7_), channel_id=1, source_target_pairs={{0,8},{8,16},{16,24},{24,28},{28,20},{20,12},{12,4},{4,0},{1,9},{9... | collective-permute-start | bytes 1769480 | tf_op jit(solution)/shard_map/ppermute | solution.py:328
  59.6 16.4 %collective-permute-start.14 = (bf16[9,32,1024]{2,1,0:T(8,128)(2,1)S(1)}, bf16[9,32,1024]{2,1,0:T(8,128)(2,1)S(1)}, u32[]{:S(2)}, u32[]{:S(2)}) collective-permute-start(bf16[9,32,1024]{2,1,0:T(8,128)(2,1)S(1)} %collective-permute-done.10.refs_2_), channel_id=1, source_target_pairs={{8,0},{16,8},{24,16},{28,24},{20,28},{12,20},{4,12},{0,4},{9,1},{1... | collective-permute-start | bytes 1769480 | tf_op jit(solution)/shard_map/ppermute | solution.py:328
  61.4 15.4 %collective-permute-start.15 = (bf16[9,32,1024]{2,1,0:T(8,128)(2,1)S(1)}, bf16[9,32,1024]{2,1,0:T(8,128)(2,1)S(1)}, u32[]{:S(2)}, u32[]{:S(2)}) collective-permute-start(bf16[9,32,1024]{2,1,0:T(8,128)(2,1)S(1)} %collective-permute-done.11.refs_6_), channel_id=1, source_target_pairs={{0,8},{8,16},{16,24},{24,28},{28,20},{20,12},{12,4},{4,0},{1,9},{9... | collective-permute-start | bytes 1769480 | tf_op jit(solution)/shard_map/ppermute | solution.py:328
  61.7 14.3 %collective-permute-start.17 = (bf16[8,32,1024]{2,1,0:T(8,128)(2,1)S(1)}, bf16[8,32,1024]{2,1,0:T(8,128)(2,1)S(1)}, u32[]{:S(2)}, u32[]{:S(2)}) collective-permute-start(bf16[8,32,1024]{2,1,0:T(8,128)(2,1)S(1)} %get-tuple-element.426.l0), channel_id=1, source_target_pairs={{0,2},{1,3},{2,0},{3,1},{4,6},{5,7},{6,4},{7,5},{8,10},{9,11},{10,... | collective-permute-start | bytes 1572872 | tf_op jit(solution)/shard_map/ppermute | solution.py:44
  76.8 10.4 %collective-permute-start.24 = (bf16[8,32,1024]{2,1,0:T(8,128)(2,1)S(1)}, bf16[8,32,1024]{2,1,0:T(8,128)(2,1)S(1)}, u32[]{:S(2)}, u32[]{:S(2)}) collective-permute-start(bf16[8,32,1024]{2,1,0:T(8,128)(2,1)S(1)} %collective-permute-done.17.l2), channel_id=1, source_target_pairs={{0,1},{1,0},{2,3},{3,2},{4,5},{5,4},{6,7},{7,6},{8,9},{9,8},{10,11... | collective-permute-start | bytes 1572872 | tf_op jit(solution)/shard_map/ppermute | solution.py:44
  76.8 10.3 %collective-permute-start.19 = (bf16[5,32,1024]{2,1,0:T(8,128)(2,1)S(1)}, bf16[5,32,1024]{2,1,0:T(8,128)(2,1)S(1)}, u32[]{:S(2)}, u32[]{:S(2)}) collective-permute-start(bf16[5,32,1024]{2,1,0:T(8,128)(2,1)S(1)} %slice.192), channel_id=1, source_target_pairs={{0,8},{8,16},{16,24},{24,28},{28,20},{20,12},{12,4},{4,0},{1,9},{9... | collective-permute-start | bytes 983048 | tf_op jit(solution)/shard_map/ppermute | solution.py:328
  77.5 9.7 %collective-permute-start.20 = (bf16[4,32,1024]{2,1,0:T(8,128)(2,1)S(1)}, bf16[4,32,1024]{2,1,0:T(8,128)(2,1)S(1)}, u32[]{:S(2)}, u32[]{:S(2)}) collective-permute-start(bf16[4,32,1024]{2,1,0:T(8,128)(2,1)S(1)} %slice.193), channel_id=1, source_target_pairs={{8,0},{16,8},{24,16},{28,24},{20,28},{12,20},{4,12},{0,4},{9,1},{1... | collective-permute-start | bytes 786440 | tf_op jit(solution)/shard_map/ppermute | solution.py:328
  79.2 6.7 %collective-permute-start.22 = (bf16[288,256]{1,0:T(8,128)(2,1)S(1)}, bf16[288,256]{1,0:T(8,128)(2,1)S(1)}, u32[]{:S(2)}, u32[]{:S(2)}) collective-permute-start(bf16[288,256]{1,0:T(8,128)(2,1)S(1)} %get-tuple-element.376), channel_id=1, source_target_pairs={{0,2},{1,3},{2,0},{3,1},{4,6},{5,7},{6,4},{7,5},{8,10},{9,11},{10,... | collective-permute-start | bytes 442376 | tf_op jit(solution)/shard_map/ppermute | solution.py:44
  79.8 7.4 %collective-permute-start.23 = (bf16[288,256]{1,0:T(8,128)(2,1)S(1)}, bf16[288,256]{1,0:T(8,128)(2,1)S(1)}, u32[]{:S(2)}, u32[]{:S(2)}) collective-permute-start(bf16[288,256]{1,0:T(8,128)(2,1)S(1)} %get-tuple-element.377), channel_id=1, source_target_pairs={{0,3},{1,2},{2,1},{3,0},{4,7},{5,6},{6,5},{7,4},{8,11},{9,10},{10,... | collective-permute-start | bytes 442376 | tf_op jit(solution)/shard_map/ppermute | solution.py:44
  87.2 10.9 %collective-permute-start.26 = (bf16[128,1024]{1,0:T(8,128)(2,1)S(1)}, bf16[128,1024]{1,0:T(8,128)(2,1)S(1)}, u32[]{:S(2)}, u32[]{:S(2)}) collective-permute-start(bf16[128,1024]{1,0:T(8,128)(2,1)S(1)} %bitcast.143), channel_id=1, source_target_pairs={{0,8},{8,16},{16,24},{24,28},{28,20},{20,12},{12,4},{4,0},{1,9},{9... | collective-permute-start | bytes 786440 | tf_op jit(solution)/shard_map/ppermute | solution.py:328
  87.4 10.6 %collective-permute-start.25 = (bf16[128,1024]{1,0:T(8,128)(2,1)S(1)}, bf16[128,1024]{1,0:T(8,128)(2,1)S(1)}, u32[]{:S(2)}, u32[]{:S(2)}) collective-permute-start(bf16[128,1024]{1,0:T(8,128)(2,1)S(1)} %bitcast.144), channel_id=1, source_target_pairs={{8,0},{16,8},{24,16},{28,24},{20,28},{12,20},{4,12},{0,4},{9,1},{1... | collective-permute-start | bytes 786440 | tf_op jit(solution)/shard_map/ppermute | solution.py:328
  89.3 7.8 %collective-permute-start.27 = (bf16[72,1024]{1,0:T(8,128)(2,1)S(1)}, bf16[72,1024]{1,0:T(8,128)(2,1)S(1)}, u32[]{:S(2)}, u32[]{:S(2)}) collective-permute-start(bf16[72,1024]{1,0:T(8,128)(2,1)S(1)} %get-tuple-element.403), channel_id=1, source_target_pairs={{0,1},{1,0},{2,3},{3,2},{4,5},{5,4},{6,7},{7,6},{8,9},{9,8},{10,11... | collective-permute-start | bytes 442376 | tf_op jit(solution)/shard_map/ppermute | solution.py:44
  89.5 7.5 %collective-permute-start.28 = (bf16[72,1024]{1,0:T(8,128)(2,1)S(1)}, bf16[72,1024]{1,0:T(8,128)(2,1)S(1)}, u32[]{:S(2)}, u32[]{:S(2)}) collective-permute-start(bf16[72,1024]{1,0:T(8,128)(2,1)S(1)} %get-tuple-element.404), channel_id=1, source_target_pairs={{0,2},{1,3},{2,0},{3,1},{4,6},{5,7},{6,4},{7,5},{8,10},{9,11},{10,... | collective-permute-start | bytes 442376 | tf_op jit(solution)/shard_map/ppermute | solution.py:44
  90.0 8.0 %collective-permute-start.29 = (bf16[72,1024]{1,0:T(8,128)(2,1)S(1)}, bf16[72,1024]{1,0:T(8,128)(2,1)S(1)}, u32[]{:S(2)}, u32[]{:S(2)}) collective-permute-start(bf16[72,1024]{1,0:T(8,128)(2,1)S(1)} %get-tuple-element.405), channel_id=1, source_target_pairs={{0,3},{1,2},{2,1},{3,0},{4,7},{5,6},{6,5},{7,4},{8,11},{9,10},{10,... | collective-permute-start | bytes 442376 | tf_op jit(solution)/shard_map/ppermute | solution.py:44
  100.3 16.9 %collective-permute-start.32 = (bf16[288,1024]{1,0:T(8,128)(2,1)S(1)}, bf16[288,1024]{1,0:T(8,128)(2,1)S(1)}, u32[]{:S(2)}, u32[]{:S(2)}) collective-permute-start(bf16[288,1024]{1,0:T(8,128)(2,1)S(1)} %add_convert_fusion), channel_id=1, source_target_pairs={{0,2},{1,3},{2,0},{3,1},{4,6},{5,7},{6,4},{7,5},{8,10},{9,11},{10,... | collective-permute-start | bytes 1769480 | tf_op jit(solution)/shard_map/ppermute | solution.py:44
  106.4 10.8 %collective-permute-start.31 = (bf16[288,1024]{1,0:T(8,128)(2,1)S(1)}, bf16[288,1024]{1,0:T(8,128)(2,1)S(1)}, u32[]{:S(2)}, u32[]{:S(2)}) collective-permute-start(bf16[288,1024]{1,0:T(8,128)(2,1)S(1)} %get-tuple-element.420), channel_id=1, source_target_pairs={{0,1},{1,0},{2,3},{3,2},{4,5},{5,4},{6,7},{7,6},{8,9},{9,8},{10,11... | collective-permute-start | bytes 1769480 | tf_op jit(solution)/shard_map/ppermute | solution.py:44
  106.5 8.6 %collective-permute-start.36 = (bf16[128,1024]{1,0:T(8,128)(2,1)S(1)}, bf16[128,1024]{1,0:T(8,128)(2,1)S(1)}, u32[]{:S(2)}, u32[]{:S(2)}) collective-permute-start(bf16[128,1024]{1,0:T(8,128)(2,1)S(1)} %collective-permute-done.25.refs_1_), channel_id=1, source_target_pairs={{8,0},{16,8},{24,16},{28,24},{20,28},{12,20},{4,12},{0,4},{9,1},{1... | collective-permute-start | bytes 786440 | tf_op jit(solution)/shard_map/ppermute | solution.py:328
  107.9 8.7 %collective-permute-start.38 = (bf16[128,1024]{1,0:T(8,128)(2,1)S(1)}, bf16[128,1024]{1,0:T(8,128)(2,1)S(1)}, u32[]{:S(2)}, u32[]{:S(2)}) collective-permute-start(bf16[128,1024]{1,0:T(8,128)(2,1)S(1)} %collective-permute-done.26.refs_7_), channel_id=1, source_target_pairs={{0,8},{8,16},{16,24},{24,28},{28,20},{20,12},{12,4},{4,0},{1,9},{9... | collective-permute-start | bytes 786440 | tf_op jit(solution)/shard_map/ppermute | solution.py:328
  115.2 10.7 %collective-permute-start.37 = (bf16[128,1024]{1,0:T(8,128)(2,1)S(1)}, bf16[128,1024]{1,0:T(8,128)(2,1)S(1)}, u32[]{:S(2)}, u32[]{:S(2)}) collective-permute-start(bf16[128,1024]{1,0:T(8,128)(2,1)S(1)} %collective-permute-done.36.refs_2_), channel_id=1, source_target_pairs={{8,0},{16,8},{24,16},{28,24},{20,28},{12,20},{4,12},{0,4},{9,1},{1... | collective-permute-start | bytes 786440 | tf_op jit(solution)/shard_map/ppermute | solution.py:328
  116.5 10.8 %collective-permute-start.39 = (bf16[128,1024]{1,0:T(8,128)(2,1)S(1)}, bf16[128,1024]{1,0:T(8,128)(2,1)S(1)}, u32[]{:S(2)}, u32[]{:S(2)}) collective-permute-start(bf16[128,1024]{1,0:T(8,128)(2,1)S(1)} %collective-permute-done.38.refs_6_), channel_id=1, source_target_pairs={{0,8},{8,16},{16,24},{24,28},{28,20},{20,12},{12,4},{4,0},{1,9},{9... | collective-permute-start | bytes 786440 | tf_op jit(solution)/shard_map/ppermute | solution.py:328
  119.6 6.3 %collective-permute-start.33 = (bf16[72,1024]{1,0:T(8,128)(2,1)S(1)}, bf16[72,1024]{1,0:T(8,128)(2,1)S(1)}, u32[]{:S(2)}, u32[]{:S(2)}) collective-permute-start(bf16[72,1024]{1,0:T(8,128)(2,1)S(1)} %get-tuple-element.431.p0), channel_id=1, source_target_pairs={{0,2},{1,3},{2,0},{3,1},{4,6},{5,7},{6,4},{7,5},{8,10},{9,11},{10,... | collective-permute-start | bytes 442376 | tf_op jit(solution)/shard_map/ppermute | solution.py:44
  125.9 7.1 %collective-permute-start.35 = (bf16[72,1024]{1,0:T(8,128)(2,1)S(1)}, bf16[72,1024]{1,0:T(8,128)(2,1)S(1)}, u32[]{:S(2)}, u32[]{:S(2)}) collective-permute-start(bf16[72,1024]{1,0:T(8,128)(2,1)S(1)} %collective-permute-done.33.p2), channel_id=1, source_target_pairs={{0,1},{1,0},{2,3},{3,2},{4,5},{5,4},{6,7},{7,6},{8,9},{9,8},{10,11... | collective-permute-start | bytes 442376 | tf_op jit(solution)/shard_map/ppermute | solution.py:44
  125.9 6.0 %collective-permute-start.41 = (bf16[64,1024]{1,0:T(8,128)(2,1)S(1)}, bf16[64,1024]{1,0:T(8,128)(2,1)S(1)}, u32[]{:S(2)}, u32[]{:S(2)}) collective-permute-start(bf16[64,1024]{1,0:T(8,128)(2,1)S(1)} %slice.253), channel_id=1, source_target_pairs={{8,0},{16,8},{24,16},{28,24},{20,28},{12,20},{4,12},{0,4},{9,1},{1... | collective-permute-start | bytes 393224 | tf_op jit(solution)/shard_map/ppermute | solution.py:328
  137.8 6.0 %collective-permute-start.43 = (bf16[72,1024]{1,0:T(8,128)(2,1)S(1)}, bf16[72,1024]{1,0:T(8,128)(2,1)S(1)}, u32[]{:S(2)}, u32[]{:S(2)}) collective-permute-start(bf16[72,1024]{1,0:T(8,128)(2,1)S(1)} %fusion.27), channel_id=1, source_target_pairs={{0,2},{1,3},{2,0},{3,1},{4,6},{5,7},{6,4},{7,5},{8,10},{9,11},{10,... | collective-permute-start | bytes 442376 | tf_op jit(solution)/shard_map/ppermute | solution.py:44
  149.7 7.1 %collective-permute-start.48 = (bf16[144,1024]{1,0:T(8,128)(2,1)S(1)}, bf16[144,1024]{1,0:T(8,128)(2,1)S(1)}, u32[]{:S(2)}, u32[]{:S(2)}) collective-permute-start(bf16[144,1024]{1,0:T(8,128)(2,1)S(1)} %pad_maximum_fusion.1), channel_id=1, source_target_pairs={{0,8},{8,16},{16,24},{24,28},{28,20},{20,12},{12,4},{4,0},{1,9},{9... | collective-permute-start | bytes 884744 | tf_op jit(solution)/shard_map/ppermute | solution.py:328
  150.1 6.9 %collective-permute-start.50 = (bf16[144,1024]{1,0:T(8,128)(2,1)S(1)}, bf16[144,1024]{1,0:T(8,128)(2,1)S(1)}, u32[]{:S(2)}, u32[]{:S(2)}) collective-permute-start(bf16[144,1024]{1,0:T(8,128)(2,1)S(1)} %pad_maximum_fusion.2), channel_id=1, source_target_pairs={{8,0},{16,8},{24,16},{28,24},{20,28},{12,20},{4,12},{0,4},{9,1},{1... | collective-permute-start | bytes 884744 | tf_op jit(solution)/shard_map/ppermute | solution.py:328
  151.9 9.5 %collective-permute-start.47 = (bf16[288,1024]{1,0:T(8,128)(2,1)S(1)}, bf16[288,1024]{1,0:T(8,128)(2,1)S(1)}, u32[]{:S(2)}, u32[]{:S(2)}) collective-permute-start(bf16[288,1024]{1,0:T(8,128)(2,1)S(1)} %get-tuple-element.494.g0), channel_id=1, source_target_pairs={{0,1},{1,0},{2,3},{3,2},{4,5},{5,4},{6,7},{7,6},{8,9},{9,8},{10,11... | collective-permute-start | bytes 1769480 | tf_op jit(solution)/shard_map/ppermute | solution.py:44
  151.9 15.7 %collective-permute-start.46 = (bf16[288,1024]{1,0:T(8,128)(2,1)S(1)}, bf16[288,1024]{1,0:T(8,128)(2,1)S(1)}, u32[]{:S(2)}, u32[]{:S(2)}) collective-permute-start(bf16[288,1024]{1,0:T(8,128)(2,1)S(1)} %get-tuple-element.494.g0), channel_id=1, source_target_pairs={{0,2},{1,3},{2,0},{3,1},{4,6},{5,7},{6,4},{7,5},{8,10},{9,11},{10,... | collective-permute-start | bytes 1769480 | tf_op jit(solution)/shard_map/ppermute | solution.py:44
  157.2 10.4 %collective-permute-start.51 = (bf16[144,1024]{1,0:T(8,128)(2,1)S(1)}, bf16[144,1024]{1,0:T(8,128)(2,1)S(1)}, u32[]{:S(2)}, u32[]{:S(2)}) collective-permute-start(bf16[144,1024]{1,0:T(8,128)(2,1)S(1)} %get-tuple-element.622), channel_id=1, source_target_pairs={{8,0},{16,8},{24,16},{28,24},{20,28},{12,20},{4,12},{0,4},{9,1},{1... | collective-permute-start | bytes 884744 | tf_op jit(solution)/shard_map/ppermute | solution.py:328
  159.0 8.6 %collective-permute-start.49 = (bf16[144,1024]{1,0:T(8,128)(2,1)S(1)}, bf16[144,1024]{1,0:T(8,128)(2,1)S(1)}, u32[]{:S(2)}, u32[]{:S(2)}) collective-permute-start(bf16[144,1024]{1,0:T(8,128)(2,1)S(1)} %get-tuple-element.623), channel_id=1, source_target_pairs={{0,8},{8,16},{16,24},{24,28},{28,20},{20,12},{12,4},{4,0},{1,9},{9... | collective-permute-start | bytes 884744 | tf_op jit(solution)/shard_map/ppermute | solution.py:328
  168.3 9.0 %collective-permute-start.56 = (bf16[144,1024]{1,0:T(8,128)(2,1)S(1)}, bf16[144,1024]{1,0:T(8,128)(2,1)S(1)}, u32[]{:S(2)}, u32[]{:S(2)}) collective-permute-start(bf16[144,1024]{1,0:T(8,128)(2,1)S(1)} %get-tuple-element.620), channel_id=1, source_target_pairs={{8,0},{16,8},{24,16},{28,24},{20,28},{12,20},{4,12},{0,4},{9,1},{1... | collective-permute-start | bytes 884744 | tf_op jit(solution)/shard_map/ppermute | solution.py:328
  170.1 8.7 %collective-permute-start.55 = (bf16[144,1024]{1,0:T(8,128)(2,1)S(1)}, bf16[144,1024]{1,0:T(8,128)(2,1)S(1)}, u32[]{:S(2)}, u32[]{:S(2)}) collective-permute-start(bf16[144,1024]{1,0:T(8,128)(2,1)S(1)} %get-tuple-element.621), channel_id=1, source_target_pairs={{0,8},{8,16},{16,24},{24,28},{28,20},{20,12},{12,4},{4,0},{1,9},{9... | collective-permute-start | bytes 884744 | tf_op jit(solution)/shard_map/ppermute | solution.py:328
  171.1 8.3 %collective-permute-start.54 = (bf16[4,32,1024]{2,1,0:T(8,128)(2,1)S(1)}, bf16[4,32,1024]{2,1,0:T(8,128)(2,1)S(1)}, u32[]{:S(2)}, u32[]{:S(2)}) collective-permute-start(bf16[4,32,1024]{2,1,0:T(8,128)(2,1)S(1)} %get-tuple-element.487), channel_id=1, source_target_pairs={{0,2},{1,3},{2,0},{3,1},{4,6},{5,7},{6,4},{7,5},{8,10},{9,11},{10,... | collective-permute-start | bytes 786440 | tf_op jit(solution)/shard_map/ppermute | solution.py:44
  179.5 11.6 %collective-permute-start.57 = (bf16[5,32,1024]{2,1,0:T(8,128)(2,1)S(1)}, bf16[5,32,1024]{2,1,0:T(8,128)(2,1)S(1)}, u32[]{:S(2)}, u32[]{:S(2)}) collective-permute-start(bf16[5,32,1024]{2,1,0:T(8,128)(2,1)S(1)} %get-tuple-element.492), channel_id=1, source_target_pairs={{0,8},{8,16},{16,24},{24,28},{28,20},{20,12},{12,4},{4,0},{1,9},{9... | collective-permute-start | bytes 983048 | tf_op jit(solution)/shard_map/ppermute | solution.py:328
  179.8 11.2 %collective-permute-start.58 = (bf16[5,32,1024]{2,1,0:T(8,128)(2,1)S(1)}, bf16[5,32,1024]{2,1,0:T(8,128)(2,1)S(1)}, u32[]{:S(2)}, u32[]{:S(2)}) collective-permute-start(bf16[5,32,1024]{2,1,0:T(8,128)(2,1)S(1)} %get-tuple-element.493), channel_id=1, source_target_pairs={{8,0},{16,8},{24,16},{28,24},{20,28},{12,20},{4,12},{0,4},{9,1},{1... | collective-permute-start | bytes 983048 | tf_op jit(solution)/shard_map/ppermute | solution.py:328
  181.5 9.5 %collective-permute-start.59 = (bf16[4,32,1024]{2,1,0:T(8,128)(2,1)S(1)}, bf16[4,32,1024]{2,1,0:T(8,128)(2,1)S(1)}, u32[]{:S(2)}, u32[]{:S(2)}) collective-permute-start(bf16[4,32,1024]{2,1,0:T(8,128)(2,1)S(1)} %get-tuple-element.502), channel_id=1, source_target_pairs={{0,2},{1,3},{2,0},{3,1},{4,6},{5,7},{6,4},{7,5},{8,10},{9,11},{10,... | collective-permute-start | bytes 786440 | tf_op jit(solution)/shard_map/ppermute | solution.py:44
  191.3 11.1 %collective-permute-start.61 = (bf16[5,32,1024]{2,1,0:T(8,128)(2,1)S(1)}, bf16[5,32,1024]{2,1,0:T(8,128)(2,1)S(1)}, u32[]{:S(2)}, u32[]{:S(2)}) collective-permute-start(bf16[5,32,1024]{2,1,0:T(8,128)(2,1)S(1)} %get-tuple-element.618), channel_id=1, source_target_pairs={{8,0},{16,8},{24,16},{28,24},{20,28},{12,20},{4,12},{0,4},{9,1},{1... | collective-permute-start | bytes 983048 | tf_op jit(solution)/shard_map/ppermute | solution.py:328
  193.0 9.4 %collective-permute-start.60 = (bf16[5,32,1024]{2,1,0:T(8,128)(2,1)S(1)}, bf16[5,32,1024]{2,1,0:T(8,128)(2,1)S(1)}, u32[]{:S(2)}, u32[]{:S(2)}) collective-permute-start(bf16[5,32,1024]{2,1,0:T(8,128)(2,1)S(1)} %get-tuple-element.619), channel_id=1, source_target_pairs={{0,8},{8,16},{16,24},{24,28},{28,20},{20,12},{12,4},{4,0},{1,9},{9... | collective-permute-start | bytes 983048 | tf_op jit(solution)/shard_map/ppermute | solution.py:328
  193.4 6.6 %collective-permute-start.63 = (bf16[288,256]{1,0:T(8,128)(2,1)S(1)}, bf16[288,256]{1,0:T(8,128)(2,1)S(1)}, u32[]{:S(2)}, u32[]{:S(2)}) collective-permute-start(bf16[288,256]{1,0:T(8,128)(2,1)S(1)} %get-tuple-element.516), channel_id=1, source_target_pairs={{0,2},{1,3},{2,0},{3,1},{4,6},{5,7},{6,4},{7,5},{8,10},{9,11},{10,... | collective-permute-start | bytes 442376 | tf_op jit(solution)/shard_map/ppermute | solution.py:44
  193.9 8.5 %collective-permute-start.64 = (bf16[288,256]{1,0:T(8,128)(2,1)S(1)}, bf16[288,256]{1,0:T(8,128)(2,1)S(1)}, u32[]{:S(2)}, u32[]{:S(2)}) collective-permute-start(bf16[288,256]{1,0:T(8,128)(2,1)S(1)} %get-tuple-element.517), channel_id=1, source_target_pairs={{0,3},{1,2},{2,1},{3,0},{4,7},{5,6},{6,5},{7,4},{8,11},{9,10},{10,... | collective-permute-start | bytes 442376 | tf_op jit(solution)/shard_map/ppermute | solution.py:44
  202.4 9.8 %collective-permute-start.65 = (bf16[5,32,1024]{2,1,0:T(8,128)(2,1)S(1)}, bf16[5,32,1024]{2,1,0:T(8,128)(2,1)S(1)}, u32[]{:S(2)}, u32[]{:S(2)}) collective-permute-start(bf16[5,32,1024]{2,1,0:T(8,128)(2,1)S(1)} %get-tuple-element.520), channel_id=1, source_target_pairs={{0,8},{8,16},{16,24},{24,28},{28,20},{20,12},{12,4},{4,0},{1,9},{9... | collective-permute-start | bytes 983048 | tf_op jit(solution)/shard_map/ppermute | solution.py:328
  202.8 9.5 %collective-permute-start.66 = (bf16[5,32,1024]{2,1,0:T(8,128)(2,1)S(1)}, bf16[5,32,1024]{2,1,0:T(8,128)(2,1)S(1)}, u32[]{:S(2)}, u32[]{:S(2)}) collective-permute-start(bf16[5,32,1024]{2,1,0:T(8,128)(2,1)S(1)} %get-tuple-element.521), channel_id=1, source_target_pairs={{8,0},{16,8},{24,16},{28,24},{20,28},{12,20},{4,12},{0,4},{9,1},{1... | collective-permute-start | bytes 983048 | tf_op jit(solution)/shard_map/ppermute | solution.py:328
  213.4 9.3 %collective-permute-start.67 = (bf16[5,32,1024]{2,1,0:T(8,128)(2,1)S(1)}, bf16[5,32,1024]{2,1,0:T(8,128)(2,1)S(1)}, u32[]{:S(2)}, u32[]{:S(2)}) collective-permute-start(bf16[5,32,1024]{2,1,0:T(8,128)(2,1)S(1)} %get-tuple-element.537), channel_id=1, source_target_pairs={{0,8},{8,16},{16,24},{24,28},{28,20},{20,12},{12,4},{4,0},{1,9},{9... | collective-permute-start | bytes 983048 | tf_op jit(solution)/shard_map/ppermute | solution.py:328
  214.3 9.1 %collective-permute-start.68 = (bf16[5,32,1024]{2,1,0:T(8,128)(2,1)S(1)}, bf16[5,32,1024]{2,1,0:T(8,128)(2,1)S(1)}, u32[]{:S(2)}, u32[]{:S(2)}) collective-permute-start(bf16[5,32,1024]{2,1,0:T(8,128)(2,1)S(1)} %get-tuple-element.538), channel_id=1, source_target_pairs={{8,0},{16,8},{24,16},{28,24},{20,28},{12,20},{4,12},{0,4},{9,1},{1... | collective-permute-start | bytes 983048 | tf_op jit(solution)/shard_map/ppermute | solution.py:328
  215.7 6.1 %collective-permute-start.72 = (bf16[72,1024]{1,0:T(8,128)(2,1)S(1)}, bf16[72,1024]{1,0:T(8,128)(2,1)S(1)}, u32[]{:S(2)}, u32[]{:S(2)}) collective-permute-start(bf16[72,1024]{1,0:T(8,128)(2,1)S(1)} %get-tuple-element.547), channel_id=1, source_target_pairs={{0,3},{1,2},{2,1},{3,0},{4,7},{5,6},{6,5},{7,4},{8,11},{9,10},{10,... | collective-permute-start | bytes 442376 | tf_op jit(solution)/shard_map/ppermute | solution.py:44
  223.4 8.3 %collective-permute-start.73 = (bf16[5,32,1024]{2,1,0:T(8,128)(2,1)S(1)}, bf16[5,32,1024]{2,1,0:T(8,128)(2,1)S(1)}, u32[]{:S(2)}, u32[]{:S(2)}) collective-permute-start(bf16[5,32,1024]{2,1,0:T(8,128)(2,1)S(1)} %get-tuple-element.549), channel_id=1, source_target_pairs={{0,8},{8,16},{16,24},{24,28},{28,20},{20,12},{12,4},{4,0},{1,9},{9... | collective-permute-start | bytes 983048 | tf_op jit(solution)/shard_map/ppermute | solution.py:328
  225.0 7.9 %collective-permute-start.74 = (bf16[5,32,1024]{2,1,0:T(8,128)(2,1)S(1)}, bf16[5,32,1024]{2,1,0:T(8,128)(2,1)S(1)}, u32[]{:S(2)}, u32[]{:S(2)}) collective-permute-start(bf16[5,32,1024]{2,1,0:T(8,128)(2,1)S(1)} %get-tuple-element.550), channel_id=1, source_target_pairs={{8,0},{16,8},{24,16},{28,24},{20,28},{12,20},{4,12},{0,4},{9,1},{1... | collective-permute-start | bytes 983048 | tf_op jit(solution)/shard_map/ppermute | solution.py:328
  225.4 7.7 %collective-permute-start.75 = (bf16[4,40,1024]{2,1,0:T(8,128)(2,1)S(1)}, bf16[4,40,1024]{2,1,0:T(8,128)(2,1)S(1)}, u32[]{:S(2)}, u32[]{:S(2)}) collective-permute-start(bf16[4,40,1024]{2,1,0:T(8,128)(2,1)S(1)} %get-tuple-element.552), channel_id=1, source_target_pairs={{0,2},{1,3},{2,0},{3,1},{4,6},{5,7},{6,4},{7,5},{8,10},{9,11},{10,... | collective-permute-start | bytes 983048 | tf_op jit(solution)/shard_map/ppermute | solution.py:44
  234.4 7.4 %collective-permute-start.77 = (bf16[5,32,1024]{2,1,0:T(8,128)(2,1)}, bf16[5,32,1024]{2,1,0:T(8,128)(2,1)}, u32[]{:S(2)}, u32[]{:S(2)}) collective-permute-start(bf16[5,32,1024]{2,1,0:T(8,128)(2,1)} %get-tuple-element.610), channel_id=1, source_target_pairs={{8,0},{16,8},{24,16},{28,24},{20,28},{12,20},{4,12},{0,4},{9,1},{1... | collective-permute-start | bytes 983048 | tf_op jit(solution)/shard_map/ppermute | solution.py:328
  236.1 7.4 %collective-permute-start.76 = (bf16[5,32,1024]{2,1,0:T(8,128)(2,1)}, bf16[5,32,1024]{2,1,0:T(8,128)(2,1)}, u32[]{:S(2)}, u32[]{:S(2)}) collective-permute-start(bf16[5,32,1024]{2,1,0:T(8,128)(2,1)} %fusion.17), channel_id=1, source_target_pairs={{0,8},{8,16},{16,24},{24,28},{28,20},{20,12},{12,4},{4,0},{1,9},{9... | collective-permute-start | bytes 983048 | tf_op jit(solution)/shard_map/ppermute | solution.py:328
  236.4 7.4 %collective-permute-start.78 = (bf16[4,40,1024]{2,1,0:T(8,128)(2,1)}, bf16[4,40,1024]{2,1,0:T(8,128)(2,1)}, u32[]{:S(2)}, u32[]{:S(2)}) collective-permute-start(bf16[4,40,1024]{2,1,0:T(8,128)(2,1)} %get-tuple-element.563), channel_id=1, source_target_pairs={{0,2},{1,3},{2,0},{3,1},{4,6},{5,7},{6,4},{7,5},{8,10},{9,11},{10,... | collective-permute-start | bytes 983048 | tf_op jit(solution)/shard_map/ppermute | solution.py:44
  243.8 9.4 %collective-permute-start.82 = (bf16[40,1024]{1,0:T(8,128)(2,1)S(1)}, bf16[40,1024]{1,0:T(8,128)(2,1)}, u32[]{:S(2)}, u32[]{:S(2)}) collective-permute-start(bf16[40,1024]{1,0:T(8,128)(2,1)S(1)} %get-tuple-element.630), channel_id=1, source_target_pairs={{8,0},{16,8},{24,16},{28,24},{20,28},{12,20},{4,12},{0,4},{9,1},{1... | collective-permute-start | bytes 245768 | tf_op jit(solution)/shard_map/ppermute | solution.py:328
  245.5 7.6 %collective-permute-start.81 = (bf16[40,1024]{1,0:T(8,128)(2,1)S(1)}, bf16[40,1024]{1,0:T(8,128)(2,1)}, u32[]{:S(2)}, u32[]{:S(2)}) collective-permute-start(bf16[40,1024]{1,0:T(8,128)(2,1)S(1)} %get-tuple-element.631), channel_id=1, source_target_pairs={{0,8},{8,16},{16,24},{24,28},{28,20},{20,12},{12,4},{4,0},{1,9},{9... | collective-permute-start | bytes 245768 | tf_op jit(solution)/shard_map/ppermute | solution.py:328
  247.8 7.4 %collective-permute-start.80 = (bf16[5,32,1024]{2,1,0:T(8,128)(2,1)}, bf16[5,32,1024]{2,1,0:T(8,128)(2,1)}, u32[]{:S(2)}, u32[]{:S(2)}) collective-permute-start(bf16[5,32,1024]{2,1,0:T(8,128)(2,1)} %fusion.4), channel_id=1, source_target_pairs={{8,0},{16,8},{24,16},{28,24},{20,28},{12,20},{4,12},{0,4},{9,1},{1... | collective-permute-start | bytes 983048 | tf_op jit(solution)/shard_map/ppermute | solution.py:328
  249.5 7.4 %collective-permute-start.79 = (bf16[5,32,1024]{2,1,0:T(8,128)(2,1)}, bf16[5,32,1024]{2,1,0:T(8,128)(2,1)}, u32[]{:S(2)}, u32[]{:S(2)}) collective-permute-start(bf16[5,32,1024]{2,1,0:T(8,128)(2,1)} %get-tuple-element.568), channel_id=1, source_target_pairs={{0,8},{8,16},{16,24},{24,28},{28,20},{20,12},{12,4},{4,0},{1,9},{9... | collective-permute-start | bytes 983048 | tf_op jit(solution)/shard_map/ppermute | solution.py:328
  257.8 6.5 %collective-permute-start.84 = (bf16[40,1024]{1,0:T(8,128)(2,1)S(1)}, bf16[40,1024]{1,0:T(8,128)(2,1)S(1)}, u32[]{:S(2)}, u32[]{:S(2)}) collective-permute-start(bf16[40,1024]{1,0:T(8,128)(2,1)S(1)} %fusion.29), channel_id=1, source_target_pairs={{8,0},{16,8},{24,16},{28,24},{20,28},{12,20},{4,12},{0,4},{9,1},{1... | collective-permute-start | bytes 245768 | tf_op jit(solution)/shard_map/ppermute | solution.py:328
  (40 other events, 375.9 us)
where the time goes:
time: 277 us
  waiting for transfers between devices  116 us (42%)
  starting transfers between devices  75.9 us (27%)
  Pallas kernels  54 us (19%)
  other arithmetic  16.2 us (6%)
  local copies, waits for them, and re-layouts  12.2 us (4%)
    ppermute x53, waiting for transfers between devices, hop(): return lax.ppermute(x, 'dp', right if turn else left)  75.7 us
    ppermute x53, starting transfers between devices, hop(): return lax.ppermute(x, 'dp', right if turn else left)  55.8 us
    pallas_call x17, Pallas kernels, kernel(): pl.pallas_call(body, out_shape=outs, in_specs=ins, out_specs=jax.tree.map...  54 us
    ppermute x35, waiting for transfers between devices, swap_row(): return lax.ppermute(x, 'row', [(i, i ^ q) for i in range(4)])  40.5 us
    ppermute x35, starting transfers between devices, swap_row(): return lax.ppermute(x, 'row', [(i, i ^ q) for i in range(4)])  20.1 us
    convert_element_type x11, other arithmetic, add_to(): return (terms[k % RING].astype(F32) + value.astype(F32)).astype(BF16)  6.45 us
  transfers between devices with their start and end apart: 88, of which 50 were waited for; matrix products, arithmetic and copies ran while one was open for 8% of the time, Pallas kernels for 18%

commit v1 on v0

--- a/solution.py
+++ b/solution.py
@@ -293,7 +293,7 @@
     return jax.ShapeDtypeStruct(dims, dtype)
 
 
-def kernel(body, outs, ins, scratch, flops, moved, *arrays, specs=None, room=24):
+def kernel(body, outs, ins, scratch, flops, moved, *arrays, specs=None, room=16):
     return pl.pallas_call(
         body,
         out_shape=outs,
@@ -323,9 +323,10 @@
     return [pltpu.make_async_copy(a, b, sems.at[i]) for i, (a, b) in enumerate(pairs)]
 
 
-def hop(x, turn):
-    right, left = ring_pairs(RING)
-    return lax.ppermute(x, "dp", right if turn else left)
+def hop(x, turn, places=1):
+    order = ring_order(RING)
+    step = places if turn else -places
+    return lax.ppermute(x, "dp", [(order[i], order[(i + step) % RING]) for i in range(RING)])
 
 
 def gather_step(state, step, low=None, high=None):
@@ -560,6 +561,13 @@
     lower[...] = out[RING // 2, upper.shape[0] :]
 
 
+def read_end(term, a, b, out, bias):
+    total = term[...].astype(F32) + a[...].astype(F32) + b[...].astype(F32)
+    rows = out.shape[1]
+    out[...] = total[:rows].T
+    bias[...] = total[rows : rows + 8]
+
+
 def spread(pairs, grad, dims):
     slots, rows, cols = dims
     count, width = grad.shape
@@ -632,28 +640,26 @@
         out[t] = t_dot(here[:, lanes], one[...])
 
 
-def conv_terms(first, number, next_to, where, half, there, g2, g3, *refs):
-    parts, (far, side, out, two) = refs[:-4], refs[-4:]
+def conv_terms(first, number, where, half, there, g2, g3, *refs):
+    parts, outs, (two, line) = refs[: -RING - 2], refs[-RING - 2 : -2], refs[-2:]
     count = g2.shape[0]
     two[:count], two[count:] = g2[...], g3[...]
-    rows, width = out.shape[2:]
+    rows, width = outs[0].shape[1:]
     group = RING * rows
 
     @pl.loop(0, number)
     def _(t):
         lanes = pl.ds(pl.multiple_of((first + t) * group, group), group)
         terms = half[first + t] + t_dot(there[:, lanes], two[...])
-        terms = terms.astype(BF16).reshape(RING, rows, width)
+        line[...] = terms.astype(BF16).reshape(RING, rows, width)
         for k in range(RING):
-            out[where[2 + RING + k], t] = terms[k]
+            outs[k][t] = line[where[2 + k]]
 
     if parts:
         own, near, low, high = parts
-        half_way = RING // 2
-        for a, b, cross in ((0, half_way, low), (half_way, RING, high)):
-            out[a:b, number] = (own[a:b] + near[0, a:b].astype(F32) + cross[...].astype(F32)).astype(BF16)
-    far[...] = out[RING // 2]
-    side[...] = out[next_to]
+        for k in range(RING):
+            cross = low[k] if k < RING // 2 else high[k - RING // 2]
+            outs[k][number] = (own[k] + near[0, k].astype(F32) + cross.astype(F32)).astype(BF16)
 
 
 def conv_back(dims, where, g0, g1, g2, g3, weight, o0, o1, o2, o3, whole, held, low):
@@ -697,10 +703,11 @@
     terms[...] = t_dot(x[...], grad_one[...]).reshape(terms.shape)
     rows = terms.shape[2]
     for k in range(RING):
-        own[k, :rows] = terms[where[2 + k], at_row(where, 0)]
-        near[0, k, :rows] = terms[where[2 + k], at_row(where, 1)].astype(BF16)
-        far[k, :rows] = terms[where[2 + k], at_row(where, 2)]
-        near[1, k, :rows] = terms[where[2 + k], at_row(where, 3)].astype(BF16)
+        to = where[2 + (k + 3) % RING]
+        own[k, :rows] = terms[to, at_row(where, 0)]
+        near[0, k, :rows] = terms[to, at_row(where, 1)].astype(BF16)
+        far[k, :rows] = terms[to, at_row(where, 2)]
+        near[1, k, :rows] = terms[to, at_row(where, 3)].astype(BF16)
         own[k, rows:] = tail
         near[0, k, rows:] = tail.astype(BF16)
         far[k, rows:] = tail
@@ -792,7 +799,8 @@
     ring = gather_step(gather_state(jnp.concatenate([last_weight, first_mine], axis=0)), 1)
     read = read_weight.T
     cots = cotangent.reshape(count, -1)
-    more, ring, where, read, cots, x = fence(more, ring, where, read, cots, x)
+    places = ((row * RING + dp) * own, (dp * 4 + row) * own, dp * outs)
+    more, ring, where, read, cots, x, places = fence(more, ring, where, read, cots, x, places)
     ring = gather_step(ring, 2)
     cots = kernel(split_columns, [quarter] * 4, [SM, VM], [], 0, 2 * count * 4 * width * 2, where, cots)
     ring, cots = fence(ring, cots)
@@ -868,10 +876,11 @@
     cross = swap_row(other, 2)
     read = gather_step(read, 2)
     mine, near, spans_near = conv_half(0, (conv_full,))
-    near = fence(near, mine)[0]
+    near, read = fence(near, read)
     near = swap_row(near, 1)
-    mine, near, cross = fence(mine, near, cross)
     read = gather_step(read, 3)
+    mine, near, cross, read = fence(mine, near, cross, read)
+    read = gather_step(read, 4, lambda v: v[: outs // 2], lambda v: v[outs // 2 :])
     hat_two, scale_two, low_two, hat_three, scale_three, pooled, last_full = kernel(
         functools.partial(stage_two, dims),
         [wide_f32, thin_f32, wide_bf16, wide_f32, thin_f32, quarter, square_of],
@@ -887,9 +896,8 @@
         norms,
         *lasts,
     )
-    read = gather_step(read, 4, lambda v: v[: outs // 2], lambda v: v[outs // 2 :])
     pool_two, pool_one = swap_row(pooled, 2), swap_row(pooled, 1)
-    pooled, pool_two, pool_one = fence(pooled, pool_two, pool_one)
+    pooled, pool_two, pool_one, read = fence(pooled, pool_two, pool_one, read)
     pools = [pooled, pool_one, pool_two, swap_row(pool_two, 1)]
     *shown, grad_low, mine, near, away = kernel(
         functools.partial(readout, slots),
@@ -979,14 +987,13 @@
     last_low = swap_row(last_low, 2)
     read_a, read_b = scatter_step(*read_far, read_terms, read_a, read_b, 1)
 
-    def weight_terms(first, number, next_to, parts):
+    def weight_terms(first, number, parts):
         held = number + len(parts) // 4
-        some = shape((held, own, width), BF16)
         return kernel(
-            functools.partial(conv_terms, first, number, next_to),
-            [some, some, shape((RING, held, own, width), BF16)],
+            functools.partial(conv_terms, first, number),
+            [shape((held, own, width), BF16)] * RING,
             [SM] + [VM] * (4 + len(parts)),
-            [pltpu.VMEM((2 * patches, width), BF16)],
+            [pltpu.VMEM((2 * patches, width), BF16), pltpu.VMEM((RING, own, width), BF16)],
             matmul * number,
             2 * square * number,
             where,
@@ -999,12 +1006,12 @@
     def add_to(terms, k, value):
         return (terms[k % RING].astype(F32) + value.astype(F32)).astype(BF16)
 
-    one_far, one_side, one = weight_terms(0, 5, 5, ())
-    one_far, one_side, one, grads, last_low, last_high, read_a, read_b = fence(
-        one_far, one_side, one, grads, last_low, last_high, read_a, read_b
+    one = weight_terms(0, 5, ())
+    one, grads, last_low, last_high, read_a, read_b = fence(
+        one, grads, last_low, last_high, read_a, read_b
     )
     last_high = swap_row(last_high, 2)
-    one_a, one_b = hop(one_far, True), hop(one_side, False)
+    one_a, one_b = hop(one[far], True), hop(one[far + 1], False)
     backs = kernel(
         functools.partial(conv_back, full),
         [piece] * 4,
@@ -1023,9 +1030,9 @@
     one_a, one_b, backs, grads, last_high = fence(one_a, one_b, backs, grads, last_high)
     one_a, one_b = hop(add_to(one, 3, one_a), True), hop(add_to(one, -2, one_b), False)
     backs = exchange_row(backs)
-    two_far, two_side, two = weight_terms(5, 4, 3, (last_own, last_near, last_low, last_high))
-    one_a, one_b, two_far, two_side, two, backs = fence(one_a, one_b, two_far, two_side, two, backs)
-    two_a, two_b = hop(two_side, True), hop(two_far, False)
+    two = weight_terms(5, 4, (last_own, last_near, last_low, last_high))
+    one_a, one_b, two, backs = fence(one_a, one_b, two, backs)
+    two_a, two_b = hop(two[far - 1], True), hop(two[far], False)
     one_a, one_b = add_to(one, 2, one_a), add_to(one, -1, one_b)
     block = (RING, own + 8, width)
     grad_one, first_own, first_near, first_far = kernel(
@@ -1050,8 +1057,8 @@
     two_a, two_b = add_to(two, 2, two_a), add_to(two, -3, two_b)
     first_near = swap_row(first_near, 1)
     shown = exchange_row(shown)
-    first_low = (first_far[:far] + first_near[1, :far].astype(F32)).astype(BF16)
-    first_high = (first_far[far:] + first_near[1, far:].astype(F32)).astype(BF16)
+    first_low = (first_far[far:] + first_near[1, far:].astype(F32)).astype(BF16)
+    first_high = (first_far[:far] + first_near[1, :far].astype(F32)).astype(BF16)
     one_a, one_b_end, two_a, two_b, first_near, first_low, first_high, shown = fence(
         one_a, one_b, two_a, two_b, first_near, first_low, first_high, shown
     )
@@ -1074,13 +1081,28 @@
         one_a, two_a, two_b, first_low, first_high, image_grad
     )
     one_a, two_b = hop(one_a, True), hop(add_to(two, -2, two_b), False)
+    first_high = (first_own[:far] + first_near[0, :far].astype(F32) + first_high.astype(F32)).astype(BF16)
     first_low = swap_row(first_low, 2)
-    first_high = (first_own[far:] + first_near[0, far:].astype(F32) + first_high.astype(F32)).astype(BF16)
-    two_a = add_to(two, 1, fence(two_a, first_high)[0])
-    one_a, two_a, two_b, first_low, first_high, shown = fence(one_a, two_a, two_b, first_low, first_high, shown)
-    first_a, first_b = hop(first_high[0], True), hop(first_high[1], False)
+    first_a, first_b, far_a = hop(first_high[0], True), hop(first_high[2], False), hop(first_high[1], True, 2)
+    two_a = add_to(two, 1, two_a)
+    read_grad, bias_rows = kernel(
+        read_end,
+        [shape((width, outs), F32), shape((8, width), F32)],
+        [VM] * 3,
+        [],
+        0,
+        10 * width * outs,
+        read_terms[0],
+        read_a,
+        read_b,
+    )
+    one_a, two_a, two_b, first_low, first_high, first_a, first_b, far_a, shown, read_grad = fence(
+        one_a, two_a, two_b, first_low, first_high, first_a, first_b, far_a, shown, read_grad
+    )
+    first_low = (first_own[far:] + first_near[0, far:].astype(F32) + first_low.astype(F32)).astype(BF16)
+    first_a = (first_low[3].astype(F32) + first_a.astype(F32) + far_a.astype(F32)).astype(BF16)
+    first_a, first_b = hop(first_a, True), hop(add_to(first_high, 3, first_b), False)
     two_a, two_b = hop(two_a, True), hop(add_to(two, -1, two_b), False)
-    first_low = (first_own[:far] + first_near[0, :far].astype(F32) + first_low.astype(F32)).astype(BF16)
     readout_out = kernel(
         join_columns,
         shape((count, 4 * width), BF16),
@@ -1091,25 +1113,20 @@
         where,
         *shown,
     ).reshape(slots, band // 2, cols // 2, 4 * width)
-    read_sum = scatter_end(read_terms, read_a, read_b)
-    two_a, two_b, first_a, first_b, first_low, readout_out, read_sum = fence(
-        two_a, two_b, first_a, first_b, first_low, readout_out, read_sum
-    )
-    first_a, first_b = hop(add_to(first_low, 3, first_a), True), hop(add_to(first_high[far - 2 :], 0, first_b), False)
-    read_grad, bias_row = read_sum[:outs].T, read_sum[outs]
-    bias_grad = lax.dynamic_slice_in_dim(bias_row, dp * outs, outs)
-    first_a, first_b, read_grad = fence(first_a, first_b, read_grad)
-    first_a, first_b = hop(add_to(first_low, 2, first_a), True), hop(add_to(first_high[far - 1 :], 0, first_b), False)
+    one_sum = scatter_end(one, one_a, one_b_end)
+    two_a, two_b, first_a, first_b, first_low, readout_out, one_sum = fence(
+        two_a, two_b, first_a, first_b, first_low, readout_out, one_sum
+    )
+    first_a, first_b = hop(add_to(first_low, 2, first_a), True), hop(add_to(first_low, 0, first_b), False)
+    bias_grad = lax.dynamic_slice(bias_rows, (0, places[2]), (1, outs), allow_negative_indices=False)[0]
     two_sum = scatter_end(two, two_a, two_b)
-    conv_grad = jnp.concatenate([scatter_end(one, one_a, one_b_end), two_sum[:4]], axis=0)
+    conv_grad = jnp.concatenate([one_sum, two_sum[:4]], axis=0)
     conv_grad = conv_grad.reshape(3, 3, own, width)
-    first_a, first_b, conv_grad = fence(first_a, first_b, conv_grad)
-    first_a = hop(add_to(first_low, 1, first_a), True)
-    tail = first_low[0].astype(F32) + first_a.astype(F32) + first_b.astype(F32)
+    tail = first_low[1].astype(F32) + first_a.astype(F32) + first_b.astype(F32)
     first_grad = tail[:own].reshape(own, 4, RING, own).transpose(0, 2, 1, 3).reshape(own, width)
     last_grad = two_sum[4]
-    swapped = lax.dynamic_slice(tail, (own, (row * RING + dp) * own), (2, own))
-    plain = lax.dynamic_slice(tail, (own + 2, (dp * 4 + row) * own), (4, own))
+    swapped = lax.dynamic_slice(tail, (own, places[0]), (2, own), allow_negative_indices=False)
+    plain = lax.dynamic_slice(tail, (own + 2, places[1]), (4, own), allow_negative_indices=False)
     norm_grad = jnp.concatenate([swapped, plain], axis=0)
     return (
         readout_out,

time: 277 us -> 269 us (0.971)
  other arithmetic: 16.2 us -> 7.24 us
  waiting for transfers between devices: 116 us -> 121 us
    ppermute x53, waiting for transfers between devices: 75.7 us -> 81.4 us  [hop(): lax.ppermute(x, 'dp', [(order[i], order[(i + step) % RING]) for i in rang...]
    convert_element_type x11 -> x12, other arithmetic: 6.45 us -> 2.69 us  [add_to(): return (terms[k % RING].astype(F32) + value.astype(F32)).astype(BF16)]
    add x3 -> x2, other arithmetic: 4.65 us -> 1.27 us  [scatter_end(): return terms[0].astype(F32) + a.astype(F32) + b.astype(F32)]
    pallas_call x17 -> x18, Pallas kernels: 54 us -> 55.2 us  [kernel(): pl.pallas_call(body, out_shape=outs, in_specs=ins, out_specs=jax.tree.map...]
  transfers between devices with their start and end apart: 88 -> 88, of which waited for: 50 -> 49; matrix products, arithmetic and copies ran while one was open for 8% -> 4% of each run, Pallas kernels for 18% -> 18%
where the time goes in v1:
time: 269 us; the launch traced here: 268 us
  waiting for transfers between devices  121 us (45%)
  starting transfers between devices  73.6 us (27%)
  Pallas kernels  55.2 us (21%)
  local copies, waits for them, and re-layouts  9.46 us (4%)
  other arithmetic  7.24 us (3%)
    ppermute x53, waiting for transfers between devices, hop(): lax.ppermute(x, 'dp', [(order[i], order[(i + step) % RING]) for i in rang...  81.4 us
    ppermute x53, starting transfers between devices, hop(): lax.ppermute(x, 'dp', [(order[i], order[(i + step) % RING]) for i in rang...  55.4 us
    pallas_call x18, Pallas kernels, kernel(): pl.pallas_call(body, out_shape=outs, in_specs=ins, out_specs=jax.tree.map...  55.2 us
    ppermute x35, waiting for transfers between devices, swap_row(): return lax.ppermute(x, 'row', [(i, i ^ q) for i in range(4)])  39.6 us
    ppermute x35, starting transfers between devices, swap_row(): return lax.ppermute(x, 'row', [(i, i ^ q) for i in range(4)])  18.2 us
  transfers between devices with their start and end apart: 88, of which 49 were waited for; matrix products, arithmetic and copies ran while one was open for 4% of the time, Pallas kernels for 18%

profile of v1, /device:TPU:0, one launch (start us, length us, event | category | flops | bytes accessed | tf_op | source)
XLA Modules:
  0.0 268.5 jit_solution(10796999815439926776)
XLA Ops:
  0.7 3.1 %collective-permute-start.1 = (bf16[9,32,1024]{2,1,0:T(8,128)(2,1)}, bf16[9,32,1024]{2,1,0:T(8,128)(2,1)S(1)}, u32[]{:S(2)}, u32[]{:S(2)}) collective-permute-start(bf16[9,32,1024]{2,1,0:T(8,128)(2,1)} %bitcast.108), channel_id=1, source_target_pairs={{0,8},{8,16},{16,24},{24,28},{28,20},{20,12},{12,4},{4,0},{1,9},{9... | collective-permute-start | bytes 1769480 | tf_op jit(solution)/shard_map/ppermute | solution.py:329
  6.2 2.1 collective-permute-start.3
  11.6 8.8 %collective-permute-done.3.refs_7_ = bf16[72,1024]{1,0:T(8,128)(2,1)S(1)} collective-permute-done((bf16[72,1024]{1,0:T(8,128)(2,1)S(1)}, bf16[72,1024]{1,0:T(8,128)(2,1)S(1)}, u32[]{:S(2)}, u32[]{:S(2)}) %collective-permute-start.3) | collective-permute-done | bytes 147488 | tf_op jit(solution)/shard_map/ppermute | solution.py:329
  20.4 1.5 collective-permute-done.2.refs_1_
  22.2 1.7 collective-permute-start.5
  24.7 2.4 collective-permute-done.4.refs_2_
  27.4 1.7 collective-permute-start.6
  29.4 3.1 %collective-permute-done.6.refs_3_ = bf16[72,1024]{1,0:T(8,128)(2,1)S(1)} collective-permute-done((bf16[72,1024]{1,0:T(8,128)(2,1)S(1)}, bf16[72,1024]{1,0:T(8,128)(2,1)S(1)}, u32[]{:S(2)}, u32[]{:S(2)}) %collective-permute-start.6) | collective-permute-done | bytes 147488 | tf_op jit(solution)/shard_map/ppermute | solution.py:329
  32.5 1.7 collective-permute-done.7.refs_5_
  34.2 1.6 collective-permute-start.9
  36.2 3.8 %collective-permute-done.8.refs_4_ = bf16[32,1024]{1,0:T(8,128)(2,1)S(1)} collective-permute-done((bf16[32,1024]{1,0:T(8,128)(2,1)S(1)}, bf16[32,1024]{1,0:T(8,128)(2,1)S(1)}, u32[]{:S(2)}, u32[]{:S(2)}) %collective-permute-start.8) | collective-permute-done | bytes 65568 | tf_op jit(solution)/shard_map/ppermute | solution.py:329
  40.7 1.6 collective-permute-start.12
  42.3 1.8 collective-permute-start.10
  44.3 13.4 %collective-permute-done.10.refs_2_ = bf16[9,32,1024]{2,1,0:T(8,128)(2,1)S(1)} collective-permute-done((bf16[9,32,1024]{2,1,0:T(8,128)(2,1)S(1)}, bf16[9,32,1024]{2,1,0:T(8,128)(2,1)S(1)}, u32[]{:S(2)}, u32[]{:S(2)}) %collective-permute-start.10) | collective-permute-done | bytes 589856 | tf_op jit(solution)/shard_map/ppermute | solution.py:329
  57.7 1.8 collective-permute-done.11.refs_6_
  59.6 1.8 collective-permute-start.14
  62.2 2.1 shard_map.154
  64.3 11.7 %collective-permute-done.17.l2 = bf16[8,32,1024]{2,1,0:T(8,128)(2,1)S(1)} collective-permute-done((bf16[8,32,1024]{2,1,0:T(8,128)(2,1)S(1)}, bf16[8,32,1024]{2,1,0:T(8,128)(2,1)S(1)}, u32[]{:S(2)}, u32[]{:S(2)}) %collective-permute-start.17) | collective-permute-done | bytes 524320 | tf_op jit(solution)/shard_map/ppermute | solution.py:44
  77.4 1.7 collective-permute-start.20
  80.5 5.4 %collective-permute-done.22.s2 = bf16[288,256]{1,0:T(8,128)(2,1)S(1)} collective-permute-done((bf16[288,256]{1,0:T(8,128)(2,1)S(1)}, bf16[288,256]{1,0:T(8,128)(2,1)S(1)}, u32[]{:S(2)}, u32[]{:S(2)}) %collective-permute-start.22) | collective-permute-done | bytes 147488 | tf_op jit(solution)/shard_map/ppermute | solution.py:44
  87.4 1.8 collective-permute-start.25
  91.1 5.9 %shard_map.155 = (f32[288,1024]{1,0:T(8,128)S(1)}, bf16[288,1024]{1,0:T(8,128)(2,1)S(1)}, bf16[576,2304]{1,0:T(8,128)(2,1)S(1)}, bf16[9,8,32,1024]{3,2,1,0:T(8,128)(2,1)S(1)}) custom-call(s32[18]{0:T(128)S(1)} %compare_select_fusion.10.where, bf16[288,256]{1,0:T(8,128)(2,1)S(1)} %get-tuple-element.460.s0, bf16[288,256]{1,0:T(8,128)(2,1)S(1)} %collective-permute-done.21.s1, ...), custom_call_target="tpu_custom_call" | custom-call | flops 42467328 | bytes 364032 | tf_op jit(solution)/shard_map/pallas_call | solution.py:297
  98.5 1.6 collective-permute-done.30
  102.9 5.4 %shard_map.156 = (f32[288,1024]{1,0:T(8,128)S(1)}, bf16[288,1024]{1,0:T(8,128)(2,1)S(1)}, bf16[576,2304]{1,0:T(8,128)(2,1)S(1)}) custom-call(s32[18]{0:T(128)S(1)} %compare_select_fusion.10.where, bf16[288,256]{1,0:T(8,128)(2,1)S(1)} %get-tuple-element.460.s0, bf16[288,256]{1,0:T(8,128)(2,1)S(1)} %collective-permute-done.21.s1, ...), custom_call_target="tpu_custom_call" | custom-call | flops 42467328 | bytes 364032 | tf_op jit(solution)/shard_map/pallas_call | solution.py:297
  110.1 1.5 collective-permute-start.36
  111.7 6.7 %collective-permute-done.35.refs_3_ = bf16[128,1024]{1,0:T(8,128)(2,1)S(1)} collective-permute-done((bf16[128,1024]{1,0:T(8,128)(2,1)S(1)}, bf16[128,1024]{1,0:T(8,128)(2,1)S(1)}, u32[]{:S(2)}, u32[]{:S(2)}) %collective-permute-start.35) | collective-permute-done | bytes 262176 | tf_op jit(solution)/shard_map/ppermute | solution.py:329
  118.6 2.3 shard_map.157
  121.0 1.4 collective-permute-start.37
  123.0 1.5 collective-permute-start.39
  124.5 3.5 %collective-permute-done.40.refs_8_ = bf16[64,1024]{1,0:T(8,128)(2,1)S(1)} collective-permute-done((bf16[64,1024]{1,0:T(8,128)(2,1)S(1)}, bf16[64,1024]{1,0:T(8,128)(2,1)S(1)}, u32[]{:S(2)}, u32[]{:S(2)}) %collective-permute-start.40) | collective-permute-done | bytes 131104 | tf_op jit(solution)/shard_map/ppermute | solution.py:329
  129.7 3.1 %shard_map.158 = (bf16[72,1024]{1,0:T(8,128)(2,1)S(1)}, bf16[72,1024]{1,0:T(8,128)(2,1)S(1)}, bf16[72,1024]{1,0:T(8,128)(2,1)S(1)}, bf16[72,1024]{1,0:T(8,128)(2...) custom-call(s32[18]{0:T(128)S(1)} %compare_select_fusion.10.where, ...), custom_call_target="tpu_custom_call" | custom-call | flops 18874368 | bytes 88064 | tf_op jit(solution)/shard_map/pallas_call | solution.py:297
  133.0 1.4 collective-permute-done.42
  135.3 2.2 shard_map.159
  137.5 3.0 %collective-permute-done.43.cross = bf16[72,1024]{1,0:T(8,128)(2,1)S(1)} collective-permute-done((bf16[72,1024]{1,0:T(8,128)(2,1)S(1)}, bf16[72,1024]{1,0:T(8,128)(2,1)S(1)}, u32[]{:S(2)}, u32[]{:S(2)}) %collective-permute-start.43) | collective-permute-done | bytes 147488 | tf_op jit(solution)/shard_map/ppermute | solution.py:44
  140.5 1.5 collective-permute-start.44
  142.5 2.6 shard_map.160
  145.6 1.5 collective-permute-done.45
  150.1 4.3 %collective-permute-done.48 = bf16[144,1024]{1,0:T(8,128)(2,1)S(1)} collective-permute-done((bf16[144,1024]{1,0:T(8,128)(2,1)S(1)}, bf16[144,1024]{1,0:T(8,128)(2,1)S(1)}, u32[]{:S(2)}, u32[]{:S(2)}) %collective-permute-start.48) | collective-permute-done | bytes 294944 | tf_op jit(solution)/shard_map/ppermute | solution.py:329
  157.7 2.1 shard_map.161
  159.8 6.1 %shard_map.162.half = f32[9,256,1024]{2,1,0:T(8,128)S(1)} custom-call(s32[18]{0:T(128)S(1)} %compare_select_fusion.10.where, bf16[576,2304]{1,0:T(8,128)(2,1)S(1)} %get-tuple-element.544.here, bf16[288,1024]{1,0:T(8,128)(2,1)S(1)} %get-tuple-element.573.g0, bf16[288,1024]{1,0:T(8,128)(2,1)S(1)} %collective-permute-done.47.g1), custom_call_target="tpu_custom_call" | custom-call | flops 42467328 | bytes 589824 | tf_op jit(solution)/shard_map/pallas_call | solution.py:297
  170.5 3.8 %shard_map.163 = (bf16[5,32,1024]{2,1,0:T(8,128)(2,1)S(1)}, bf16[5,32,1024]{2,1,0:T(8,128)(2,1)S(1)}, bf16[5,32,1024]{2,1,0:T(8,128)(2,1)S(1)}, bf16[5,32,1024]{...) custom-call(s32[18]{0:T(128)S(1)} %compare_select_fusion.10.where, ...), custom_call_target="tpu_custom_call" | custom-call | flops 47185920 | bytes 327680 | tf_op jit(solution)/shard_map/pallas_call | solution.py:297
  176.3 1.4 collective-permute-done.54.refs_2_
  180.9 8.0 %shard_map.164 = (bf16[288,256]{1,0:T(8,128)(2,1)S(1)}, bf16[288,256]{1,0:T(8,128)(2,1)S(1)}, bf16[288,256]{1,0:T(8,128)(2,1)S(1)}, bf16[288,256]{1,0:T(8,128)(2,1)S(1)}) custom-call(s32[18]{0:T(128)S(1)} %compare_select_fusion.10.where, bf16[288,1024]{1,0:T(8,128)(2,1)S(1)} %get-tuple-element.573.g0, bf16[288,1024]{1,0:T(8,128)(2,1)S(1)} %collective-permute-done.47.g1, ...), custom_call_target="tpu_custom_call" | custom-call | flops 84934656 | bytes 350208 | tf_op jit(solution)/shard_map/pallas_call | solution.py:297
  189.7 1.6 collective-permute-start.60
  193.1 3.4 %shard_map.165 = (bf16[5,32,1024]{2,1,0:T(8,128)(2,1)S(1)}, bf16[5,32,1024]{2,1,0:T(8,128)(2,1)S(1)}, bf16[5,32,1024]{2,1,0:T(8,128)(2,1)S(1)}, bf16[5,32,1024]{...) custom-call(s32[18]{0:T(128)S(1)} %compare_select_fusion.10.where, ...), custom_call_target="tpu_custom_call" | custom-call | flops 37748736 | bytes 262144 | tf_op jit(solution)/shard_map/pallas_call | solution.py:297
  197.9 2.4 collective-permute-done.64.b3
  202.4 3.2 %shard_map.166 = (bf16[288,1024]{1,0:T(8,128)(2,1)S(1)}, f32[8,40,1024]{2,1,0:T(8,128)S(1)}, bf16[2,8,40,1024]{3,2,1,0:T(8,128)(2,1)S(1)}, f32[8,40,1024]{2,1,0:T(8,128)S(1)}) custom-call(s32[18]{0:T(128)S(1)} %compare_select_fusion.10.where, bf16[288,256]{1,0:T(8,128)(2,1)S(1)} %get-tuple-element.608.b0, bf16[288,256]{1,0:T(8,128)(2,1)S(1)} %collective-permute-done.62.b1, ...), custom_call_target="tpu_custom_call" | custom-call | flops 9437184 | bytes 135168 | tf_op jit(solution)/shard_map/pallas_call | solution.py:297
  205.7 4.4 %collective-permute-done.65 = bf16[5,32,1024]{2,1,0:T(8,128)(2,1)S(1)} collective-permute-done((bf16[5,32,1024]{2,1,0:T(8,128)(2,1)S(1)}, bf16[5,32,1024]{2,1,0:T(8,128)(2,1)S(1)}, u32[]{:S(2)}, u32[]{:S(2)}) %collective-permute-start.65) | collective-permute-done | bytes 327712 | tf_op jit(solution)/shard_map/ppermute | solution.py:329
  212.2 1.7 collective-permute-start.68
  214.7 2.4 collective-permute-done.71.i2
  217.1 3.2 %collective-permute-done.72.i3 = bf16[72,1024]{1,0:T(8,128)(2,1)S(1)} collective-permute-done((bf16[72,1024]{1,0:T(8,128)(2,1)S(1)}, bf16[72,1024]{1,0:T(8,128)(2,1)S(1)}, u32[]{:S(2)}, u32[]{:S(2)}) %collective-permute-start.72) | collective-permute-done | bytes 147488 | tf_op jit(solution)/shard_map/ppermute | solution.py:44
  221.6 1.7 collective-permute-start.74
  223.3 1.5 collective-permute-start.75
  225.9 2.2 shard_map.167
  228.1 2.0 collective-permute-done.73
  232.1 1.6 collective-permute-start.76
  235.8 1.7 collective-permute-start.80
  238.9 2.8 %collective-permute-done.80 = bf16[40,1024]{1,0:T(8,128)(2,1)S(1)} collective-permute-done((bf16[40,1024]{1,0:T(8,128)(2,1)S(1)}, bf16[40,1024]{1,0:T(8,128)(2,1)S(1)}, u32[]{:S(2)}, u32[]{:S(2)}) %collective-permute-start.80) | collective-permute-done | bytes 81952 | tf_op jit(solution)/shard_map/ppermute | solution.py:329
  241.7 1.5 collective-permute-done.79
  243.4 2.7 collective-permute-start.85
  247.5 1.5 collective-permute-start.82
  250.3 5.5 %collective-permute-done.84 = bf16[40,1024]{1,0:T(8,128)(2,1)} collective-permute-done((bf16[40,1024]{1,0:T(8,128)(2,1)S(1)}, bf16[40,1024]{1,0:T(8,128)(2,1)}, u32[]{:S(2)}, u32[]{:S(2)}) %collective-permute-start.84) | collective-permute-done | bytes 81952 | tf_op jit(solution)/shard_map/ppermute | solution.py:329
  260.0 1.8 collective-permute-start.86
  264.5 1.7 collective-permute-done.87
  (209 shorter events, 70.9 us)
Async XLA Ops:
  0.7 21.2 %collective-permute-start.1 = (bf16[9,32,1024]{2,1,0:T(8,128)(2,1)}, bf16[9,32,1024]{2,1,0:T(8,128)(2,1)S(1)}, u32[]{:S(2)}, u32[]{:S(2)}) collective-permute-start(bf16[9,32,1024]{2,1,0:T(8,128)(2,1)} %bitcast.108), channel_id=1, source_target_pairs={{0,8},{8,16},{16,24},{24,28},{28,20},{20,12},{12,4},{4,0},{1,9},{9... | collective-permute-start | bytes 1769480 | tf_op jit(solution)/shard_map/ppermute | solution.py:329
  3.8 18.2 %collective-permute-start = (bf16[9,32,1024]{2,1,0:T(8,128)(2,1)}, bf16[9,32,1024]{2,1,0:T(8,128)(2,1)S(1)}, u32[]{:S(2)}, u32[]{:S(2)}) collective-permute-start(bf16[9,32,1024]{2,1,0:T(8,128)(2,1)} %bitcast.109), channel_id=1, source_target_pairs={{0,4},{8,0},{16,8},{24,16},{28,24},{20,28},{12,20},{4,12},{1,5},{9... | collective-permute-start | bytes 1769480 | tf_op jit(solution)/shard_map/ppermute | solution.py:329
  6.2 14.2 %collective-permute-start.3 = (bf16[72,1024]{1,0:T(8,128)(2,1)S(1)}, bf16[72,1024]{1,0:T(8,128)(2,1)S(1)}, u32[]{:S(2)}, u32[]{:S(2)}) collective-permute-start(bf16[72,1024]{1,0:T(8,128)(2,1)S(1)} %concatenate.17.refs_0_), channel_id=1, source_target_pairs={{0,8},{8,16},{16,24},{24,28},{28,20},{20,12},{12,4},{4,0},{1,9},{9... | collective-permute-start | bytes 442376 | tf_op jit(solution)/shard_map/ppermute | solution.py:329
  8.2 13.7 %collective-permute-start.2 = (bf16[72,1024]{1,0:T(8,128)(2,1)S(1)}, bf16[72,1024]{1,0:T(8,128)(2,1)S(1)}, u32[]{:S(2)}, u32[]{:S(2)}) collective-permute-start(bf16[72,1024]{1,0:T(8,128)(2,1)S(1)} %concatenate.17.refs_0_), channel_id=1, source_target_pairs={{0,4},{8,0},{16,8},{24,16},{28,24},{20,28},{12,20},{4,12},{1,5},{9... | collective-permute-start | bytes 442376 | tf_op jit(solution)/shard_map/ppermute | solution.py:329
  34.2 5.9 %collective-permute-start.9 = (bf16[40,1024]{1,0:T(8,128)(2,1)S(1)}, bf16[40,1024]{1,0:T(8,128)(2,1)S(1)}, u32[]{:S(2)}, u32[]{:S(2)}) collective-permute-start(bf16[40,1024]{1,0:T(8,128)(2,1)S(1)} %slice.147), channel_id=1, source_target_pairs={{0,4},{8,0},{16,8},{24,16},{28,24},{20,28},{12,20},{4,12},{1,5},{9... | collective-permute-start | bytes 245768 | tf_op jit(solution)/shard_map/ppermute | solution.py:329
  40.7 18.9 %collective-permute-start.13 = (bf16[8,40,1024]{2,1,0:T(8,128)(2,1)S(1)}, bf16[8,40,1024]{2,1,0:T(8,128)(2,1)S(1)}, u32[]{:S(2)}, u32[]{:S(2)}) collective-permute-start(bf16[8,40,1024]{2,1,0:T(8,128)(2,1)S(1)} %get-tuple-element.404.f0), channel_id=1, source_target_pairs={{0,1},{1,0},{2,3},{3,2},{4,5},{5,4},{6,7},{7,6},{8,9},{9,8},{10,11... | collective-permute-start | bytes 1966088 | tf_op jit(solution)/shard_map/ppermute | solution.py:44
  40.7 18.8 %collective-permute-start.12 = (bf16[8,40,1024]{2,1,0:T(8,128)(2,1)S(1)}, bf16[8,40,1024]{2,1,0:T(8,128)(2,1)S(1)}, u32[]{:S(2)}, u32[]{:S(2)}) collective-permute-start(bf16[8,40,1024]{2,1,0:T(8,128)(2,1)S(1)} %get-tuple-element.404.f0), channel_id=1, source_target_pairs={{0,2},{1,3},{2,0},{3,1},{4,6},{5,7},{6,4},{7,5},{8,10},{9,11},{10,... | collective-permute-start | bytes 1966088 | tf_op jit(solution)/shard_map/ppermute | solution.py:44
  42.3 15.4 %collective-permute-start.10 = (bf16[9,32,1024]{2,1,0:T(8,128)(2,1)S(1)}, bf16[9,32,1024]{2,1,0:T(8,128)(2,1)S(1)}, u32[]{:S(2)}, u32[]{:S(2)}) collective-permute-start(bf16[9,32,1024]{2,1,0:T(8,128)(2,1)S(1)} %collective-permute-done.refs_1_), channel_id=1, source_target_pairs={{0,4},{8,0},{16,8},{24,16},{28,24},{20,28},{12,20},{4,12},{1,5},{9... | collective-permute-start | bytes 1769480 | tf_op jit(solution)/shard_map/ppermute | solution.py:329
  44.1 15.4 %collective-permute-start.11 = (bf16[9,32,1024]{2,1,0:T(8,128)(2,1)S(1)}, bf16[9,32,1024]{2,1,0:T(8,128)(2,1)S(1)}, u32[]{:S(2)}, u32[]{:S(2)}) collective-permute-start(bf16[9,32,1024]{2,1,0:T(8,128)(2,1)S(1)} %collective-permute-done.1.refs_7_), channel_id=1, source_target_pairs={{0,8},{8,16},{16,24},{24,28},{28,20},{20,12},{12,4},{4,0},{1,9},{9... | collective-permute-start | bytes 1769480 | tf_op jit(solution)/shard_map/ppermute | solution.py:329
  59.6 16.4 %collective-permute-start.14 = (bf16[9,32,1024]{2,1,0:T(8,128)(2,1)S(1)}, bf16[9,32,1024]{2,1,0:T(8,128)(2,1)S(1)}, u32[]{:S(2)}, u32[]{:S(2)}) collective-permute-start(bf16[9,32,1024]{2,1,0:T(8,128)(2,1)S(1)} %collective-permute-done.10.refs_2_), channel_id=1, source_target_pairs={{0,4},{8,0},{16,8},{24,16},{28,24},{20,28},{12,20},{4,12},{1,5},{9... | collective-permute-start | bytes 1769480 | tf_op jit(solution)/shard_map/ppermute | solution.py:329
  61.3 15.4 %collective-permute-start.15 = (bf16[9,32,1024]{2,1,0:T(8,128)(2,1)S(1)}, bf16[9,32,1024]{2,1,0:T(8,128)(2,1)S(1)}, u32[]{:S(2)}, u32[]{:S(2)}) collective-permute-start(bf16[9,32,1024]{2,1,0:T(8,128)(2,1)S(1)} %collective-permute-done.11.refs_6_), channel_id=1, source_target_pairs={{0,8},{8,16},{16,24},{24,28},{28,20},{20,12},{12,4},{4,0},{1,9},{9... | collective-permute-start | bytes 1769480 | tf_op jit(solution)/shard_map/ppermute | solution.py:329
  61.6 14.3 %collective-permute-start.17 = (bf16[8,32,1024]{2,1,0:T(8,128)(2,1)S(1)}, bf16[8,32,1024]{2,1,0:T(8,128)(2,1)S(1)}, u32[]{:S(2)}, u32[]{:S(2)}) collective-permute-start(bf16[8,32,1024]{2,1,0:T(8,128)(2,1)S(1)} %get-tuple-element.485.l0), channel_id=1, source_target_pairs={{0,2},{1,3},{2,0},{3,1},{4,6},{5,7},{6,4},{7,5},{8,10},{9,11},{10,... | collective-permute-start | bytes 1572872 | tf_op jit(solution)/shard_map/ppermute | solution.py:44
  76.8 10.4 %collective-permute-start.24 = (bf16[8,32,1024]{2,1,0:T(8,128)(2,1)S(1)}, bf16[8,32,1024]{2,1,0:T(8,128)(2,1)S(1)}, u32[]{:S(2)}, u32[]{:S(2)}) collective-permute-start(bf16[8,32,1024]{2,1,0:T(8,128)(2,1)S(1)} %collective-permute-done.17.l2), channel_id=1, source_target_pairs={{0,1},{1,0},{2,3},{3,2},{4,5},{5,4},{6,7},{7,6},{8,9},{9,8},{10,11... | collective-permute-start | bytes 1572872 | tf_op jit(solution)/shard_map/ppermute | solution.py:44
  76.8 10.3 %collective-permute-start.19 = (bf16[5,32,1024]{2,1,0:T(8,128)(2,1)S(1)}, bf16[5,32,1024]{2,1,0:T(8,128)(2,1)S(1)}, u32[]{:S(2)}, u32[]{:S(2)}) collective-permute-start(bf16[5,32,1024]{2,1,0:T(8,128)(2,1)S(1)} %slice.148), channel_id=1, source_target_pairs={{0,8},{8,16},{16,24},{24,28},{28,20},{20,12},{12,4},{4,0},{1,9},{9... | collective-permute-start | bytes 983048 | tf_op jit(solution)/shard_map/ppermute | solution.py:329
  77.4 9.7 %collective-permute-start.20 = (bf16[4,32,1024]{2,1,0:T(8,128)(2,1)S(1)}, bf16[4,32,1024]{2,1,0:T(8,128)(2,1)S(1)}, u32[]{:S(2)}, u32[]{:S(2)}) collective-permute-start(bf16[4,32,1024]{2,1,0:T(8,128)(2,1)S(1)} %slice.149), channel_id=1, source_target_pairs={{0,4},{8,0},{16,8},{24,16},{28,24},{20,28},{12,20},{4,12},{1,5},{9... | collective-permute-start | bytes 786440 | tf_op jit(solution)/shard_map/ppermute | solution.py:329
  79.2 6.7 %collective-permute-start.22 = (bf16[288,256]{1,0:T(8,128)(2,1)S(1)}, bf16[288,256]{1,0:T(8,128)(2,1)S(1)}, u32[]{:S(2)}, u32[]{:S(2)}) collective-permute-start(bf16[288,256]{1,0:T(8,128)(2,1)S(1)} %get-tuple-element.423), channel_id=1, source_target_pairs={{0,2},{1,3},{2,0},{3,1},{4,6},{5,7},{6,4},{7,5},{8,10},{9,11},{10,... | collective-permute-start | bytes 442376 | tf_op jit(solution)/shard_map/ppermute | solution.py:44
  79.7 7.4 %collective-permute-start.23 = (bf16[288,256]{1,0:T(8,128)(2,1)S(1)}, bf16[288,256]{1,0:T(8,128)(2,1)S(1)}, u32[]{:S(2)}, u32[]{:S(2)}) collective-permute-start(bf16[288,256]{1,0:T(8,128)(2,1)S(1)} %get-tuple-element.424), channel_id=1, source_target_pairs={{0,3},{1,2},{2,1},{3,0},{4,7},{5,6},{6,5},{7,4},{8,11},{9,10},{10,... | collective-permute-start | bytes 442376 | tf_op jit(solution)/shard_map/ppermute | solution.py:44
  87.1 10.9 %collective-permute-start.26 = (bf16[128,1024]{1,0:T(8,128)(2,1)S(1)}, bf16[128,1024]{1,0:T(8,128)(2,1)S(1)}, u32[]{:S(2)}, u32[]{:S(2)}) collective-permute-start(bf16[128,1024]{1,0:T(8,128)(2,1)S(1)} %bitcast.105), channel_id=1, source_target_pairs={{0,8},{8,16},{16,24},{24,28},{28,20},{20,12},{12,4},{4,0},{1,9},{9... | collective-permute-start | bytes 786440 | tf_op jit(solution)/shard_map/ppermute | solution.py:329
  87.4 10.6 %collective-permute-start.25 = (bf16[128,1024]{1,0:T(8,128)(2,1)S(1)}, bf16[128,1024]{1,0:T(8,128)(2,1)S(1)}, u32[]{:S(2)}, u32[]{:S(2)}) collective-permute-start(bf16[128,1024]{1,0:T(8,128)(2,1)S(1)} %bitcast.106), channel_id=1, source_target_pairs={{0,4},{8,0},{16,8},{24,16},{28,24},{20,28},{12,20},{4,12},{1,5},{9... | collective-permute-start | bytes 786440 | tf_op jit(solution)/shard_map/ppermute | solution.py:329
  89.2 7.7 %collective-permute-start.27 = (bf16[72,1024]{1,0:T(8,128)(2,1)S(1)}, bf16[72,1024]{1,0:T(8,128)(2,1)S(1)}, u32[]{:S(2)}, u32[]{:S(2)}) collective-permute-start(bf16[72,1024]{1,0:T(8,128)(2,1)S(1)} %get-tuple-element.450), channel_id=1, source_target_pairs={{0,1},{1,0},{2,3},{3,2},{4,5},{5,4},{6,7},{7,6},{8,9},{9,8},{10,11... | collective-permute-start | bytes 442376 | tf_op jit(solution)/shard_map/ppermute | solution.py:44
  89.4 7.5 %collective-permute-start.28 = (bf16[72,1024]{1,0:T(8,128)(2,1)S(1)}, bf16[72,1024]{1,0:T(8,128)(2,1)S(1)}, u32[]{:S(2)}, u32[]{:S(2)}) collective-permute-start(bf16[72,1024]{1,0:T(8,128)(2,1)S(1)} %get-tuple-element.451), channel_id=1, source_target_pairs={{0,2},{1,3},{2,0},{3,1},{4,6},{5,7},{6,4},{7,5},{8,10},{9,11},{10,... | collective-permute-start | bytes 442376 | tf_op jit(solution)/shard_map/ppermute | solution.py:44
  90.0 8.0 %collective-permute-start.29 = (bf16[72,1024]{1,0:T(8,128)(2,1)S(1)}, bf16[72,1024]{1,0:T(8,128)(2,1)S(1)}, u32[]{:S(2)}, u32[]{:S(2)}) collective-permute-start(bf16[72,1024]{1,0:T(8,128)(2,1)S(1)} %get-tuple-element.452), channel_id=1, source_target_pairs={{0,3},{1,2},{2,1},{3,0},{4,7},{5,6},{6,5},{7,4},{8,11},{9,10},{10,... | collective-permute-start | bytes 442376 | tf_op jit(solution)/shard_map/ppermute | solution.py:44
  100.3 8.6 %collective-permute-start.31 = (bf16[128,1024]{1,0:T(8,128)(2,1)S(1)}, bf16[128,1024]{1,0:T(8,128)(2,1)S(1)}, u32[]{:S(2)}, u32[]{:S(2)}) collective-permute-start(bf16[128,1024]{1,0:T(8,128)(2,1)S(1)} %collective-permute-done.25.refs_1_), channel_id=1, source_target_pairs={{0,4},{8,0},{16,8},{24,16},{28,24},{20,28},{12,20},{4,12},{1,5},{9... | collective-permute-start | bytes 786440 | tf_op jit(solution)/shard_map/ppermute | solution.py:329
  101.3 8.3 %collective-permute-start.32 = (bf16[128,1024]{1,0:T(8,128)(2,1)S(1)}, bf16[128,1024]{1,0:T(8,128)(2,1)S(1)}, u32[]{:S(2)}, u32[]{:S(2)}) collective-permute-start(bf16[128,1024]{1,0:T(8,128)(2,1)S(1)} %collective-permute-done.26.refs_7_), channel_id=1, source_target_pairs={{0,8},{8,16},{16,24},{24,28},{28,20},{20,12},{12,4},{4,0},{1,9},{9... | collective-permute-start | bytes 786440 | tf_op jit(solution)/shard_map/ppermute | solution.py:329
  102.4 16.2 %collective-permute-start.34 = (bf16[288,1024]{1,0:T(8,128)(2,1)S(1)}, bf16[288,1024]{1,0:T(8,128)(2,1)S(1)}, u32[]{:S(2)}, u32[]{:S(2)}) collective-permute-start(bf16[288,1024]{1,0:T(8,128)(2,1)S(1)} %add_convert_fusion), channel_id=1, source_target_pairs={{0,2},{1,3},{2,0},{3,1},{4,6},{5,7},{6,4},{7,5},{8,10},{9,11},{10,... | collective-permute-start | bytes 1769480 | tf_op jit(solution)/shard_map/ppermute | solution.py:44
  109.6 9.0 %collective-permute-start.33 = (bf16[288,1024]{1,0:T(8,128)(2,1)S(1)}, bf16[288,1024]{1,0:T(8,128)(2,1)S(1)}, u32[]{:S(2)}, u32[]{:S(2)}) collective-permute-start(bf16[288,1024]{1,0:T(8,128)(2,1)S(1)} %get-tuple-element.472), channel_id=1, source_target_pairs={{0,1},{1,0},{2,3},{3,2},{4,5},{5,4},{6,7},{7,6},{8,9},{9,8},{10,11... | collective-permute-start | bytes 1769480 | tf_op jit(solution)/shard_map/ppermute | solution.py:44
  109.6 8.7 %collective-permute-start.35 = (bf16[128,1024]{1,0:T(8,128)(2,1)S(1)}, bf16[128,1024]{1,0:T(8,128)(2,1)S(1)}, u32[]{:S(2)}, u32[]{:S(2)}) collective-permute-start(bf16[128,1024]{1,0:T(8,128)(2,1)S(1)} %collective-permute-done.31.refs_2_), channel_id=1, source_target_pairs={{0,4},{8,0},{16,8},{24,16},{28,24},{20,28},{12,20},{4,12},{1,5},{9... | collective-permute-start | bytes 786440 | tf_op jit(solution)/shard_map/ppermute | solution.py:329
  110.1 8.4 %collective-permute-start.36 = (bf16[128,1024]{1,0:T(8,128)(2,1)S(1)}, bf16[128,1024]{1,0:T(8,128)(2,1)S(1)}, u32[]{:S(2)}, u32[]{:S(2)}) collective-permute-start(bf16[128,1024]{1,0:T(8,128)(2,1)S(1)} %collective-permute-done.32.refs_6_), channel_id=1, source_target_pairs={{0,8},{8,16},{16,24},{24,28},{28,20},{20,12},{12,4},{4,0},{1,9},{9... | collective-permute-start | bytes 786440 | tf_op jit(solution)/shard_map/ppermute | solution.py:329
  120.9 7.4 %collective-permute-start.38 = (bf16[72,1024]{1,0:T(8,128)(2,1)S(1)}, bf16[72,1024]{1,0:T(8,128)(2,1)S(1)}, u32[]{:S(2)}, u32[]{:S(2)}) collective-permute-start(bf16[72,1024]{1,0:T(8,128)(2,1)S(1)} %get-tuple-element.499.p0), channel_id=1, source_target_pairs={{0,1},{1,0},{2,3},{3,2},{4,5},{5,4},{6,7},{7,6},{8,9},{9,8},{10,11... | collective-permute-start | bytes 442376 | tf_op jit(solution)/shard_map/ppermute | solution.py:44
  121.0 7.3 %collective-permute-start.37 = (bf16[72,1024]{1,0:T(8,128)(2,1)S(1)}, bf16[72,1024]{1,0:T(8,128)(2,1)S(1)}, u32[]{:S(2)}, u32[]{:S(2)}) collective-permute-start(bf16[72,1024]{1,0:T(8,128)(2,1)S(1)} %get-tuple-element.499.p0), channel_id=1, source_target_pairs={{0,2},{1,3},{2,0},{3,1},{4,6},{5,7},{6,4},{7,5},{8,10},{9,11},{10,... | collective-permute-start | bytes 442376 | tf_op jit(solution)/shard_map/ppermute | solution.py:44
  134.5 6.0 %collective-permute-start.43 = (bf16[72,1024]{1,0:T(8,128)(2,1)S(1)}, bf16[72,1024]{1,0:T(8,128)(2,1)S(1)}, u32[]{:S(2)}, u32[]{:S(2)}) collective-permute-start(bf16[72,1024]{1,0:T(8,128)(2,1)S(1)} %fusion.14), channel_id=1, source_target_pairs={{0,2},{1,3},{2,0},{3,1},{4,6},{5,7},{6,4},{7,5},{8,10},{9,11},{10,... | collective-permute-start | bytes 442376 | tf_op jit(solution)/shard_map/ppermute | solution.py:44
  147.2 7.1 %collective-permute-start.48 = (bf16[144,1024]{1,0:T(8,128)(2,1)S(1)}, bf16[144,1024]{1,0:T(8,128)(2,1)S(1)}, u32[]{:S(2)}, u32[]{:S(2)}) collective-permute-start(bf16[144,1024]{1,0:T(8,128)(2,1)S(1)} %pad_maximum_fusion.1), channel_id=1, source_target_pairs={{0,8},{8,16},{16,24},{24,28},{28,20},{20,12},{12,4},{4,0},{1,9},{9... | collective-permute-start | bytes 884744 | tf_op jit(solution)/shard_map/ppermute | solution.py:329
  148.4 7.0 %collective-permute-start.50 = (bf16[144,1024]{1,0:T(8,128)(2,1)S(1)}, bf16[144,1024]{1,0:T(8,128)(2,1)S(1)}, u32[]{:S(2)}, u32[]{:S(2)}) collective-permute-start(bf16[144,1024]{1,0:T(8,128)(2,1)S(1)} %pad_maximum_fusion.2), channel_id=1, source_target_pairs={{0,4},{8,0},{16,8},{24,16},{28,24},{20,28},{12,20},{4,12},{1,5},{9... | collective-permute-start | bytes 884744 | tf_op jit(solution)/shard_map/ppermute | solution.py:329
  149.4 10.4 %collective-permute-start.47 = (bf16[288,1024]{1,0:T(8,128)(2,1)S(1)}, bf16[288,1024]{1,0:T(8,128)(2,1)S(1)}, u32[]{:S(2)}, u32[]{:S(2)}) collective-permute-start(bf16[288,1024]{1,0:T(8,128)(2,1)S(1)} %get-tuple-element.573.g0), channel_id=1, source_target_pairs={{0,1},{1,0},{2,3},{3,2},{4,5},{5,4},{6,7},{7,6},{8,9},{9,8},{10,11... | collective-permute-start | bytes 1769480 | tf_op jit(solution)/shard_map/ppermute | solution.py:44
  149.4 16.4 %collective-permute-start.46 = (bf16[288,1024]{1,0:T(8,128)(2,1)S(1)}, bf16[288,1024]{1,0:T(8,128)(2,1)S(1)}, u32[]{:S(2)}, u32[]{:S(2)}) collective-permute-start(bf16[288,1024]{1,0:T(8,128)(2,1)S(1)} %get-tuple-element.573.g0), channel_id=1, source_target_pairs={{0,2},{1,3},{2,0},{3,1},{4,6},{5,7},{6,4},{7,5},{8,10},{9,11},{10,... | collective-permute-start | bytes 1769480 | tf_op jit(solution)/shard_map/ppermute | solution.py:44
  155.6 10.2 %collective-permute-start.51 = (bf16[144,1024]{1,0:T(8,128)(2,1)S(1)}, bf16[144,1024]{1,0:T(8,128)(2,1)S(1)}, u32[]{:S(2)}, u32[]{:S(2)}) collective-permute-start(bf16[144,1024]{1,0:T(8,128)(2,1)S(1)} %get-tuple-element.708), channel_id=1, source_target_pairs={{0,4},{8,0},{16,8},{24,16},{28,24},{20,28},{12,20},{4,12},{1,5},{9... | collective-permute-start | bytes 884744 | tf_op jit(solution)/shard_map/ppermute | solution.py:329
  156.5 9.3 %collective-permute-start.49 = (bf16[144,1024]{1,0:T(8,128)(2,1)S(1)}, bf16[144,1024]{1,0:T(8,128)(2,1)S(1)}, u32[]{:S(2)}, u32[]{:S(2)}) collective-permute-start(bf16[144,1024]{1,0:T(8,128)(2,1)S(1)} %get-tuple-element.709), channel_id=1, source_target_pairs={{0,8},{8,16},{16,24},{24,28},{28,20},{20,12},{12,4},{4,0},{1,9},{9... | collective-permute-start | bytes 884744 | tf_op jit(solution)/shard_map/ppermute | solution.py:329
  166.7 9.0 %collective-permute-start.56 = (bf16[144,1024]{1,0:T(8,128)(2,1)S(1)}, bf16[144,1024]{1,0:T(8,128)(2,1)S(1)}, u32[]{:S(2)}, u32[]{:S(2)}) collective-permute-start(bf16[144,1024]{1,0:T(8,128)(2,1)S(1)} %get-tuple-element.706), channel_id=1, source_target_pairs={{0,4},{8,0},{16,8},{24,16},{28,24},{20,28},{12,20},{4,12},{1,5},{9... | collective-permute-start | bytes 884744 | tf_op jit(solution)/shard_map/ppermute | solution.py:329
  167.6 8.7 %collective-permute-start.55 = (bf16[144,1024]{1,0:T(8,128)(2,1)S(1)}, bf16[144,1024]{1,0:T(8,128)(2,1)S(1)}, u32[]{:S(2)}, u32[]{:S(2)}) collective-permute-start(bf16[144,1024]{1,0:T(8,128)(2,1)S(1)} %get-tuple-element.707), channel_id=1, source_target_pairs={{0,8},{8,16},{16,24},{24,28},{28,20},{20,12},{12,4},{4,0},{1,9},{9... | collective-permute-start | bytes 884744 | tf_op jit(solution)/shard_map/ppermute | solution.py:329
  169.4 8.3 %collective-permute-start.54 = (bf16[4,32,1024]{2,1,0:T(8,128)(2,1)S(1)}, bf16[4,32,1024]{2,1,0:T(8,128)(2,1)S(1)}, u32[]{:S(2)}, u32[]{:S(2)}) collective-permute-start(bf16[4,32,1024]{2,1,0:T(8,128)(2,1)S(1)} %get-tuple-element.564), channel_id=1, source_target_pairs={{0,2},{1,3},{2,0},{3,1},{4,6},{5,7},{6,4},{7,5},{8,10},{9,11},{10,... | collective-permute-start | bytes 786440 | tf_op jit(solution)/shard_map/ppermute | solution.py:44
  177.8 11.1 %collective-permute-start.57 = (bf16[5,32,1024]{2,1,0:T(8,128)(2,1)S(1)}, bf16[5,32,1024]{2,1,0:T(8,128)(2,1)S(1)}, u32[]{:S(2)}, u32[]{:S(2)}) collective-permute-start(bf16[5,32,1024]{2,1,0:T(8,128)(2,1)S(1)} %get-tuple-element.571), channel_id=1, source_target_pairs={{0,8},{8,16},{16,24},{24,28},{28,20},{20,12},{12,4},{4,0},{1,9},{9... | collective-permute-start | bytes 983048 | tf_op jit(solution)/shard_map/ppermute | solution.py:329
  178.4 10.5 %collective-permute-start.58 = (bf16[5,32,1024]{2,1,0:T(8,128)(2,1)S(1)}, bf16[5,32,1024]{2,1,0:T(8,128)(2,1)S(1)}, u32[]{:S(2)}, u32[]{:S(2)}) collective-permute-start(bf16[5,32,1024]{2,1,0:T(8,128)(2,1)S(1)} %get-tuple-element.572), channel_id=1, source_target_pairs={{0,4},{8,0},{16,8},{24,16},{28,24},{20,28},{12,20},{4,12},{1,5},{9... | collective-permute-start | bytes 983048 | tf_op jit(solution)/shard_map/ppermute | solution.py:329
  179.8 9.1 %collective-permute-start.59 = (bf16[4,32,1024]{2,1,0:T(8,128)(2,1)S(1)}, bf16[4,32,1024]{2,1,0:T(8,128)(2,1)S(1)}, u32[]{:S(2)}, u32[]{:S(2)}) collective-permute-start(bf16[4,32,1024]{2,1,0:T(8,128)(2,1)S(1)} %get-tuple-element.581), channel_id=1, source_target_pairs={{0,2},{1,3},{2,0},{3,1},{4,6},{5,7},{6,4},{7,5},{8,10},{9,11},{10,... | collective-permute-start | bytes 786440 | tf_op jit(solution)/shard_map/ppermute | solution.py:44
  189.0 11.3 %collective-permute-start.61 = (bf16[5,32,1024]{2,1,0:T(8,128)(2,1)S(1)}, bf16[5,32,1024]{2,1,0:T(8,128)(2,1)S(1)}, u32[]{:S(2)}, u32[]{:S(2)}) collective-permute-start(bf16[5,32,1024]{2,1,0:T(8,128)(2,1)S(1)} %add_convert_fusion.9), channel_id=1, source_target_pairs={{0,4},{8,0},{16,8},{24,16},{28,24},{20,28},{12,20},{4,12},{1,5},{9... | collective-permute-start | bytes 983048 | tf_op jit(solution)/shard_map/ppermute | solution.py:329
  189.7 10.6 %collective-permute-start.60 = (bf16[5,32,1024]{2,1,0:T(8,128)(2,1)S(1)}, bf16[5,32,1024]{2,1,0:T(8,128)(2,1)S(1)}, u32[]{:S(2)}, u32[]{:S(2)}) collective-permute-start(bf16[5,32,1024]{2,1,0:T(8,128)(2,1)S(1)} %add_convert_fusion.10), channel_id=1, source_target_pairs={{0,8},{8,16},{16,24},{24,28},{28,20},{20,12},{12,4},{4,0},{1,9},{9... | collective-permute-start | bytes 983048 | tf_op jit(solution)/shard_map/ppermute | solution.py:329
  191.2 6.6 %collective-permute-start.63 = (bf16[288,256]{1,0:T(8,128)(2,1)S(1)}, bf16[288,256]{1,0:T(8,128)(2,1)S(1)}, u32[]{:S(2)}, u32[]{:S(2)}) collective-permute-start(bf16[288,256]{1,0:T(8,128)(2,1)S(1)} %get-tuple-element.601), channel_id=1, source_target_pairs={{0,2},{1,3},{2,0},{3,1},{4,6},{5,7},{6,4},{7,5},{8,10},{9,11},{10,... | collective-permute-start | bytes 442376 | tf_op jit(solution)/shard_map/ppermute | solution.py:44
  192.2 8.1 %collective-permute-start.64 = (bf16[288,256]{1,0:T(8,128)(2,1)S(1)}, bf16[288,256]{1,0:T(8,128)(2,1)S(1)}, u32[]{:S(2)}, u32[]{:S(2)}) collective-permute-start(bf16[288,256]{1,0:T(8,128)(2,1)S(1)} %get-tuple-element.602), channel_id=1, source_target_pairs={{0,3},{1,2},{2,1},{3,0},{4,7},{5,6},{6,5},{7,4},{8,11},{9,10},{10,... | collective-permute-start | bytes 442376 | tf_op jit(solution)/shard_map/ppermute | solution.py:44
  200.3 9.8 %collective-permute-start.65 = (bf16[5,32,1024]{2,1,0:T(8,128)(2,1)S(1)}, bf16[5,32,1024]{2,1,0:T(8,128)(2,1)S(1)}, u32[]{:S(2)}, u32[]{:S(2)}) collective-permute-start(bf16[5,32,1024]{2,1,0:T(8,128)(2,1)S(1)} %get-tuple-element.606), channel_id=1, source_target_pairs={{0,8},{8,16},{16,24},{24,28},{28,20},{20,12},{12,4},{4,0},{1,9},{9... | collective-permute-start | bytes 983048 | tf_op jit(solution)/shard_map/ppermute | solution.py:329
  201.3 9.5 %collective-permute-start.66 = (bf16[5,32,1024]{2,1,0:T(8,128)(2,1)S(1)}, bf16[5,32,1024]{2,1,0:T(8,128)(2,1)S(1)}, u32[]{:S(2)}, u32[]{:S(2)}) collective-permute-start(bf16[5,32,1024]{2,1,0:T(8,128)(2,1)S(1)} %get-tuple-element.607), channel_id=1, source_target_pairs={{0,4},{8,0},{16,8},{24,16},{28,24},{20,28},{12,20},{4,12},{1,5},{9... | collective-permute-start | bytes 983048 | tf_op jit(solution)/shard_map/ppermute | solution.py:329
  211.9 9.3 %collective-permute-start.67 = (bf16[5,32,1024]{2,1,0:T(8,128)(2,1)S(1)}, bf16[5,32,1024]{2,1,0:T(8,128)(2,1)S(1)}, u32[]{:S(2)}, u32[]{:S(2)}) collective-permute-start(bf16[5,32,1024]{2,1,0:T(8,128)(2,1)S(1)} %add_convert_fusion.8), channel_id=1, source_target_pairs={{0,8},{8,16},{16,24},{24,28},{28,20},{20,12},{12,4},{4,0},{1,9},{9... | collective-permute-start | bytes 983048 | tf_op jit(solution)/shard_map/ppermute | solution.py:329
  212.2 9.1 %collective-permute-start.68 = (bf16[5,32,1024]{2,1,0:T(8,128)(2,1)S(1)}, bf16[5,32,1024]{2,1,0:T(8,128)(2,1)S(1)}, u32[]{:S(2)}, u32[]{:S(2)}) collective-permute-start(bf16[5,32,1024]{2,1,0:T(8,128)(2,1)S(1)} %add_convert_fusion.7), channel_id=1, source_target_pairs={{0,4},{8,0},{16,8},{24,16},{28,24},{20,28},{12,20},{4,12},{1,5},{9... | collective-permute-start | bytes 983048 | tf_op jit(solution)/shard_map/ppermute | solution.py:329
  214.2 6.2 %collective-permute-start.72 = (bf16[72,1024]{1,0:T(8,128)(2,1)S(1)}, bf16[72,1024]{1,0:T(8,128)(2,1)S(1)}, u32[]{:S(2)}, u32[]{:S(2)}) collective-permute-start(bf16[72,1024]{1,0:T(8,128)(2,1)S(1)} %get-tuple-element.634), channel_id=1, source_target_pairs={{0,3},{1,2},{2,1},{3,0},{4,7},{5,6},{6,5},{7,4},{8,11},{9,10},{10,... | collective-permute-start | bytes 442376 | tf_op jit(solution)/shard_map/ppermute | solution.py:44
  221.3 8.8 %collective-permute-start.73 = (bf16[5,32,1024]{2,1,0:T(8,128)(2,1)S(1)}, bf16[5,32,1024]{2,1,0:T(8,128)(2,1)S(1)}, u32[]{:S(2)}, u32[]{:S(2)}) collective-permute-start(bf16[5,32,1024]{2,1,0:T(8,128)(2,1)S(1)} %add_convert_fusion.6), channel_id=1, source_target_pairs={{0,8},{8,16},{16,24},{24,28},{28,20},{20,12},{12,4},{4,0},{1,9},{9... | collective-permute-start | bytes 983048 | tf_op jit(solution)/shard_map/ppermute | solution.py:329
  221.6 8.5 %collective-permute-start.74 = (bf16[5,32,1024]{2,1,0:T(8,128)(2,1)S(1)}, bf16[5,32,1024]{2,1,0:T(8,128)(2,1)S(1)}, u32[]{:S(2)}, u32[]{:S(2)}) collective-permute-start(bf16[5,32,1024]{2,1,0:T(8,128)(2,1)S(1)} %add_convert_fusion.5), channel_id=1, source_target_pairs={{0,4},{8,0},{16,8},{24,16},{28,24},{20,28},{12,20},{4,12},{1,5},{9... | collective-permute-start | bytes 983048 | tf_op jit(solution)/shard_map/ppermute | solution.py:329
  223.3 8.2 %collective-permute-start.75 = (bf16[4,40,1024]{2,1,0:T(8,128)(2,1)S(1)}, bf16[4,40,1024]{2,1,0:T(8,128)(2,1)S(1)}, u32[]{:S(2)}, u32[]{:S(2)}) collective-permute-start(bf16[4,40,1024]{2,1,0:T(8,128)(2,1)S(1)} %get-tuple-element.639), channel_id=1, source_target_pairs={{0,2},{1,3},{2,0},{3,1},{4,6},{5,7},{6,4},{7,5},{8,10},{9,11},{10,... | collective-permute-start | bytes 983048 | tf_op jit(solution)/shard_map/ppermute | solution.py:44
  231.7 7.1 %collective-permute-start.81 = (bf16[40,1024]{1,0:T(8,128)(2,1)S(1)}, bf16[40,1024]{1,0:T(8,128)(2,1)S(1)}, u32[]{:S(2)}, u32[]{:S(2)}) collective-permute-start(bf16[40,1024]{1,0:T(8,128)(2,1)S(1)} %get-tuple-element.718), channel_id=1, source_target_pairs={{0,16},{8,24},{16,28},{24,20},{28,12},{20,4},{12,0},{4,8},{1,17},{... | collective-permute-start | bytes 245768 | tf_op jit(solution)/shard_map/ppermute | solution.py:329
  232.1 11.2 %collective-permute-start.76 = (bf16[5,32,1024]{2,1,0:T(8,128)(2,1)S(1)}, bf16[5,32,1024]{2,1,0:T(8,128)(2,1)S(1)}, u32[]{:S(2)}, u32[]{:S(2)}) collective-permute-start(bf16[5,32,1024]{2,1,0:T(8,128)(2,1)S(1)} %add_convert_fusion.4), channel_id=1, source_target_pairs={{0,8},{8,16},{16,24},{24,28},{28,20},{20,12},{12,4},{4,0},{1,9},{9... | collective-permute-start | bytes 983048 | tf_op jit(solution)/shard_map/ppermute | solution.py:329
  233.7 9.5 %collective-permute-start.77 = (bf16[5,32,1024]{2,1,0:T(8,128)(2,1)S(1)}, bf16[5,32,1024]{2,1,0:T(8,128)(2,1)S(1)}, u32[]{:S(2)}, u32[]{:S(2)}) collective-permute-start(bf16[5,32,1024]{2,1,0:T(8,128)(2,1)S(1)} %add_convert_fusion.2), channel_id=1, source_target_pairs={{0,4},{8,0},{16,8},{24,16},{28,24},{20,28},{12,20},{4,12},{1,5},{9... | collective-permute-start | bytes 983048 | tf_op jit(solution)/shard_map/ppermute | solution.py:329
  234.3 9.0 %collective-permute-start.78 = (bf16[4,40,1024]{2,1,0:T(8,128)(2,1)S(1)}, bf16[4,40,1024]{2,1,0:T(8,128)(2,1)S(1)}, u32[]{:S(2)}, u32[]{:S(2)}) collective-permute-start(bf16[4,40,1024]{2,1,0:T(8,128)(2,1)S(1)} %get-tuple-element.648), channel_id=1, source_target_pairs={{0,2},{1,3},{2,0},{3,1},{4,6},{5,7},{6,4},{7,5},{8,10},{9,11},{10,... | collective-permute-start | bytes 983048 | tf_op jit(solution)/shard_map/ppermute | solution.py:44
  235.8 6.0 %collective-permute-start.80 = (bf16[40,1024]{1,0:T(8,128)(2,1)S(1)}, bf16[40,1024]{1,0:T(8,128)(2,1)S(1)}, u32[]{:S(2)}, u32[]{:S(2)}) collective-permute-start(bf16[40,1024]{1,0:T(8,128)(2,1)S(1)} %get-tuple-element.719), channel_id=1, source_target_pairs={{0,4},{8,0},{16,8},{24,16},{28,24},{20,28},{12,20},{4,12},{1,5},{9... | collective-permute-start | bytes 245768 | tf_op jit(solution)/shard_map/ppermute | solution.py:329
  243.4 6.9 %collective-permute-start.85 = (bf16[40,1024]{1,0:T(8,128)(2,1)S(1)}, bf16[40,1024]{1,0:T(8,128)(2,1)}, u32[]{:S(2)}, u32[]{:S(2)}) collective-permute-start(bf16[40,1024]{1,0:T(8,128)(2,1)S(1)} %fusion.18), channel_id=1, source_target_pairs={{0,4},{8,0},{16,8},{24,16},{28,24},{20,28},{12,20},{4,12},{1,5},{9... | collective-permute-start | bytes 245768 | tf_op jit(solution)/shard_map/ppermute | solution.py:329
  246.9 8.9 %collective-permute-start.83 = (bf16[5,32,1024]{2,1,0:T(8,128)(2,1)}, bf16[5,32,1024]{2,1,0:T(8,128)(2,1)S(1)}, u32[]{:S(2)}, u32[]{:S(2)}) collective-permute-start(bf16[5,32,1024]{2,1,0:T(8,128)(2,1)} %add_convert_fusion.1), channel_id=1, source_target_pairs={{0,4},{8,0},{16,8},{24,16},{28,24},{20,28},{12,20},{4,12},{1,5},{9... | collective-permute-start | bytes 983048 | tf_op jit(solution)/shard_map/ppermute | solution.py:329
  247.5 8.3 %collective-permute-start.82 = (bf16[5,32,1024]{2,1,0:T(8,128)(2,1)S(1)}, bf16[5,32,1024]{2,1,0:T(8,128)(2,1)}, u32[]{:S(2)}, u32[]{:S(2)}) collective-permute-start(bf16[5,32,1024]{2,1,0:T(8,128)(2,1)S(1)} %add_convert_fusion.3), channel_id=1, source_target_pairs={{0,8},{8,16},{16,24},{24,28},{28,20},{20,12},{12,4},{4,0},{1,9},{9... | collective-permute-start | bytes 983048 | tf_op jit(solution)/shard_map/ppermute | solution.py:329
  249.0 6.8 %collective-permute-start.84 = (bf16[40,1024]{1,0:T(8,128)(2,1)S(1)}, bf16[40,1024]{1,0:T(8,128)(2,1)}, u32[]{:S(2)}, u32[]{:S(2)}) collective-permute-start(bf16[40,1024]{1,0:T(8,128)(2,1)S(1)} %fusion.20), channel_id=1, source_target_pairs={{0,8},{8,16},{16,24},{24,28},{28,20},{20,12},{12,4},{4,0},{1,9},{9... | collective-permute-start | bytes 245768 | tf_op jit(solution)/shard_map/ppermute | solution.py:329
  (31 other events, 201.7 us)

commit v2 on v1

--- a/solution.py
+++ b/solution.py
@@ -568,6 +568,27 @@
     bias[...] = total[rows : rows + 8]
 
 
+def conv_end(one, one_a, one_b, two, two_a, two_b, conv, last):
+    taps = one.shape[0]
+    conv[:taps] = one[...].astype(F32) + one_a[...].astype(F32) + one_b[...].astype(F32)
+    total = two[...].astype(F32) + two_a[...].astype(F32) + two_b[...].astype(F32)
+    conv[taps:] = total[:-1]
+    last[...] = total[-1]
+
+
+def first_end(where, term, a, b, grad, norm):
+    total = term[...].astype(F32) + a[...].astype(F32) + b[...].astype(F32)
+    rows, width = grad.shape
+    for g in range(RING):
+        for r in range(4):
+            to, at = (g * 4 + r) * rows, (r * RING + g) * rows
+            grad[:, to : to + rows] = total[:rows, at : at + rows]
+    block = total[rows:]
+    swapped, plain = [pltpu.roll(block, lax.rem(width - where[i], width), 1)[:, :rows] for i in (18, 19)]
+    line = lax.broadcasted_iota(jnp.int32, swapped.shape, 0)
+    norm[...] = jnp.where(line < 2, swapped, plain)
+
+
 def spread(pairs, grad, dims):
     slots, rows, cols = dims
     count, width = grad.shape
@@ -758,12 +779,13 @@
     outs = read_weight.shape[1]
     taps = 9
     DMA = pltpu.SemaphoreType.DMA
-    index = jnp.arange(18, dtype=jnp.int32)
+    index = jnp.arange(20, dtype=jnp.int32)
     place_of = lambda d: jnp.where(d % 2 == 0, d // 2, RING - 1 - d // 2)
     place = (place_of(dp) + index - 2) % RING
     ahead = jnp.where(place < RING // 2, 2 * place, 2 * (RING - 1 - place) + 1)
     steps = (place_of(index - 10) - place_of(dp)) % RING
     where = jnp.where(index == 0, row, jnp.where(index == 1, live_count[0], jnp.where(index < 10, ahead, steps)))
+    where = jnp.where(index == 18, (row * RING + dp) * own, jnp.where(index == 19, (dp * 4 + row) * own, where))
     where = where.astype(jnp.int32)
 
     first_mine = first_weight.reshape(own, RING, 4, own).transpose(0, 2, 1, 3).reshape(own, width)
@@ -799,8 +821,8 @@
     ring = gather_step(gather_state(jnp.concatenate([last_weight, first_mine], axis=0)), 1)
     read = read_weight.T
     cots = cotangent.reshape(count, -1)
-    places = ((row * RING + dp) * own, (dp * 4 + row) * own, dp * outs)
-    more, ring, where, read, cots, x, places = fence(more, ring, where, read, cots, x, places)
+    bias_place = dp * outs
+    more, ring, where, read, cots, x, bias_place = fence(more, ring, where, read, cots, x, bias_place)
     ring = gather_step(ring, 2)
     cots = kernel(split_columns, [quarter] * 4, [SM, VM], [], 0, 2 * count * 4 * width * 2, where, cots)
     ring, cots = fence(ring, cots)
@@ -1113,21 +1135,39 @@
         where,
         *shown,
     ).reshape(slots, band // 2, cols // 2, 4 * width)
-    one_sum = scatter_end(one, one_a, one_b_end)
-    two_a, two_b, first_a, first_b, first_low, readout_out, one_sum = fence(
-        two_a, two_b, first_a, first_b, first_low, readout_out, one_sum
+    two_a, two_b, first_a, first_b, first_low, readout_out = fence(
+        two_a, two_b, first_a, first_b, first_low, readout_out
     )
     first_a, first_b = hop(add_to(first_low, 2, first_a), True), hop(add_to(first_low, 0, first_b), False)
-    bias_grad = lax.dynamic_slice(bias_rows, (0, places[2]), (1, outs), allow_negative_indices=False)[0]
-    two_sum = scatter_end(two, two_a, two_b)
-    conv_grad = jnp.concatenate([one_sum, two_sum[:4]], axis=0)
+    bias_grad = lax.dynamic_slice(bias_rows, (0, bias_place), (1, outs), allow_negative_indices=False)[0]
+    conv_grad, last_grad = kernel(
+        conv_end,
+        [shape((taps, own, width), F32), shape((own, width), F32)],
+        [VM] * 6,
+        [],
+        0,
+        10 * (taps + 1) * own * width,
+        one[0],
+        one_a,
+        one_b_end,
+        two[0],
+        two_a,
+        two_b,
+    )
     conv_grad = conv_grad.reshape(3, 3, own, width)
-    tail = first_low[1].astype(F32) + first_a.astype(F32) + first_b.astype(F32)
-    first_grad = tail[:own].reshape(own, 4, RING, own).transpose(0, 2, 1, 3).reshape(own, width)
-    last_grad = two_sum[4]
-    swapped = lax.dynamic_slice(tail, (own, places[0]), (2, own), allow_negative_indices=False)
-    plain = lax.dynamic_slice(tail, (own + 2, places[1]), (4, own), allow_negative_indices=False)
-    norm_grad = jnp.concatenate([swapped, plain], axis=0)
+    first_grad, norm_grad = kernel(
+        first_end,
+        [shape((own, width), F32), shape((8, own), F32)],
+        [SM] + [VM] * 3,
+        [],
+        0,
+        10 * own * width,
+        where,
+        first_low[1],
+        first_a,
+        first_b,
+    )
+    norm_grad = norm_grad[:6]
     return (
         readout_out,
         image_grad,

time: 269 us -> 265 us (0.985)
  waiting for transfers between devices: 121 us -> 117 us
    ppermute x53, waiting for transfers between devices: 81.4 us -> 77.1 us  [hop(): lax.ppermute(x, 'dp', [(order[i], order[(i + step) % RING]) for i in rang...]
    pallas_call x18 -> x20, Pallas kernels: 55.2 us -> 57.6 us  [kernel(): pl.pallas_call(body, out_shape=outs, in_specs=ins, out_specs=jax.tree.map...]
  transfers between devices with their start and end apart: 88 -> 88, of which waited for: 49 -> 47; matrix products, arithmetic and copies ran while one was open for 4% -> 5% of each run, Pallas kernels for 18% -> 19%
where the time goes in v2:
time: 265 us; the launch traced here: 264 us
  waiting for transfers between devices  117 us (44%)
  starting transfers between devices  73.5 us (28%)
  Pallas kernels  57.6 us (22%)
  local copies, waits for them, and re-layouts  9.23 us (3%)
  other arithmetic  5.45 us (2%)
    ppermute x53, waiting for transfers between devices, hop(): lax.ppermute(x, 'dp', [(order[i], order[(i + step) % RING]) for i in rang...  77.1 us
    pallas_call x20, Pallas kernels, kernel(): pl.pallas_call(body, out_shape=outs, in_specs=ins, out_specs=jax.tree.map...  57.6 us
    ppermute x53, starting transfers between devices, hop(): lax.ppermute(x, 'dp', [(order[i], order[(i + step) % RING]) for i in rang...  55.1 us
    ppermute x35, waiting for transfers between devices, swap_row(): return lax.ppermute(x, 'row', [(i, i ^ q) for i in range(4)])  39.6 us
    ppermute x35, starting transfers between devices, swap_row(): return lax.ppermute(x, 'row', [(i, i ^ q) for i in range(4)])  18.4 us
  transfers between devices with their start and end apart: 88, of which 47 were waited for; matrix products, arithmetic and copies ran while one was open for 5% of the time, Pallas kernels for 19%

profile of v2, /device:TPU:0, one launch (start us, length us, event | category | flops | bytes accessed | tf_op | source)
XLA Modules:
  0.0 264.4 jit_solution(6530479431088129866)
XLA Ops:
  0.7 3.1 %collective-permute-start.1 = (bf16[9,32,1024]{2,1,0:T(8,128)(2,1)}, bf16[9,32,1024]{2,1,0:T(8,128)(2,1)S(1)}, u32[]{:S(2)}, u32[]{:S(2)}) collective-permute-start(bf16[9,32,1024]{2,1,0:T(8,128)(2,1)} %bitcast.105), channel_id=1, source_target_pairs={{0,8},{8,16},{16,24},{24,28},{28,20},{20,12},{12,4},{4,0},{1,9},{9... | collective-permute-start | bytes 1769480 | tf_op jit(solution)/shard_map/ppermute | solution.py:329
  6.2 2.1 collective-permute-start.3
  11.6 8.8 %collective-permute-done.3.refs_7_ = bf16[72,1024]{1,0:T(8,128)(2,1)S(1)} collective-permute-done((bf16[72,1024]{1,0:T(8,128)(2,1)S(1)}, bf16[72,1024]{1,0:T(8,128)(2,1)S(1)}, u32[]{:S(2)}, u32[]{:S(2)}) %collective-permute-start.3) | collective-permute-done | bytes 147488 | tf_op jit(solution)/shard_map/ppermute | solution.py:329
  20.4 1.5 collective-permute-done.2.refs_1_
  22.2 1.7 collective-permute-start.5
  24.7 2.4 collective-permute-done.4.refs_2_
  27.4 1.7 collective-permute-start.6
  29.4 3.1 %collective-permute-done.6.refs_3_ = bf16[72,1024]{1,0:T(8,128)(2,1)S(1)} collective-permute-done((bf16[72,1024]{1,0:T(8,128)(2,1)S(1)}, bf16[72,1024]{1,0:T(8,128)(2,1)S(1)}, u32[]{:S(2)}, u32[]{:S(2)}) %collective-permute-start.6) | collective-permute-done | bytes 147488 | tf_op jit(solution)/shard_map/ppermute | solution.py:329
  32.5 1.7 collective-permute-done.7.refs_5_
  34.2 1.6 collective-permute-start.9
  36.2 3.8 %collective-permute-done.8.refs_4_ = bf16[32,1024]{1,0:T(8,128)(2,1)S(1)} collective-permute-done((bf16[32,1024]{1,0:T(8,128)(2,1)S(1)}, bf16[32,1024]{1,0:T(8,128)(2,1)S(1)}, u32[]{:S(2)}, u32[]{:S(2)}) %collective-permute-start.8) | collective-permute-done | bytes 65568 | tf_op jit(solution)/shard_map/ppermute | solution.py:329
  40.7 1.6 collective-permute-start.12
  42.3 1.8 collective-permute-start.10
  44.3 13.4 %collective-permute-done.10.refs_2_ = bf16[9,32,1024]{2,1,0:T(8,128)(2,1)S(1)} collective-permute-done((bf16[9,32,1024]{2,1,0:T(8,128)(2,1)S(1)}, bf16[9,32,1024]{2,1,0:T(8,128)(2,1)S(1)}, u32[]{:S(2)}, u32[]{:S(2)}) %collective-permute-start.10) | collective-permute-done | bytes 589856 | tf_op jit(solution)/shard_map/ppermute | solution.py:329
  57.7 1.8 collective-permute-done.11.refs_6_
  59.6 1.8 collective-permute-start.14
  62.2 2.0 shard_map.154
  64.3 11.7 %collective-permute-done.17.l2 = bf16[8,32,1024]{2,1,0:T(8,128)(2,1)S(1)} collective-permute-done((bf16[8,32,1024]{2,1,0:T(8,128)(2,1)S(1)}, bf16[8,32,1024]{2,1,0:T(8,128)(2,1)S(1)}, u32[]{:S(2)}, u32[]{:S(2)}) %collective-permute-start.17) | collective-permute-done | bytes 524320 | tf_op jit(solution)/shard_map/ppermute | solution.py:44
  77.4 1.7 collective-permute-start.20
  80.5 5.4 %collective-permute-done.22.s2 = bf16[288,256]{1,0:T(8,128)(2,1)S(1)} collective-permute-done((bf16[288,256]{1,0:T(8,128)(2,1)S(1)}, bf16[288,256]{1,0:T(8,128)(2,1)S(1)}, u32[]{:S(2)}, u32[]{:S(2)}) %collective-permute-start.22) | collective-permute-done | bytes 147488 | tf_op jit(solution)/shard_map/ppermute | solution.py:44
  87.4 1.8 collective-permute-start.25
  91.1 5.9 %shard_map.155 = (f32[288,1024]{1,0:T(8,128)S(1)}, bf16[288,1024]{1,0:T(8,128)(2,1)S(1)}, bf16[576,2304]{1,0:T(8,128)(2,1)S(1)}, bf16[9,8,32,1024]{3,2,1,0:T(8,128)(2,1)S(1)}) custom-call(s32[20]{0:T(128)S(1)} %compare_select_fusion.12.where, bf16[288,256]{1,0:T(8,128)(2,1)S(1)} %get-tuple-element.461.s0, bf16[288,256]{1,0:T(8,128)(2,1)S(1)} %collective-permute-done.21.s1, ...), custom_call_target="tpu_custom_call" | custom-call | flops 42467328 | bytes 364032 | tf_op jit(solution)/shard_map/pallas_call | solution.py:297
  98.5 1.6 collective-permute-done.30
  102.9 5.4 %shard_map.156 = (f32[288,1024]{1,0:T(8,128)S(1)}, bf16[288,1024]{1,0:T(8,128)(2,1)S(1)}, bf16[576,2304]{1,0:T(8,128)(2,1)S(1)}) custom-call(s32[20]{0:T(128)S(1)} %compare_select_fusion.12.where, bf16[288,256]{1,0:T(8,128)(2,1)S(1)} %get-tuple-element.461.s0, bf16[288,256]{1,0:T(8,128)(2,1)S(1)} %collective-permute-done.21.s1, ...), custom_call_target="tpu_custom_call" | custom-call | flops 42467328 | bytes 364032 | tf_op jit(solution)/shard_map/pallas_call | solution.py:297
  110.1 1.5 collective-permute-start.36
  111.7 6.7 %collective-permute-done.35.refs_3_ = bf16[128,1024]{1,0:T(8,128)(2,1)S(1)} collective-permute-done((bf16[128,1024]{1,0:T(8,128)(2,1)S(1)}, bf16[128,1024]{1,0:T(8,128)(2,1)S(1)}, u32[]{:S(2)}, u32[]{:S(2)}) %collective-permute-start.35) | collective-permute-done | bytes 262176 | tf_op jit(solution)/shard_map/ppermute | solution.py:329
  118.6 2.3 shard_map.157
  123.2 1.5 collective-permute-start.39
  124.7 3.5 %collective-permute-done.40.refs_8_ = bf16[64,1024]{1,0:T(8,128)(2,1)S(1)} collective-permute-done((bf16[64,1024]{1,0:T(8,128)(2,1)S(1)}, bf16[64,1024]{1,0:T(8,128)(2,1)S(1)}, u32[]{:S(2)}, u32[]{:S(2)}) %collective-permute-start.40) | collective-permute-done | bytes 131104 | tf_op jit(solution)/shard_map/ppermute | solution.py:329
  129.9 3.1 %shard_map.158 = (bf16[72,1024]{1,0:T(8,128)(2,1)S(1)}, bf16[72,1024]{1,0:T(8,128)(2,1)S(1)}, bf16[72,1024]{1,0:T(8,128)(2,1)S(1)}, bf16[72,1024]{1,0:T(8,128)(2...) custom-call(s32[20]{0:T(128)S(1)} %compare_select_fusion.12.where, ...), custom_call_target="tpu_custom_call" | custom-call | flops 18874368 | bytes 88064 | tf_op jit(solution)/shard_map/pallas_call | solution.py:297
  133.2 1.4 collective-permute-done.42
  135.5 2.2 shard_map.159
  137.7 3.0 %collective-permute-done.43.cross = bf16[72,1024]{1,0:T(8,128)(2,1)S(1)} collective-permute-done((bf16[72,1024]{1,0:T(8,128)(2,1)S(1)}, bf16[72,1024]{1,0:T(8,128)(2,1)S(1)}, u32[]{:S(2)}, u32[]{:S(2)}) %collective-permute-start.43) | collective-permute-done | bytes 147488 | tf_op jit(solution)/shard_map/ppermute | solution.py:44
  140.7 1.5 collective-permute-start.44
  142.7 2.6 shard_map.160
  145.8 1.5 collective-permute-done.45
  150.2 4.3 %collective-permute-done.48 = bf16[144,1024]{1,0:T(8,128)(2,1)S(1)} collective-permute-done((bf16[144,1024]{1,0:T(8,128)(2,1)S(1)}, bf16[144,1024]{1,0:T(8,128)(2,1)S(1)}, u32[]{:S(2)}, u32[]{:S(2)}) %collective-permute-start.48) | collective-permute-done | bytes 294944 | tf_op jit(solution)/shard_map/ppermute | solution.py:329
  157.8 2.1 shard_map.161
  159.9 6.0 %shard_map.162.half = f32[9,256,1024]{2,1,0:T(8,128)S(1)} custom-call(s32[20]{0:T(128)S(1)} %compare_select_fusion.12.where, bf16[576,2304]{1,0:T(8,128)(2,1)S(1)} %get-tuple-element.545.here, bf16[288,1024]{1,0:T(8,128)(2,1)S(1)} %get-tuple-element.574.g0, bf16[288,1024]{1,0:T(8,128)(2,1)S(1)} %collective-permute-done.47.g1), custom_call_target="tpu_custom_call" | custom-call | flops 42467328 | bytes 589824 | tf_op jit(solution)/shard_map/pallas_call | solution.py:297
  170.6 3.8 %shard_map.163 = (bf16[5,32,1024]{2,1,0:T(8,128)(2,1)S(1)}, bf16[5,32,1024]{2,1,0:T(8,128)(2,1)S(1)}, bf16[5,32,1024]{2,1,0:T(8,128)(2,1)S(1)}, bf16[5,32,1024]{...) custom-call(s32[20]{0:T(128)S(1)} %compare_select_fusion.12.where, ...), custom_call_target="tpu_custom_call" | custom-call | flops 47185920 | bytes 327680 | tf_op jit(solution)/shard_map/pallas_call | solution.py:297
  176.5 1.4 collective-permute-done.54.refs_2_
  181.0 7.9 %shard_map.164 = (bf16[288,256]{1,0:T(8,128)(2,1)S(1)}, bf16[288,256]{1,0:T(8,128)(2,1)S(1)}, bf16[288,256]{1,0:T(8,128)(2,1)S(1)}, bf16[288,256]{1,0:T(8,128)(2,1)S(1)}) custom-call(s32[20]{0:T(128)S(1)} %compare_select_fusion.12.where, bf16[288,1024]{1,0:T(8,128)(2,1)S(1)} %get-tuple-element.574.g0, bf16[288,1024]{1,0:T(8,128)(2,1)S(1)} %collective-permute-done.47.g1, ...), custom_call_target="tpu_custom_call" | custom-call | flops 84934656 | bytes 350208 | tf_op jit(solution)/shard_map/pallas_call | solution.py:297
  189.7 1.6 collective-permute-start.60
  193.1 3.3 %shard_map.165 = (bf16[5,32,1024]{2,1,0:T(8,128)(2,1)S(1)}, bf16[5,32,1024]{2,1,0:T(8,128)(2,1)S(1)}, bf16[5,32,1024]{2,1,0:T(8,128)(2,1)S(1)}, bf16[5,32,1024]{...) custom-call(s32[20]{0:T(128)S(1)} %compare_select_fusion.12.where, ...), custom_call_target="tpu_custom_call" | custom-call | flops 37748736 | bytes 262144 | tf_op jit(solution)/shard_map/pallas_call | solution.py:297
  196.5 1.4 collective-permute-done.63.b2
  197.9 2.4 collective-permute-done.64.b3
  202.4 3.2 %shard_map.166 = (bf16[288,1024]{1,0:T(8,128)(2,1)S(1)}, f32[8,40,1024]{2,1,0:T(8,128)S(1)}, bf16[2,8,40,1024]{3,2,1,0:T(8,128)(2,1)S(1)}, f32[8,40,1024]{2,1,0:T(8,128)S(1)}) custom-call(s32[20]{0:T(128)S(1)} %compare_select_fusion.12.where, bf16[288,256]{1,0:T(8,128)(2,1)S(1)} %get-tuple-element.609.b0, bf16[288,256]{1,0:T(8,128)(2,1)S(1)} %collective-permute-done.62.b1, ...), custom_call_target="tpu_custom_call" | custom-call | flops 9437184 | bytes 135168 | tf_op jit(solution)/shard_map/pallas_call | solution.py:297
  205.7 4.4 %collective-permute-done.65 = bf16[5,32,1024]{2,1,0:T(8,128)(2,1)S(1)} collective-permute-done((bf16[5,32,1024]{2,1,0:T(8,128)(2,1)S(1)}, bf16[5,32,1024]{2,1,0:T(8,128)(2,1)S(1)}, u32[]{:S(2)}, u32[]{:S(2)}) %collective-permute-start.65) | collective-permute-done | bytes 327712 | tf_op jit(solution)/shard_map/ppermute | solution.py:329
  212.3 1.7 collective-permute-start.68
  214.7 2.4 collective-permute-done.71.i2
  217.2 3.2 %collective-permute-done.72.i3 = bf16[72,1024]{1,0:T(8,128)(2,1)S(1)} collective-permute-done((bf16[72,1024]{1,0:T(8,128)(2,1)S(1)}, bf16[72,1024]{1,0:T(8,128)(2,1)S(1)}, u32[]{:S(2)}, u32[]{:S(2)}) %collective-permute-start.72) | collective-permute-done | bytes 147488 | tf_op jit(solution)/shard_map/ppermute | solution.py:44
  221.7 1.7 collective-permute-start.74
  223.4 1.5 collective-permute-start.75
  224.9 2.2 shard_map.167
  227.2 3.0 %collective-permute-done.73 = bf16[5,32,1024]{2,1,0:T(8,128)(2,1)S(1)} collective-permute-done((bf16[5,32,1024]{2,1,0:T(8,128)(2,1)S(1)}, bf16[5,32,1024]{2,1,0:T(8,128)(2,1)S(1)}, u32[]{:S(2)}, u32[]{:S(2)}) %collective-permute-start.73) | collective-permute-done | bytes 327712 | tf_op jit(solution)/shard_map/ppermute | solution.py:329
  232.0 1.6 collective-permute-start.76
  236.3 1.7 collective-permute-start.80
  238.9 2.8 %collective-permute-done.80 = bf16[40,1024]{1,0:T(8,128)(2,1)S(1)} collective-permute-done((bf16[40,1024]{1,0:T(8,128)(2,1)S(1)}, bf16[40,1024]{1,0:T(8,128)(2,1)S(1)}, u32[]{:S(2)}, u32[]{:S(2)}) %collective-permute-start.80) | collective-permute-done | bytes 81952 | tf_op jit(solution)/shard_map/ppermute | solution.py:329
  241.7 1.5 collective-permute-done.79
  244.0 2.6 collective-permute-start.85
  248.0 1.5 collective-permute-start.82
  252.4 3.8 %collective-permute-done.84 = bf16[40,1024]{1,0:T(8,128)(2,1)S(1)} collective-permute-done((bf16[40,1024]{1,0:T(8,128)(2,1)}, bf16[40,1024]{1,0:T(8,128)(2,1)S(1)}, u32[]{:S(2)}, u32[]{:S(2)}) %collective-permute-start.84) | collective-permute-done | bytes 81952 | tf_op jit(solution)/shard_map/ppermute | solution.py:329
  257.7 1.6 collective-permute-start.86
  259.2 2.6 copy.24
  (199 shorter events, 67.3 us)
Async XLA Ops:
  0.7 21.2 %collective-permute-start.1 = (bf16[9,32,1024]{2,1,0:T(8,128)(2,1)}, bf16[9,32,1024]{2,1,0:T(8,128)(2,1)S(1)}, u32[]{:S(2)}, u32[]{:S(2)}) collective-permute-start(bf16[9,32,1024]{2,1,0:T(8,128)(2,1)} %bitcast.105), channel_id=1, source_target_pairs={{0,8},{8,16},{16,24},{24,28},{28,20},{20,12},{12,4},{4,0},{1,9},{9... | collective-permute-start | bytes 1769480 | tf_op jit(solution)/shard_map/ppermute | solution.py:329
  3.8 18.2 %collective-permute-start = (bf16[9,32,1024]{2,1,0:T(8,128)(2,1)}, bf16[9,32,1024]{2,1,0:T(8,128)(2,1)S(1)}, u32[]{:S(2)}, u32[]{:S(2)}) collective-permute-start(bf16[9,32,1024]{2,1,0:T(8,128)(2,1)} %bitcast.106), channel_id=1, source_target_pairs={{0,4},{8,0},{16,8},{24,16},{28,24},{20,28},{12,20},{4,12},{1,5},{9... | collective-permute-start | bytes 1769480 | tf_op jit(solution)/shard_map/ppermute | solution.py:329
  6.2 14.2 %collective-permute-start.3 = (bf16[72,1024]{1,0:T(8,128)(2,1)S(1)}, bf16[72,1024]{1,0:T(8,128)(2,1)S(1)}, u32[]{:S(2)}, u32[]{:S(2)}) collective-permute-start(bf16[72,1024]{1,0:T(8,128)(2,1)S(1)} %concatenate.11.refs_0_), channel_id=1, source_target_pairs={{0,8},{8,16},{16,24},{24,28},{28,20},{20,12},{12,4},{4,0},{1,9},{9... | collective-permute-start | bytes 442376 | tf_op jit(solution)/shard_map/ppermute | solution.py:329
  8.2 13.7 %collective-permute-start.2 = (bf16[72,1024]{1,0:T(8,128)(2,1)S(1)}, bf16[72,1024]{1,0:T(8,128)(2,1)S(1)}, u32[]{:S(2)}, u32[]{:S(2)}) collective-permute-start(bf16[72,1024]{1,0:T(8,128)(2,1)S(1)} %concatenate.11.refs_0_), channel_id=1, source_target_pairs={{0,4},{8,0},{16,8},{24,16},{28,24},{20,28},{12,20},{4,12},{1,5},{9... | collective-permute-start | bytes 442376 | tf_op jit(solution)/shard_map/ppermute | solution.py:329
  34.2 5.9 %collective-permute-start.9 = (bf16[40,1024]{1,0:T(8,128)(2,1)S(1)}, bf16[40,1024]{1,0:T(8,128)(2,1)S(1)}, u32[]{:S(2)}, u32[]{:S(2)}) collective-permute-start(bf16[40,1024]{1,0:T(8,128)(2,1)S(1)} %slice.141), channel_id=1, source_target_pairs={{0,4},{8,0},{16,8},{24,16},{28,24},{20,28},{12,20},{4,12},{1,5},{9... | collective-permute-start | bytes 245768 | tf_op jit(solution)/shard_map/ppermute | solution.py:329
  40.7 18.9 %collective-permute-start.13 = (bf16[8,40,1024]{2,1,0:T(8,128)(2,1)S(1)}, bf16[8,40,1024]{2,1,0:T(8,128)(2,1)S(1)}, u32[]{:S(2)}, u32[]{:S(2)}) collective-permute-start(bf16[8,40,1024]{2,1,0:T(8,128)(2,1)S(1)} %get-tuple-element.405.f0), channel_id=1, source_target_pairs={{0,1},{1,0},{2,3},{3,2},{4,5},{5,4},{6,7},{7,6},{8,9},{9,8},{10,11... | collective-permute-start | bytes 1966088 | tf_op jit(solution)/shard_map/ppermute | solution.py:44
  40.7 18.8 %collective-permute-start.12 = (bf16[8,40,1024]{2,1,0:T(8,128)(2,1)S(1)}, bf16[8,40,1024]{2,1,0:T(8,128)(2,1)S(1)}, u32[]{:S(2)}, u32[]{:S(2)}) collective-permute-start(bf16[8,40,1024]{2,1,0:T(8,128)(2,1)S(1)} %get-tuple-element.405.f0), channel_id=1, source_target_pairs={{0,2},{1,3},{2,0},{3,1},{4,6},{5,7},{6,4},{7,5},{8,10},{9,11},{10,... | collective-permute-start | bytes 1966088 | tf_op jit(solution)/shard_map/ppermute | solution.py:44
  42.3 15.4 %collective-permute-start.10 = (bf16[9,32,1024]{2,1,0:T(8,128)(2,1)S(1)}, bf16[9,32,1024]{2,1,0:T(8,128)(2,1)S(1)}, u32[]{:S(2)}, u32[]{:S(2)}) collective-permute-start(bf16[9,32,1024]{2,1,0:T(8,128)(2,1)S(1)} %collective-permute-done.refs_1_), channel_id=1, source_target_pairs={{0,4},{8,0},{16,8},{24,16},{28,24},{20,28},{12,20},{4,12},{1,5},{9... | collective-permute-start | bytes 1769480 | tf_op jit(solution)/shard_map/ppermute | solution.py:329
  44.1 15.4 %collective-permute-start.11 = (bf16[9,32,1024]{2,1,0:T(8,128)(2,1)S(1)}, bf16[9,32,1024]{2,1,0:T(8,128)(2,1)S(1)}, u32[]{:S(2)}, u32[]{:S(2)}) collective-permute-start(bf16[9,32,1024]{2,1,0:T(8,128)(2,1)S(1)} %collective-permute-done.1.refs_7_), channel_id=1, source_target_pairs={{0,8},{8,16},{16,24},{24,28},{28,20},{20,12},{12,4},{4,0},{1,9},{9... | collective-permute-start | bytes 1769480 | tf_op jit(solution)/shard_map/ppermute | solution.py:329
  59.6 16.4 %collective-permute-start.14 = (bf16[9,32,1024]{2,1,0:T(8,128)(2,1)S(1)}, bf16[9,32,1024]{2,1,0:T(8,128)(2,1)S(1)}, u32[]{:S(2)}, u32[]{:S(2)}) collective-permute-start(bf16[9,32,1024]{2,1,0:T(8,128)(2,1)S(1)} %collective-permute-done.10.refs_2_), channel_id=1, source_target_pairs={{0,4},{8,0},{16,8},{24,16},{28,24},{20,28},{12,20},{4,12},{1,5},{9... | collective-permute-start | bytes 1769480 | tf_op jit(solution)/shard_map/ppermute | solution.py:329
  61.3 15.4 %collective-permute-start.15 = (bf16[9,32,1024]{2,1,0:T(8,128)(2,1)S(1)}, bf16[9,32,1024]{2,1,0:T(8,128)(2,1)S(1)}, u32[]{:S(2)}, u32[]{:S(2)}) collective-permute-start(bf16[9,32,1024]{2,1,0:T(8,128)(2,1)S(1)} %collective-permute-done.11.refs_6_), channel_id=1, source_target_pairs={{0,8},{8,16},{16,24},{24,28},{28,20},{20,12},{12,4},{4,0},{1,9},{9... | collective-permute-start | bytes 1769480 | tf_op jit(solution)/shard_map/ppermute | solution.py:329
  61.6 14.3 %collective-permute-start.17 = (bf16[8,32,1024]{2,1,0:T(8,128)(2,1)S(1)}, bf16[8,32,1024]{2,1,0:T(8,128)(2,1)S(1)}, u32[]{:S(2)}, u32[]{:S(2)}) collective-permute-start(bf16[8,32,1024]{2,1,0:T(8,128)(2,1)S(1)} %get-tuple-element.486.l0), channel_id=1, source_target_pairs={{0,2},{1,3},{2,0},{3,1},{4,6},{5,7},{6,4},{7,5},{8,10},{9,11},{10,... | collective-permute-start | bytes 1572872 | tf_op jit(solution)/shard_map/ppermute | solution.py:44
  76.8 10.4 %collective-permute-start.24 = (bf16[8,32,1024]{2,1,0:T(8,128)(2,1)S(1)}, bf16[8,32,1024]{2,1,0:T(8,128)(2,1)S(1)}, u32[]{:S(2)}, u32[]{:S(2)}) collective-permute-start(bf16[8,32,1024]{2,1,0:T(8,128)(2,1)S(1)} %collective-permute-done.17.l2), channel_id=1, source_target_pairs={{0,1},{1,0},{2,3},{3,2},{4,5},{5,4},{6,7},{7,6},{8,9},{9,8},{10,11... | collective-permute-start | bytes 1572872 | tf_op jit(solution)/shard_map/ppermute | solution.py:44
  76.8 10.3 %collective-permute-start.19 = (bf16[5,32,1024]{2,1,0:T(8,128)(2,1)S(1)}, bf16[5,32,1024]{2,1,0:T(8,128)(2,1)S(1)}, u32[]{:S(2)}, u32[]{:S(2)}) collective-permute-start(bf16[5,32,1024]{2,1,0:T(8,128)(2,1)S(1)} %slice.142), channel_id=1, source_target_pairs={{0,8},{8,16},{16,24},{24,28},{28,20},{20,12},{12,4},{4,0},{1,9},{9... | collective-permute-start | bytes 983048 | tf_op jit(solution)/shard_map/ppermute | solution.py:329
  77.4 9.7 %collective-permute-start.20 = (bf16[4,32,1024]{2,1,0:T(8,128)(2,1)S(1)}, bf16[4,32,1024]{2,1,0:T(8,128)(2,1)S(1)}, u32[]{:S(2)}, u32[]{:S(2)}) collective-permute-start(bf16[4,32,1024]{2,1,0:T(8,128)(2,1)S(1)} %slice.143), channel_id=1, source_target_pairs={{0,4},{8,0},{16,8},{24,16},{28,24},{20,28},{12,20},{4,12},{1,5},{9... | collective-permute-start | bytes 786440 | tf_op jit(solution)/shard_map/ppermute | solution.py:329
  79.2 6.7 %collective-permute-start.22 = (bf16[288,256]{1,0:T(8,128)(2,1)S(1)}, bf16[288,256]{1,0:T(8,128)(2,1)S(1)}, u32[]{:S(2)}, u32[]{:S(2)}) collective-permute-start(bf16[288,256]{1,0:T(8,128)(2,1)S(1)} %get-tuple-element.424), channel_id=1, source_target_pairs={{0,2},{1,3},{2,0},{3,1},{4,6},{5,7},{6,4},{7,5},{8,10},{9,11},{10,... | collective-permute-start | bytes 442376 | tf_op jit(solution)/shard_map/ppermute | solution.py:44
  79.7 7.4 %collective-permute-start.23 = (bf16[288,256]{1,0:T(8,128)(2,1)S(1)}, bf16[288,256]{1,0:T(8,128)(2,1)S(1)}, u32[]{:S(2)}, u32[]{:S(2)}) collective-permute-start(bf16[288,256]{1,0:T(8,128)(2,1)S(1)} %get-tuple-element.425), channel_id=1, source_target_pairs={{0,3},{1,2},{2,1},{3,0},{4,7},{5,6},{6,5},{7,4},{8,11},{9,10},{10,... | collective-permute-start | bytes 442376 | tf_op jit(solution)/shard_map/ppermute | solution.py:44
  87.1 10.9 %collective-permute-start.26 = (bf16[128,1024]{1,0:T(8,128)(2,1)S(1)}, bf16[128,1024]{1,0:T(8,128)(2,1)S(1)}, u32[]{:S(2)}, u32[]{:S(2)}) collective-permute-start(bf16[128,1024]{1,0:T(8,128)(2,1)S(1)} %bitcast.102), channel_id=1, source_target_pairs={{0,8},{8,16},{16,24},{24,28},{28,20},{20,12},{12,4},{4,0},{1,9},{9... | collective-permute-start | bytes 786440 | tf_op jit(solution)/shard_map/ppermute | solution.py:329
  87.4 10.6 %collective-permute-start.25 = (bf16[128,1024]{1,0:T(8,128)(2,1)S(1)}, bf16[128,1024]{1,0:T(8,128)(2,1)S(1)}, u32[]{:S(2)}, u32[]{:S(2)}) collective-permute-start(bf16[128,1024]{1,0:T(8,128)(2,1)S(1)} %bitcast.103), channel_id=1, source_target_pairs={{0,4},{8,0},{16,8},{24,16},{28,24},{20,28},{12,20},{4,12},{1,5},{9... | collective-permute-start | bytes 786440 | tf_op jit(solution)/shard_map/ppermute | solution.py:329
  89.2 7.7 %collective-permute-start.27 = (bf16[72,1024]{1,0:T(8,128)(2,1)S(1)}, bf16[72,1024]{1,0:T(8,128)(2,1)S(1)}, u32[]{:S(2)}, u32[]{:S(2)}) collective-permute-start(bf16[72,1024]{1,0:T(8,128)(2,1)S(1)} %get-tuple-element.451), channel_id=1, source_target_pairs={{0,1},{1,0},{2,3},{3,2},{4,5},{5,4},{6,7},{7,6},{8,9},{9,8},{10,11... | collective-permute-start | bytes 442376 | tf_op jit(solution)/shard_map/ppermute | solution.py:44
  89.4 7.5 %collective-permute-start.28 = (bf16[72,1024]{1,0:T(8,128)(2,1)S(1)}, bf16[72,1024]{1,0:T(8,128)(2,1)S(1)}, u32[]{:S(2)}, u32[]{:S(2)}) collective-permute-start(bf16[72,1024]{1,0:T(8,128)(2,1)S(1)} %get-tuple-element.452), channel_id=1, source_target_pairs={{0,2},{1,3},{2,0},{3,1},{4,6},{5,7},{6,4},{7,5},{8,10},{9,11},{10,... | collective-permute-start | bytes 442376 | tf_op jit(solution)/shard_map/ppermute | solution.py:44
  90.0 8.0 %collective-permute-start.29 = (bf16[72,1024]{1,0:T(8,128)(2,1)S(1)}, bf16[72,1024]{1,0:T(8,128)(2,1)S(1)}, u32[]{:S(2)}, u32[]{:S(2)}) collective-permute-start(bf16[72,1024]{1,0:T(8,128)(2,1)S(1)} %get-tuple-element.453), channel_id=1, source_target_pairs={{0,3},{1,2},{2,1},{3,0},{4,7},{5,6},{6,5},{7,4},{8,11},{9,10},{10,... | collective-permute-start | bytes 442376 | tf_op jit(solution)/shard_map/ppermute | solution.py:44
  100.3 8.6 %collective-permute-start.31 = (bf16[128,1024]{1,0:T(8,128)(2,1)S(1)}, bf16[128,1024]{1,0:T(8,128)(2,1)S(1)}, u32[]{:S(2)}, u32[]{:S(2)}) collective-permute-start(bf16[128,1024]{1,0:T(8,128)(2,1)S(1)} %collective-permute-done.25.refs_1_), channel_id=1, source_target_pairs={{0,4},{8,0},{16,8},{24,16},{28,24},{20,28},{12,20},{4,12},{1,5},{9... | collective-permute-start | bytes 786440 | tf_op jit(solution)/shard_map/ppermute | solution.py:329
  101.3 8.3 %collective-permute-start.32 = (bf16[128,1024]{1,0:T(8,128)(2,1)S(1)}, bf16[128,1024]{1,0:T(8,128)(2,1)S(1)}, u32[]{:S(2)}, u32[]{:S(2)}) collective-permute-start(bf16[128,1024]{1,0:T(8,128)(2,1)S(1)} %collective-permute-done.26.refs_7_), channel_id=1, source_target_pairs={{0,8},{8,16},{16,24},{24,28},{28,20},{20,12},{12,4},{4,0},{1,9},{9... | collective-permute-start | bytes 786440 | tf_op jit(solution)/shard_map/ppermute | solution.py:329
  102.4 16.2 %collective-permute-start.34 = (bf16[288,1024]{1,0:T(8,128)(2,1)S(1)}, bf16[288,1024]{1,0:T(8,128)(2,1)S(1)}, u32[]{:S(2)}, u32[]{:S(2)}) collective-permute-start(bf16[288,1024]{1,0:T(8,128)(2,1)S(1)} %add_convert_fusion), channel_id=1, source_target_pairs={{0,2},{1,3},{2,0},{3,1},{4,6},{5,7},{6,4},{7,5},{8,10},{9,11},{10,... | collective-permute-start | bytes 1769480 | tf_op jit(solution)/shard_map/ppermute | solution.py:44
  109.6 9.0 %collective-permute-start.33 = (bf16[288,1024]{1,0:T(8,128)(2,1)S(1)}, bf16[288,1024]{1,0:T(8,128)(2,1)S(1)}, u32[]{:S(2)}, u32[]{:S(2)}) collective-permute-start(bf16[288,1024]{1,0:T(8,128)(2,1)S(1)} %get-tuple-element.473), channel_id=1, source_target_pairs={{0,1},{1,0},{2,3},{3,2},{4,5},{5,4},{6,7},{7,6},{8,9},{9,8},{10,11... | collective-permute-start | bytes 1769480 | tf_op jit(solution)/shard_map/ppermute | solution.py:44
  109.6 8.7 %collective-permute-start.35 = (bf16[128,1024]{1,0:T(8,128)(2,1)S(1)}, bf16[128,1024]{1,0:T(8,128)(2,1)S(1)}, u32[]{:S(2)}, u32[]{:S(2)}) collective-permute-start(bf16[128,1024]{1,0:T(8,128)(2,1)S(1)} %collective-permute-done.31.refs_2_), channel_id=1, source_target_pairs={{0,4},{8,0},{16,8},{24,16},{28,24},{20,28},{12,20},{4,12},{1,5},{9... | collective-permute-start | bytes 786440 | tf_op jit(solution)/shard_map/ppermute | solution.py:329
  110.1 8.4 %collective-permute-start.36 = (bf16[128,1024]{1,0:T(8,128)(2,1)S(1)}, bf16[128,1024]{1,0:T(8,128)(2,1)S(1)}, u32[]{:S(2)}, u32[]{:S(2)}) collective-permute-start(bf16[128,1024]{1,0:T(8,128)(2,1)S(1)} %collective-permute-done.32.refs_6_), channel_id=1, source_target_pairs={{0,8},{8,16},{16,24},{24,28},{28,20},{20,12},{12,4},{4,0},{1,9},{9... | collective-permute-start | bytes 786440 | tf_op jit(solution)/shard_map/ppermute | solution.py:329
  120.9 7.6 %collective-permute-start.38 = (bf16[72,1024]{1,0:T(8,128)(2,1)S(1)}, bf16[72,1024]{1,0:T(8,128)(2,1)S(1)}, u32[]{:S(2)}, u32[]{:S(2)}) collective-permute-start(bf16[72,1024]{1,0:T(8,128)(2,1)S(1)} %get-tuple-element.500.p0), channel_id=1, source_target_pairs={{0,1},{1,0},{2,3},{3,2},{4,5},{5,4},{6,7},{7,6},{8,9},{9,8},{10,11... | collective-permute-start | bytes 442376 | tf_op jit(solution)/shard_map/ppermute | solution.py:44
  121.0 7.5 %collective-permute-start.37 = (bf16[72,1024]{1,0:T(8,128)(2,1)S(1)}, bf16[72,1024]{1,0:T(8,128)(2,1)S(1)}, u32[]{:S(2)}, u32[]{:S(2)}) collective-permute-start(bf16[72,1024]{1,0:T(8,128)(2,1)S(1)} %get-tuple-element.500.p0), channel_id=1, source_target_pairs={{0,2},{1,3},{2,0},{3,1},{4,6},{5,7},{6,4},{7,5},{8,10},{9,11},{10,... | collective-permute-start | bytes 442376 | tf_op jit(solution)/shard_map/ppermute | solution.py:44
  134.7 6.0 %collective-permute-start.43 = (bf16[72,1024]{1,0:T(8,128)(2,1)S(1)}, bf16[72,1024]{1,0:T(8,128)(2,1)S(1)}, u32[]{:S(2)}, u32[]{:S(2)}) collective-permute-start(bf16[72,1024]{1,0:T(8,128)(2,1)S(1)} %fusion.14), channel_id=1, source_target_pairs={{0,2},{1,3},{2,0},{3,1},{4,6},{5,7},{6,4},{7,5},{8,10},{9,11},{10,... | collective-permute-start | bytes 442376 | tf_op jit(solution)/shard_map/ppermute | solution.py:44
  147.4 7.2 %collective-permute-start.48 = (bf16[144,1024]{1,0:T(8,128)(2,1)S(1)}, bf16[144,1024]{1,0:T(8,128)(2,1)S(1)}, u32[]{:S(2)}, u32[]{:S(2)}) collective-permute-start(bf16[144,1024]{1,0:T(8,128)(2,1)S(1)} %pad_maximum_fusion), channel_id=1, source_target_pairs={{0,8},{8,16},{16,24},{24,28},{28,20},{20,12},{12,4},{4,0},{1,9},{9... | collective-permute-start | bytes 884744 | tf_op jit(solution)/shard_map/ppermute | solution.py:329
  148.6 6.9 %collective-permute-start.50 = (bf16[144,1024]{1,0:T(8,128)(2,1)S(1)}, bf16[144,1024]{1,0:T(8,128)(2,1)S(1)}, u32[]{:S(2)}, u32[]{:S(2)}) collective-permute-start(bf16[144,1024]{1,0:T(8,128)(2,1)S(1)} %pad_maximum_fusion.1), channel_id=1, source_target_pairs={{0,4},{8,0},{16,8},{24,16},{28,24},{20,28},{12,20},{4,12},{1,5},{9... | collective-permute-start | bytes 884744 | tf_op jit(solution)/shard_map/ppermute | solution.py:329
  149.6 10.4 %collective-permute-start.47 = (bf16[288,1024]{1,0:T(8,128)(2,1)S(1)}, bf16[288,1024]{1,0:T(8,128)(2,1)S(1)}, u32[]{:S(2)}, u32[]{:S(2)}) collective-permute-start(bf16[288,1024]{1,0:T(8,128)(2,1)S(1)} %get-tuple-element.574.g0), channel_id=1, source_target_pairs={{0,1},{1,0},{2,3},{3,2},{4,5},{5,4},{6,7},{7,6},{8,9},{9,8},{10,11... | collective-permute-start | bytes 1769480 | tf_op jit(solution)/shard_map/ppermute | solution.py:44
  149.6 16.4 %collective-permute-start.46 = (bf16[288,1024]{1,0:T(8,128)(2,1)S(1)}, bf16[288,1024]{1,0:T(8,128)(2,1)S(1)}, u32[]{:S(2)}, u32[]{:S(2)}) collective-permute-start(bf16[288,1024]{1,0:T(8,128)(2,1)S(1)} %get-tuple-element.574.g0), channel_id=1, source_target_pairs={{0,2},{1,3},{2,0},{3,1},{4,6},{5,7},{6,4},{7,5},{8,10},{9,11},{10,... | collective-permute-start | bytes 1769480 | tf_op jit(solution)/shard_map/ppermute | solution.py:44
  155.8 10.2 %collective-permute-start.51 = (bf16[144,1024]{1,0:T(8,128)(2,1)S(1)}, bf16[144,1024]{1,0:T(8,128)(2,1)S(1)}, u32[]{:S(2)}, u32[]{:S(2)}) collective-permute-start(bf16[144,1024]{1,0:T(8,128)(2,1)S(1)} %get-tuple-element.710), channel_id=1, source_target_pairs={{0,4},{8,0},{16,8},{24,16},{28,24},{20,28},{12,20},{4,12},{1,5},{9... | collective-permute-start | bytes 884744 | tf_op jit(solution)/shard_map/ppermute | solution.py:329
  156.7 9.2 %collective-permute-start.49 = (bf16[144,1024]{1,0:T(8,128)(2,1)S(1)}, bf16[144,1024]{1,0:T(8,128)(2,1)S(1)}, u32[]{:S(2)}, u32[]{:S(2)}) collective-permute-start(bf16[144,1024]{1,0:T(8,128)(2,1)S(1)} %get-tuple-element.711), channel_id=1, source_target_pairs={{0,8},{8,16},{16,24},{24,28},{28,20},{20,12},{12,4},{4,0},{1,9},{9... | collective-permute-start | bytes 884744 | tf_op jit(solution)/shard_map/ppermute | solution.py:329
  166.8 9.0 %collective-permute-start.56 = (bf16[144,1024]{1,0:T(8,128)(2,1)S(1)}, bf16[144,1024]{1,0:T(8,128)(2,1)S(1)}, u32[]{:S(2)}, u32[]{:S(2)}) collective-permute-start(bf16[144,1024]{1,0:T(8,128)(2,1)S(1)} %get-tuple-element.708), channel_id=1, source_target_pairs={{0,4},{8,0},{16,8},{24,16},{28,24},{20,28},{12,20},{4,12},{1,5},{9... | collective-permute-start | bytes 884744 | tf_op jit(solution)/shard_map/ppermute | solution.py:329
  167.7 8.7 %collective-permute-start.55 = (bf16[144,1024]{1,0:T(8,128)(2,1)S(1)}, bf16[144,1024]{1,0:T(8,128)(2,1)S(1)}, u32[]{:S(2)}, u32[]{:S(2)}) collective-permute-start(bf16[144,1024]{1,0:T(8,128)(2,1)S(1)} %get-tuple-element.709), channel_id=1, source_target_pairs={{0,8},{8,16},{16,24},{24,28},{28,20},{20,12},{12,4},{4,0},{1,9},{9... | collective-permute-start | bytes 884744 | tf_op jit(solution)/shard_map/ppermute | solution.py:329
  169.5 8.3 %collective-permute-start.54 = (bf16[4,32,1024]{2,1,0:T(8,128)(2,1)S(1)}, bf16[4,32,1024]{2,1,0:T(8,128)(2,1)S(1)}, u32[]{:S(2)}, u32[]{:S(2)}) collective-permute-start(bf16[4,32,1024]{2,1,0:T(8,128)(2,1)S(1)} %get-tuple-element.565), channel_id=1, source_target_pairs={{0,2},{1,3},{2,0},{3,1},{4,6},{5,7},{6,4},{7,5},{8,10},{9,11},{10,... | collective-permute-start | bytes 786440 | tf_op jit(solution)/shard_map/ppermute | solution.py:44
  177.9 11.0 %collective-permute-start.57 = (bf16[5,32,1024]{2,1,0:T(8,128)(2,1)S(1)}, bf16[5,32,1024]{2,1,0:T(8,128)(2,1)S(1)}, u32[]{:S(2)}, u32[]{:S(2)}) collective-permute-start(bf16[5,32,1024]{2,1,0:T(8,128)(2,1)S(1)} %get-tuple-element.572), channel_id=1, source_target_pairs={{0,8},{8,16},{16,24},{24,28},{28,20},{20,12},{12,4},{4,0},{1,9},{9... | collective-permute-start | bytes 983048 | tf_op jit(solution)/shard_map/ppermute | solution.py:329
  178.5 10.4 %collective-permute-start.58 = (bf16[5,32,1024]{2,1,0:T(8,128)(2,1)S(1)}, bf16[5,32,1024]{2,1,0:T(8,128)(2,1)S(1)}, u32[]{:S(2)}, u32[]{:S(2)}) collective-permute-start(bf16[5,32,1024]{2,1,0:T(8,128)(2,1)S(1)} %get-tuple-element.573), channel_id=1, source_target_pairs={{0,4},{8,0},{16,8},{24,16},{28,24},{20,28},{12,20},{4,12},{1,5},{9... | collective-permute-start | bytes 983048 | tf_op jit(solution)/shard_map/ppermute | solution.py:329
  179.9 9.0 %collective-permute-start.59 = (bf16[4,32,1024]{2,1,0:T(8,128)(2,1)S(1)}, bf16[4,32,1024]{2,1,0:T(8,128)(2,1)S(1)}, u32[]{:S(2)}, u32[]{:S(2)}) collective-permute-start(bf16[4,32,1024]{2,1,0:T(8,128)(2,1)S(1)} %get-tuple-element.582), channel_id=1, source_target_pairs={{0,2},{1,3},{2,0},{3,1},{4,6},{5,7},{6,4},{7,5},{8,10},{9,11},{10,... | collective-permute-start | bytes 786440 | tf_op jit(solution)/shard_map/ppermute | solution.py:44
  189.0 11.3 %collective-permute-start.61 = (bf16[5,32,1024]{2,1,0:T(8,128)(2,1)S(1)}, bf16[5,32,1024]{2,1,0:T(8,128)(2,1)S(1)}, u32[]{:S(2)}, u32[]{:S(2)}) collective-permute-start(bf16[5,32,1024]{2,1,0:T(8,128)(2,1)S(1)} %add_convert_fusion.9), channel_id=1, source_target_pairs={{0,4},{8,0},{16,8},{24,16},{28,24},{20,28},{12,20},{4,12},{1,5},{9... | collective-permute-start | bytes 983048 | tf_op jit(solution)/shard_map/ppermute | solution.py:329
  189.7 10.6 %collective-permute-start.60 = (bf16[5,32,1024]{2,1,0:T(8,128)(2,1)S(1)}, bf16[5,32,1024]{2,1,0:T(8,128)(2,1)S(1)}, u32[]{:S(2)}, u32[]{:S(2)}) collective-permute-start(bf16[5,32,1024]{2,1,0:T(8,128)(2,1)S(1)} %add_convert_fusion.10), channel_id=1, source_target_pairs={{0,8},{8,16},{16,24},{24,28},{28,20},{20,12},{12,4},{4,0},{1,9},{9... | collective-permute-start | bytes 983048 | tf_op jit(solution)/shard_map/ppermute | solution.py:329
  191.3 6.6 %collective-permute-start.63 = (bf16[288,256]{1,0:T(8,128)(2,1)S(1)}, bf16[288,256]{1,0:T(8,128)(2,1)S(1)}, u32[]{:S(2)}, u32[]{:S(2)}) collective-permute-start(bf16[288,256]{1,0:T(8,128)(2,1)S(1)} %get-tuple-element.602), channel_id=1, source_target_pairs={{0,2},{1,3},{2,0},{3,1},{4,6},{5,7},{6,4},{7,5},{8,10},{9,11},{10,... | collective-permute-start | bytes 442376 | tf_op jit(solution)/shard_map/ppermute | solution.py:44
  192.2 8.1 %collective-permute-start.64 = (bf16[288,256]{1,0:T(8,128)(2,1)S(1)}, bf16[288,256]{1,0:T(8,128)(2,1)S(1)}, u32[]{:S(2)}, u32[]{:S(2)}) collective-permute-start(bf16[288,256]{1,0:T(8,128)(2,1)S(1)} %get-tuple-element.603), channel_id=1, source_target_pairs={{0,3},{1,2},{2,1},{3,0},{4,7},{5,6},{6,5},{7,4},{8,11},{9,10},{10,... | collective-permute-start | bytes 442376 | tf_op jit(solution)/shard_map/ppermute | solution.py:44
  200.3 9.8 %collective-permute-start.65 = (bf16[5,32,1024]{2,1,0:T(8,128)(2,1)S(1)}, bf16[5,32,1024]{2,1,0:T(8,128)(2,1)S(1)}, u32[]{:S(2)}, u32[]{:S(2)}) collective-permute-start(bf16[5,32,1024]{2,1,0:T(8,128)(2,1)S(1)} %get-tuple-element.607), channel_id=1, source_target_pairs={{0,8},{8,16},{16,24},{24,28},{28,20},{20,12},{12,4},{4,0},{1,9},{9... | collective-permute-start | bytes 983048 | tf_op jit(solution)/shard_map/ppermute | solution.py:329
  201.3 9.5 %collective-permute-start.66 = (bf16[5,32,1024]{2,1,0:T(8,128)(2,1)S(1)}, bf16[5,32,1024]{2,1,0:T(8,128)(2,1)S(1)}, u32[]{:S(2)}, u32[]{:S(2)}) collective-permute-start(bf16[5,32,1024]{2,1,0:T(8,128)(2,1)S(1)} %get-tuple-element.608), channel_id=1, source_target_pairs={{0,4},{8,0},{16,8},{24,16},{28,24},{20,28},{12,20},{4,12},{1,5},{9... | collective-permute-start | bytes 983048 | tf_op jit(solution)/shard_map/ppermute | solution.py:329
  211.9 9.3 %collective-permute-start.67 = (bf16[5,32,1024]{2,1,0:T(8,128)(2,1)S(1)}, bf16[5,32,1024]{2,1,0:T(8,128)(2,1)S(1)}, u32[]{:S(2)}, u32[]{:S(2)}) collective-permute-start(bf16[5,32,1024]{2,1,0:T(8,128)(2,1)S(1)} %add_convert_fusion.8), channel_id=1, source_target_pairs={{0,8},{8,16},{16,24},{24,28},{28,20},{20,12},{12,4},{4,0},{1,9},{9... | collective-permute-start | bytes 983048 | tf_op jit(solution)/shard_map/ppermute | solution.py:329
  212.3 9.1 %collective-permute-start.68 = (bf16[5,32,1024]{2,1,0:T(8,128)(2,1)S(1)}, bf16[5,32,1024]{2,1,0:T(8,128)(2,1)S(1)}, u32[]{:S(2)}, u32[]{:S(2)}) collective-permute-start(bf16[5,32,1024]{2,1,0:T(8,128)(2,1)S(1)} %add_convert_fusion.7), channel_id=1, source_target_pairs={{0,4},{8,0},{16,8},{24,16},{28,24},{20,28},{12,20},{4,12},{1,5},{9... | collective-permute-start | bytes 983048 | tf_op jit(solution)/shard_map/ppermute | solution.py:329
  214.2 6.2 %collective-permute-start.72 = (bf16[72,1024]{1,0:T(8,128)(2,1)S(1)}, bf16[72,1024]{1,0:T(8,128)(2,1)S(1)}, u32[]{:S(2)}, u32[]{:S(2)}) collective-permute-start(bf16[72,1024]{1,0:T(8,128)(2,1)S(1)} %get-tuple-element.635), channel_id=1, source_target_pairs={{0,3},{1,2},{2,1},{3,0},{4,7},{5,6},{6,5},{7,4},{8,11},{9,10},{10,... | collective-permute-start | bytes 442376 | tf_op jit(solution)/shard_map/ppermute | solution.py:44
  221.4 8.8 %collective-permute-start.73 = (bf16[5,32,1024]{2,1,0:T(8,128)(2,1)S(1)}, bf16[5,32,1024]{2,1,0:T(8,128)(2,1)S(1)}, u32[]{:S(2)}, u32[]{:S(2)}) collective-permute-start(bf16[5,32,1024]{2,1,0:T(8,128)(2,1)S(1)} %add_convert_fusion.6), channel_id=1, source_target_pairs={{0,8},{8,16},{16,24},{24,28},{28,20},{20,12},{12,4},{4,0},{1,9},{9... | collective-permute-start | bytes 983048 | tf_op jit(solution)/shard_map/ppermute | solution.py:329
  221.7 8.5 %collective-permute-start.74 = (bf16[5,32,1024]{2,1,0:T(8,128)(2,1)S(1)}, bf16[5,32,1024]{2,1,0:T(8,128)(2,1)S(1)}, u32[]{:S(2)}, u32[]{:S(2)}) collective-permute-start(bf16[5,32,1024]{2,1,0:T(8,128)(2,1)S(1)} %add_convert_fusion.5), channel_id=1, source_target_pairs={{0,4},{8,0},{16,8},{24,16},{28,24},{20,28},{12,20},{4,12},{1,5},{9... | collective-permute-start | bytes 983048 | tf_op jit(solution)/shard_map/ppermute | solution.py:329
  223.4 8.2 %collective-permute-start.75 = (bf16[4,40,1024]{2,1,0:T(8,128)(2,1)S(1)}, bf16[4,40,1024]{2,1,0:T(8,128)(2,1)S(1)}, u32[]{:S(2)}, u32[]{:S(2)}) collective-permute-start(bf16[4,40,1024]{2,1,0:T(8,128)(2,1)S(1)} %get-tuple-element.640), channel_id=1, source_target_pairs={{0,2},{1,3},{2,0},{3,1},{4,6},{5,7},{6,4},{7,5},{8,10},{9,11},{10,... | collective-permute-start | bytes 983048 | tf_op jit(solution)/shard_map/ppermute | solution.py:44
  231.8 7.0 %collective-permute-start.81 = (bf16[40,1024]{1,0:T(8,128)(2,1)S(1)}, bf16[40,1024]{1,0:T(8,128)(2,1)S(1)}, u32[]{:S(2)}, u32[]{:S(2)}) collective-permute-start(bf16[40,1024]{1,0:T(8,128)(2,1)S(1)} %get-tuple-element.720), channel_id=1, source_target_pairs={{0,16},{8,24},{16,28},{24,20},{28,12},{20,4},{12,0},{4,8},{1,17},{... | collective-permute-start | bytes 245768 | tf_op jit(solution)/shard_map/ppermute | solution.py:329
  232.0 11.2 %collective-permute-start.76 = (bf16[5,32,1024]{2,1,0:T(8,128)(2,1)S(1)}, bf16[5,32,1024]{2,1,0:T(8,128)(2,1)S(1)}, u32[]{:S(2)}, u32[]{:S(2)}) collective-permute-start(bf16[5,32,1024]{2,1,0:T(8,128)(2,1)S(1)} %add_convert_fusion.4), channel_id=1, source_target_pairs={{0,8},{8,16},{16,24},{24,28},{28,20},{20,12},{12,4},{4,0},{1,9},{9... | collective-permute-start | bytes 983048 | tf_op jit(solution)/shard_map/ppermute | solution.py:329
  233.7 9.5 %collective-permute-start.77 = (bf16[5,32,1024]{2,1,0:T(8,128)(2,1)S(1)}, bf16[5,32,1024]{2,1,0:T(8,128)(2,1)S(1)}, u32[]{:S(2)}, u32[]{:S(2)}) collective-permute-start(bf16[5,32,1024]{2,1,0:T(8,128)(2,1)S(1)} %add_convert_fusion.2), channel_id=1, source_target_pairs={{0,4},{8,0},{16,8},{24,16},{28,24},{20,28},{12,20},{4,12},{1,5},{9... | collective-permute-start | bytes 983048 | tf_op jit(solution)/shard_map/ppermute | solution.py:329
  234.2 9.0 %collective-permute-start.78 = (bf16[4,40,1024]{2,1,0:T(8,128)(2,1)S(1)}, bf16[4,40,1024]{2,1,0:T(8,128)(2,1)S(1)}, u32[]{:S(2)}, u32[]{:S(2)}) collective-permute-start(bf16[4,40,1024]{2,1,0:T(8,128)(2,1)S(1)} %get-tuple-element.649), channel_id=1, source_target_pairs={{0,2},{1,3},{2,0},{3,1},{4,6},{5,7},{6,4},{7,5},{8,10},{9,11},{10,... | collective-permute-start | bytes 983048 | tf_op jit(solution)/shard_map/ppermute | solution.py:44
  244.0 8.4 %collective-permute-start.85 = (bf16[40,1024]{1,0:T(8,128)(2,1)}, bf16[40,1024]{1,0:T(8,128)(2,1)}, u32[]{:S(2)}, u32[]{:S(2)}) collective-permute-start(bf16[40,1024]{1,0:T(8,128)(2,1)} %fusion.17), channel_id=1, source_target_pairs={{0,4},{8,0},{16,8},{24,16},{28,24},{20,28},{12,20},{4,12},{1,5},{9... | collective-permute-start | bytes 245768 | tf_op jit(solution)/shard_map/ppermute | solution.py:329
  247.5 8.7 %collective-permute-start.83 = (bf16[5,32,1024]{2,1,0:T(8,128)(2,1)}, bf16[5,32,1024]{2,1,0:T(8,128)(2,1)S(1)}, u32[]{:S(2)}, u32[]{:S(2)}) collective-permute-start(bf16[5,32,1024]{2,1,0:T(8,128)(2,1)} %add_convert_fusion.1), channel_id=1, source_target_pairs={{0,4},{8,0},{16,8},{24,16},{28,24},{20,28},{12,20},{4,12},{1,5},{9... | collective-permute-start | bytes 983048 | tf_op jit(solution)/shard_map/ppermute | solution.py:329
  248.0 8.2 %collective-permute-start.82 = (bf16[5,32,1024]{2,1,0:T(8,128)(2,1)S(1)}, bf16[5,32,1024]{2,1,0:T(8,128)(2,1)S(1)}, u32[]{:S(2)}, u32[]{:S(2)}) collective-permute-start(bf16[5,32,1024]{2,1,0:T(8,128)(2,1)S(1)} %add_convert_fusion.3), channel_id=1, source_target_pairs={{0,8},{8,16},{16,24},{24,28},{28,20},{20,12},{12,4},{4,0},{1,9},{9... | collective-permute-start | bytes 983048 | tf_op jit(solution)/shard_map/ppermute | solution.py:329
  250.2 6.0 %collective-permute-start.84 = (bf16[40,1024]{1,0:T(8,128)(2,1)}, bf16[40,1024]{1,0:T(8,128)(2,1)S(1)}, u32[]{:S(2)}, u32[]{:S(2)}) collective-permute-start(bf16[40,1024]{1,0:T(8,128)(2,1)} %fusion.19), channel_id=1, source_target_pairs={{0,8},{8,16},{16,24},{24,28},{28,20},{20,12},{12,4},{4,0},{1,9},{9... | collective-permute-start | bytes 245768 | tf_op jit(solution)/shard_map/ppermute | solution.py:329
  257.1 5.9 %collective-permute-start.87 = (bf16[40,1024]{1,0:T(8,128)(2,1)S(1)}, bf16[40,1024]{1,0:T(8,128)(2,1)S(1)}, u32[]{:S(2)}, u32[]{:S(2)}) collective-permute-start(bf16[40,1024]{1,0:T(8,128)(2,1)S(1)} %get-tuple-element.718), channel_id=1, source_target_pairs={{0,4},{8,0},{16,8},{24,16},{28,24},{20,28},{12,20},{4,12},{1,5},{9... | collective-permute-start | bytes 245768 | tf_op jit(solution)/shard_map/ppermute | solution.py:329
  (31 other events, 206.7 us)

commit v3 on v2

--- a/solution.py
+++ b/solution.py
@@ -691,14 +691,11 @@
     group = o0.shape[1]
     width = whole.shape[1]
     held[...] = jnp.zeros_like(held)
-    @pl.loop(0, 3)
-    def _(u):
-        at = pl.ds(pl.multiple_of(8 + u * cols, 8), patches)
+    for u in range(3):
         for v in range(3):
             part = dot_t(whole[...], weight[u * 3 + v].reshape(group, width))
             for i in range(slots):
-                held[v, i, at, :] += part[i * patches : (i + 1) * patches]
-
+                held[v, i, 8 + u * cols : 8 + u * cols + patches, :] += part[i * patches : (i + 1) * patches]
     col = lax.broadcasted_iota(jnp.int32, (patches, group), 0) % cols
     for i in range(slots):
         value = held[1, i, 8 + cols : 8 + cols + patches, :]

time: 265 us -> 263 us (level)
  no operation moved by 1% of the time
where the time goes in v3:
time: 263 us
  waiting for transfers between devices  117 us (44%)
  starting transfers between devices  73.5 us (28%)
  Pallas kernels  56.3 us (21%)
  local copies, waits for them, and re-layouts  9.23 us (4%)
  other arithmetic  5.45 us (2%)
    ppermute x53, waiting for transfers between devices, hop(): lax.ppermute(x, 'dp', [(order[i], order[(i + step) % RING]) for i in rang...  77.1 us
    pallas_call x20, Pallas kernels, kernel(): pl.pallas_call(body, out_shape=outs, in_specs=ins, out_specs=jax.tree.map...  56.3 us
    ppermute x53, starting transfers between devices, hop(): lax.ppermute(x, 'dp', [(order[i], order[(i + step) % RING]) for i in rang...  55 us
    ppermute x35, waiting for transfers between devices, swap_row(): return lax.ppermute(x, 'row', [(i, i ^ q) for i in range(4)])  39.6 us
    ppermute x35, starting transfers between devices, swap_row(): return lax.ppermute(x, 'row', [(i, i ^ q) for i in range(4)])  18.5 us
  transfers between devices with their start and end apart: 88, of which 47 were waited for; matrix products, arithmetic and copies ran while one was open for 5% of the time, Pallas kernels for 19%

profile of v3, /device:TPU:0, one launch (start us, length us, event | category | flops | bytes accessed | tf_op | source)
XLA Modules:
  0.0 263.1 jit_solution(1449468464360265638)
XLA Ops:
  0.7 3.1 %collective-permute-start.1 = (bf16[9,32,1024]{2,1,0:T(8,128)(2,1)}, bf16[9,32,1024]{2,1,0:T(8,128)(2,1)S(1)}, u32[]{:S(2)}, u32[]{:S(2)}) collective-permute-start(bf16[9,32,1024]{2,1,0:T(8,128)(2,1)} %bitcast.105), channel_id=1, source_target_pairs={{0,8},{8,16},{16,24},{24,28},{28,20},{20,12},{12,4},{4,0},{1,9},{9... | collective-permute-start | bytes 1769480 | tf_op jit(solution)/shard_map/ppermute | solution.py:329
  6.2 2.1 collective-permute-start.3
  11.6 8.8 %collective-permute-done.3.refs_7_ = bf16[72,1024]{1,0:T(8,128)(2,1)S(1)} collective-permute-done((bf16[72,1024]{1,0:T(8,128)(2,1)S(1)}, bf16[72,1024]{1,0:T(8,128)(2,1)S(1)}, u32[]{:S(2)}, u32[]{:S(2)}) %collective-permute-start.3) | collective-permute-done | bytes 147488 | tf_op jit(solution)/shard_map/ppermute | solution.py:329
  20.4 1.5 collective-permute-done.2.refs_1_
  22.2 1.7 collective-permute-start.5
  24.7 2.4 collective-permute-done.4.refs_2_
  27.4 1.7 collective-permute-start.6
  29.4 3.1 %collective-permute-done.6.refs_3_ = bf16[72,1024]{1,0:T(8,128)(2,1)S(1)} collective-permute-done((bf16[72,1024]{1,0:T(8,128)(2,1)S(1)}, bf16[72,1024]{1,0:T(8,128)(2,1)S(1)}, u32[]{:S(2)}, u32[]{:S(2)}) %collective-permute-start.6) | collective-permute-done | bytes 147488 | tf_op jit(solution)/shard_map/ppermute | solution.py:329
  32.5 1.7 collective-permute-done.7.refs_5_
  34.2 1.6 collective-permute-start.9
  36.2 3.8 %collective-permute-done.8.refs_4_ = bf16[32,1024]{1,0:T(8,128)(2,1)S(1)} collective-permute-done((bf16[32,1024]{1,0:T(8,128)(2,1)S(1)}, bf16[32,1024]{1,0:T(8,128)(2,1)S(1)}, u32[]{:S(2)}, u32[]{:S(2)}) %collective-permute-start.8) | collective-permute-done | bytes 65568 | tf_op jit(solution)/shard_map/ppermute | solution.py:329
  40.7 1.6 collective-permute-start.12
  42.3 1.8 collective-permute-start.10
  44.3 13.4 %collective-permute-done.10.refs_2_ = bf16[9,32,1024]{2,1,0:T(8,128)(2,1)S(1)} collective-permute-done((bf16[9,32,1024]{2,1,0:T(8,128)(2,1)S(1)}, bf16[9,32,1024]{2,1,0:T(8,128)(2,1)S(1)}, u32[]{:S(2)}, u32[]{:S(2)}) %collective-permute-start.10) | collective-permute-done | bytes 589856 | tf_op jit(solution)/shard_map/ppermute | solution.py:329
  57.7 1.8 collective-permute-done.11.refs_6_
  59.6 1.8 collective-permute-start.14
  62.2 2.0 shard_map.154
  64.3 11.7 %collective-permute-done.17.l2 = bf16[8,32,1024]{2,1,0:T(8,128)(2,1)S(1)} collective-permute-done((bf16[8,32,1024]{2,1,0:T(8,128)(2,1)S(1)}, bf16[8,32,1024]{2,1,0:T(8,128)(2,1)S(1)}, u32[]{:S(2)}, u32[]{:S(2)}) %collective-permute-start.17) | collective-permute-done | bytes 524320 | tf_op jit(solution)/shard_map/ppermute | solution.py:44
  77.4 1.7 collective-permute-start.20
  80.5 5.4 %collective-permute-done.22.s2 = bf16[288,256]{1,0:T(8,128)(2,1)S(1)} collective-permute-done((bf16[288,256]{1,0:T(8,128)(2,1)S(1)}, bf16[288,256]{1,0:T(8,128)(2,1)S(1)}, u32[]{:S(2)}, u32[]{:S(2)}) %collective-permute-start.22) | collective-permute-done | bytes 147488 | tf_op jit(solution)/shard_map/ppermute | solution.py:44
  87.4 1.8 collective-permute-start.25
  91.1 5.9 %shard_map.155 = (f32[288,1024]{1,0:T(8,128)S(1)}, bf16[288,1024]{1,0:T(8,128)(2,1)S(1)}, bf16[576,2304]{1,0:T(8,128)(2,1)S(1)}, bf16[9,8,32,1024]{3,2,1,0:T(8,128)(2,1)S(1)}) custom-call(s32[20]{0:T(128)S(1)} %compare_select_fusion.12.where, bf16[288,256]{1,0:T(8,128)(2,1)S(1)} %get-tuple-element.461.s0, bf16[288,256]{1,0:T(8,128)(2,1)S(1)} %collective-permute-done.21.s1, ...), custom_call_target="tpu_custom_call" | custom-call | flops 42467328 | bytes 364032 | tf_op jit(solution)/shard_map/pallas_call | solution.py:297
  98.5 1.6 collective-permute-done.30
  102.9 5.4 %shard_map.156 = (f32[288,1024]{1,0:T(8,128)S(1)}, bf16[288,1024]{1,0:T(8,128)(2,1)S(1)}, bf16[576,2304]{1,0:T(8,128)(2,1)S(1)}) custom-call(s32[20]{0:T(128)S(1)} %compare_select_fusion.12.where, bf16[288,256]{1,0:T(8,128)(2,1)S(1)} %get-tuple-element.461.s0, bf16[288,256]{1,0:T(8,128)(2,1)S(1)} %collective-permute-done.21.s1, ...), custom_call_target="tpu_custom_call" | custom-call | flops 42467328 | bytes 364032 | tf_op jit(solution)/shard_map/pallas_call | solution.py:297
  110.1 1.5 collective-permute-start.36
  111.7 6.7 %collective-permute-done.35.refs_3_ = bf16[128,1024]{1,0:T(8,128)(2,1)S(1)} collective-permute-done((bf16[128,1024]{1,0:T(8,128)(2,1)S(1)}, bf16[128,1024]{1,0:T(8,128)(2,1)S(1)}, u32[]{:S(2)}, u32[]{:S(2)}) %collective-permute-start.35) | collective-permute-done | bytes 262176 | tf_op jit(solution)/shard_map/ppermute | solution.py:329
  118.6 2.3 shard_map.157
  121.0 1.4 collective-permute-start.37
  123.2 1.5 collective-permute-start.39
  124.7 3.5 %collective-permute-done.40.refs_8_ = bf16[64,1024]{1,0:T(8,128)(2,1)S(1)} collective-permute-done((bf16[64,1024]{1,0:T(8,128)(2,1)S(1)}, bf16[64,1024]{1,0:T(8,128)(2,1)S(1)}, u32[]{:S(2)}, u32[]{:S(2)}) %collective-permute-start.40) | collective-permute-done | bytes 131104 | tf_op jit(solution)/shard_map/ppermute | solution.py:329
  129.9 3.1 %shard_map.158 = (bf16[72,1024]{1,0:T(8,128)(2,1)S(1)}, bf16[72,1024]{1,0:T(8,128)(2,1)S(1)}, bf16[72,1024]{1,0:T(8,128)(2,1)S(1)}, bf16[72,1024]{1,0:T(8,128)(2...) custom-call(s32[20]{0:T(128)S(1)} %compare_select_fusion.12.where, ...), custom_call_target="tpu_custom_call" | custom-call | flops 18874368 | bytes 88064 | tf_op jit(solution)/shard_map/pallas_call | solution.py:297
  133.2 1.4 collective-permute-done.42
  135.5 2.2 shard_map.159
  137.7 3.0 %collective-permute-done.43.cross = bf16[72,1024]{1,0:T(8,128)(2,1)S(1)} collective-permute-done((bf16[72,1024]{1,0:T(8,128)(2,1)S(1)}, bf16[72,1024]{1,0:T(8,128)(2,1)S(1)}, u32[]{:S(2)}, u32[]{:S(2)}) %collective-permute-start.43) | collective-permute-done | bytes 147488 | tf_op jit(solution)/shard_map/ppermute | solution.py:44
  140.7 1.5 collective-permute-start.44
  142.7 2.6 shard_map.160
  145.8 1.5 collective-permute-done.45
  150.2 4.3 %collective-permute-done.48 = bf16[144,1024]{1,0:T(8,128)(2,1)S(1)} collective-permute-done((bf16[144,1024]{1,0:T(8,128)(2,1)S(1)}, bf16[144,1024]{1,0:T(8,128)(2,1)S(1)}, u32[]{:S(2)}, u32[]{:S(2)}) %collective-permute-start.48) | collective-permute-done | bytes 294944 | tf_op jit(solution)/shard_map/ppermute | solution.py:329
  157.8 2.1 shard_map.161
  159.9 6.0 %shard_map.162.half = f32[9,256,1024]{2,1,0:T(8,128)S(1)} custom-call(s32[20]{0:T(128)S(1)} %compare_select_fusion.12.where, bf16[576,2304]{1,0:T(8,128)(2,1)S(1)} %get-tuple-element.545.here, bf16[288,1024]{1,0:T(8,128)(2,1)S(1)} %get-tuple-element.574.g0, bf16[288,1024]{1,0:T(8,128)(2,1)S(1)} %collective-permute-done.47.g1), custom_call_target="tpu_custom_call" | custom-call | flops 42467328 | bytes 589824 | tf_op jit(solution)/shard_map/pallas_call | solution.py:297
  170.6 3.8 %shard_map.163 = (bf16[5,32,1024]{2,1,0:T(8,128)(2,1)S(1)}, bf16[5,32,1024]{2,1,0:T(8,128)(2,1)S(1)}, bf16[5,32,1024]{2,1,0:T(8,128)(2,1)S(1)}, bf16[5,32,1024]{...) custom-call(s32[20]{0:T(128)S(1)} %compare_select_fusion.12.where, ...), custom_call_target="tpu_custom_call" | custom-call | flops 47185920 | bytes 327680 | tf_op jit(solution)/shard_map/pallas_call | solution.py:297
  174.4 1.4 collective-permute-done.56.b
  176.5 1.4 collective-permute-done.54.refs_2_
  178.5 1.4 collective-permute-start.58
  181.0 6.6 %shard_map.164 = (bf16[288,256]{1,0:T(8,128)(2,1)S(1)}, bf16[288,256]{1,0:T(8,128)(2,1)S(1)}, bf16[288,256]{1,0:T(8,128)(2,1)S(1)}, bf16[288,256]{1,0:T(8,128)(2,1)S(1)}) custom-call(s32[20]{0:T(128)S(1)} %compare_select_fusion.12.where, bf16[288,1024]{1,0:T(8,128)(2,1)S(1)} %get-tuple-element.574.g0, bf16[288,1024]{1,0:T(8,128)(2,1)S(1)} %collective-permute-done.47.g1, ...), custom_call_target="tpu_custom_call" | custom-call | flops 84934656 | bytes 350208 | tf_op jit(solution)/shard_map/pallas_call | solution.py:297
  191.8 3.3 %shard_map.165 = (bf16[5,32,1024]{2,1,0:T(8,128)(2,1)S(1)}, bf16[5,32,1024]{2,1,0:T(8,128)(2,1)S(1)}, bf16[5,32,1024]{2,1,0:T(8,128)(2,1)S(1)}, bf16[5,32,1024]{...) custom-call(s32[20]{0:T(128)S(1)} %compare_select_fusion.12.where, ...), custom_call_target="tpu_custom_call" | custom-call | flops 37748736 | bytes 262144 | tf_op jit(solution)/shard_map/pallas_call | solution.py:297
  195.2 1.4 collective-permute-done.63.b2
  196.6 2.4 collective-permute-done.64.b3
  201.1 3.2 %shard_map.166 = (bf16[288,1024]{1,0:T(8,128)(2,1)S(1)}, f32[8,40,1024]{2,1,0:T(8,128)S(1)}, bf16[2,8,40,1024]{3,2,1,0:T(8,128)(2,1)S(1)}, f32[8,40,1024]{2,1,0:T(8,128)S(1)}) custom-call(s32[20]{0:T(128)S(1)} %compare_select_fusion.12.where, bf16[288,256]{1,0:T(8,128)(2,1)S(1)} %get-tuple-element.609.b0, bf16[288,256]{1,0:T(8,128)(2,1)S(1)} %collective-permute-done.62.b1, ...), custom_call_target="tpu_custom_call" | custom-call | flops 9437184 | bytes 135168 | tf_op jit(solution)/shard_map/pallas_call | solution.py:297
  204.4 4.4 %collective-permute-done.65 = bf16[5,32,1024]{2,1,0:T(8,128)(2,1)S(1)} collective-permute-done((bf16[5,32,1024]{2,1,0:T(8,128)(2,1)S(1)}, bf16[5,32,1024]{2,1,0:T(8,128)(2,1)S(1)}, u32[]{:S(2)}, u32[]{:S(2)}) %collective-permute-start.65) | collective-permute-done | bytes 327712 | tf_op jit(solution)/shard_map/ppermute | solution.py:329
  211.0 1.6 collective-permute-start.68
  213.4 2.4 collective-permute-done.71.i2
  215.8 3.2 %collective-permute-done.72.i3 = bf16[72,1024]{1,0:T(8,128)(2,1)S(1)} collective-permute-done((bf16[72,1024]{1,0:T(8,128)(2,1)S(1)}, bf16[72,1024]{1,0:T(8,128)(2,1)S(1)}, u32[]{:S(2)}, u32[]{:S(2)}) %collective-permute-start.72) | collective-permute-done | bytes 147488 | tf_op jit(solution)/shard_map/ppermute | solution.py:44
  220.4 1.7 collective-permute-start.74
  222.1 1.5 collective-permute-start.75
  223.6 2.2 shard_map.167
  225.9 3.0 %collective-permute-done.73 = bf16[5,32,1024]{2,1,0:T(8,128)(2,1)S(1)} collective-permute-done((bf16[5,32,1024]{2,1,0:T(8,128)(2,1)S(1)}, bf16[5,32,1024]{2,1,0:T(8,128)(2,1)S(1)}, u32[]{:S(2)}, u32[]{:S(2)}) %collective-permute-start.73) | collective-permute-done | bytes 327712 | tf_op jit(solution)/shard_map/ppermute | solution.py:329
  231.1 1.5 collective-permute-start.76
  237.6 3.0 %collective-permute-done.80 = bf16[40,1024]{1,0:T(8,128)(2,1)S(1)} collective-permute-done((bf16[40,1024]{1,0:T(8,128)(2,1)S(1)}, bf16[40,1024]{1,0:T(8,128)(2,1)S(1)}, u32[]{:S(2)}, u32[]{:S(2)}) %collective-permute-start.80) | collective-permute-done | bytes 81952 | tf_op jit(solution)/shard_map/ppermute | solution.py:329
  242.7 2.6 collective-permute-start.85
  246.7 1.5 collective-permute-start.82
  251.1 3.7 %collective-permute-done.84 = bf16[40,1024]{1,0:T(8,128)(2,1)S(1)} collective-permute-done((bf16[40,1024]{1,0:T(8,128)(2,1)}, bf16[40,1024]{1,0:T(8,128)(2,1)S(1)}, u32[]{:S(2)}, u32[]{:S(2)}) %collective-permute-start.84) | collective-permute-done | bytes 81952 | tf_op jit(solution)/shard_map/ppermute | solution.py:329
  256.3 1.5 collective-permute-start.86
  257.9 2.6 copy.24
  (199 shorter events, 67.7 us)
Async XLA Ops:
  0.7 21.2 %collective-permute-start.1 = (bf16[9,32,1024]{2,1,0:T(8,128)(2,1)}, bf16[9,32,1024]{2,1,0:T(8,128)(2,1)S(1)}, u32[]{:S(2)}, u32[]{:S(2)}) collective-permute-start(bf16[9,32,1024]{2,1,0:T(8,128)(2,1)} %bitcast.105), channel_id=1, source_target_pairs={{0,8},{8,16},{16,24},{24,28},{28,20},{20,12},{12,4},{4,0},{1,9},{9... | collective-permute-start | bytes 1769480 | tf_op jit(solution)/shard_map/ppermute | solution.py:329
  3.8 18.2 %collective-permute-start = (bf16[9,32,1024]{2,1,0:T(8,128)(2,1)}, bf16[9,32,1024]{2,1,0:T(8,128)(2,1)S(1)}, u32[]{:S(2)}, u32[]{:S(2)}) collective-permute-start(bf16[9,32,1024]{2,1,0:T(8,128)(2,1)} %bitcast.106), channel_id=1, source_target_pairs={{0,4},{8,0},{16,8},{24,16},{28,24},{20,28},{12,20},{4,12},{1,5},{9... | collective-permute-start | bytes 1769480 | tf_op jit(solution)/shard_map/ppermute | solution.py:329
  6.2 14.2 %collective-permute-start.3 = (bf16[72,1024]{1,0:T(8,128)(2,1)S(1)}, bf16[72,1024]{1,0:T(8,128)(2,1)S(1)}, u32[]{:S(2)}, u32[]{:S(2)}) collective-permute-start(bf16[72,1024]{1,0:T(8,128)(2,1)S(1)} %concatenate.11.refs_0_), channel_id=1, source_target_pairs={{0,8},{8,16},{16,24},{24,28},{28,20},{20,12},{12,4},{4,0},{1,9},{9... | collective-permute-start | bytes 442376 | tf_op jit(solution)/shard_map/ppermute | solution.py:329
  8.2 13.7 %collective-permute-start.2 = (bf16[72,1024]{1,0:T(8,128)(2,1)S(1)}, bf16[72,1024]{1,0:T(8,128)(2,1)S(1)}, u32[]{:S(2)}, u32[]{:S(2)}) collective-permute-start(bf16[72,1024]{1,0:T(8,128)(2,1)S(1)} %concatenate.11.refs_0_), channel_id=1, source_target_pairs={{0,4},{8,0},{16,8},{24,16},{28,24},{20,28},{12,20},{4,12},{1,5},{9... | collective-permute-start | bytes 442376 | tf_op jit(solution)/shard_map/ppermute | solution.py:329
  34.2 5.9 %collective-permute-start.9 = (bf16[40,1024]{1,0:T(8,128)(2,1)S(1)}, bf16[40,1024]{1,0:T(8,128)(2,1)S(1)}, u32[]{:S(2)}, u32[]{:S(2)}) collective-permute-start(bf16[40,1024]{1,0:T(8,128)(2,1)S(1)} %slice.141), channel_id=1, source_target_pairs={{0,4},{8,0},{16,8},{24,16},{28,24},{20,28},{12,20},{4,12},{1,5},{9... | collective-permute-start | bytes 245768 | tf_op jit(solution)/shard_map/ppermute | solution.py:329
  40.7 18.9 %collective-permute-start.13 = (bf16[8,40,1024]{2,1,0:T(8,128)(2,1)S(1)}, bf16[8,40,1024]{2,1,0:T(8,128)(2,1)S(1)}, u32[]{:S(2)}, u32[]{:S(2)}) collective-permute-start(bf16[8,40,1024]{2,1,0:T(8,128)(2,1)S(1)} %get-tuple-element.405.f0), channel_id=1, source_target_pairs={{0,1},{1,0},{2,3},{3,2},{4,5},{5,4},{6,7},{7,6},{8,9},{9,8},{10,11... | collective-permute-start | bytes 1966088 | tf_op jit(solution)/shard_map/ppermute | solution.py:44
  40.7 18.8 %collective-permute-start.12 = (bf16[8,40,1024]{2,1,0:T(8,128)(2,1)S(1)}, bf16[8,40,1024]{2,1,0:T(8,128)(2,1)S(1)}, u32[]{:S(2)}, u32[]{:S(2)}) collective-permute-start(bf16[8,40,1024]{2,1,0:T(8,128)(2,1)S(1)} %get-tuple-element.405.f0), channel_id=1, source_target_pairs={{0,2},{1,3},{2,0},{3,1},{4,6},{5,7},{6,4},{7,5},{8,10},{9,11},{10,... | collective-permute-start | bytes 1966088 | tf_op jit(solution)/shard_map/ppermute | solution.py:44
  42.3 15.4 %collective-permute-start.10 = (bf16[9,32,1024]{2,1,0:T(8,128)(2,1)S(1)}, bf16[9,32,1024]{2,1,0:T(8,128)(2,1)S(1)}, u32[]{:S(2)}, u32[]{:S(2)}) collective-permute-start(bf16[9,32,1024]{2,1,0:T(8,128)(2,1)S(1)} %collective-permute-done.refs_1_), channel_id=1, source_target_pairs={{0,4},{8,0},{16,8},{24,16},{28,24},{20,28},{12,20},{4,12},{1,5},{9... | collective-permute-start | bytes 1769480 | tf_op jit(solution)/shard_map/ppermute | solution.py:329
  44.1 15.4 %collective-permute-start.11 = (bf16[9,32,1024]{2,1,0:T(8,128)(2,1)S(1)}, bf16[9,32,1024]{2,1,0:T(8,128)(2,1)S(1)}, u32[]{:S(2)}, u32[]{:S(2)}) collective-permute-start(bf16[9,32,1024]{2,1,0:T(8,128)(2,1)S(1)} %collective-permute-done.1.refs_7_), channel_id=1, source_target_pairs={{0,8},{8,16},{16,24},{24,28},{28,20},{20,12},{12,4},{4,0},{1,9},{9... | collective-permute-start | bytes 1769480 | tf_op jit(solution)/shard_map/ppermute | solution.py:329
  59.6 16.4 %collective-permute-start.14 = (bf16[9,32,1024]{2,1,0:T(8,128)(2,1)S(1)}, bf16[9,32,1024]{2,1,0:T(8,128)(2,1)S(1)}, u32[]{:S(2)}, u32[]{:S(2)}) collective-permute-start(bf16[9,32,1024]{2,1,0:T(8,128)(2,1)S(1)} %collective-permute-done.10.refs_2_), channel_id=1, source_target_pairs={{0,4},{8,0},{16,8},{24,16},{28,24},{20,28},{12,20},{4,12},{1,5},{9... | collective-permute-start | bytes 1769480 | tf_op jit(solution)/shard_map/ppermute | solution.py:329
  61.3 15.4 %collective-permute-start.15 = (bf16[9,32,1024]{2,1,0:T(8,128)(2,1)S(1)}, bf16[9,32,1024]{2,1,0:T(8,128)(2,1)S(1)}, u32[]{:S(2)}, u32[]{:S(2)}) collective-permute-start(bf16[9,32,1024]{2,1,0:T(8,128)(2,1)S(1)} %collective-permute-done.11.refs_6_), channel_id=1, source_target_pairs={{0,8},{8,16},{16,24},{24,28},{28,20},{20,12},{12,4},{4,0},{1,9},{9... | collective-permute-start | bytes 1769480 | tf_op jit(solution)/shard_map/ppermute | solution.py:329
  61.6 14.3 %collective-permute-start.17 = (bf16[8,32,1024]{2,1,0:T(8,128)(2,1)S(1)}, bf16[8,32,1024]{2,1,0:T(8,128)(2,1)S(1)}, u32[]{:S(2)}, u32[]{:S(2)}) collective-permute-start(bf16[8,32,1024]{2,1,0:T(8,128)(2,1)S(1)} %get-tuple-element.486.l0), channel_id=1, source_target_pairs={{0,2},{1,3},{2,0},{3,1},{4,6},{5,7},{6,4},{7,5},{8,10},{9,11},{10,... | collective-permute-start | bytes 1572872 | tf_op jit(solution)/shard_map/ppermute | solution.py:44
  76.8 10.4 %collective-permute-start.24 = (bf16[8,32,1024]{2,1,0:T(8,128)(2,1)S(1)}, bf16[8,32,1024]{2,1,0:T(8,128)(2,1)S(1)}, u32[]{:S(2)}, u32[]{:S(2)}) collective-permute-start(bf16[8,32,1024]{2,1,0:T(8,128)(2,1)S(1)} %collective-permute-done.17.l2), channel_id=1, source_target_pairs={{0,1},{1,0},{2,3},{3,2},{4,5},{5,4},{6,7},{7,6},{8,9},{9,8},{10,11... | collective-permute-start | bytes 1572872 | tf_op jit(solution)/shard_map/ppermute | solution.py:44
  76.8 10.3 %collective-permute-start.19 = (bf16[5,32,1024]{2,1,0:T(8,128)(2,1)S(1)}, bf16[5,32,1024]{2,1,0:T(8,128)(2,1)S(1)}, u32[]{:S(2)}, u32[]{:S(2)}) collective-permute-start(bf16[5,32,1024]{2,1,0:T(8,128)(2,1)S(1)} %slice.142), channel_id=1, source_target_pairs={{0,8},{8,16},{16,24},{24,28},{28,20},{20,12},{12,4},{4,0},{1,9},{9... | collective-permute-start | bytes 983048 | tf_op jit(solution)/shard_map/ppermute | solution.py:329
  77.4 9.7 %collective-permute-start.20 = (bf16[4,32,1024]{2,1,0:T(8,128)(2,1)S(1)}, bf16[4,32,1024]{2,1,0:T(8,128)(2,1)S(1)}, u32[]{:S(2)}, u32[]{:S(2)}) collective-permute-start(bf16[4,32,1024]{2,1,0:T(8,128)(2,1)S(1)} %slice.143), channel_id=1, source_target_pairs={{0,4},{8,0},{16,8},{24,16},{28,24},{20,28},{12,20},{4,12},{1,5},{9... | collective-permute-start | bytes 786440 | tf_op jit(solution)/shard_map/ppermute | solution.py:329
  79.2 6.7 %collective-permute-start.22 = (bf16[288,256]{1,0:T(8,128)(2,1)S(1)}, bf16[288,256]{1,0:T(8,128)(2,1)S(1)}, u32[]{:S(2)}, u32[]{:S(2)}) collective-permute-start(bf16[288,256]{1,0:T(8,128)(2,1)S(1)} %get-tuple-element.424), channel_id=1, source_target_pairs={{0,2},{1,3},{2,0},{3,1},{4,6},{5,7},{6,4},{7,5},{8,10},{9,11},{10,... | collective-permute-start | bytes 442376 | tf_op jit(solution)/shard_map/ppermute | solution.py:44
  79.7 7.4 %collective-permute-start.23 = (bf16[288,256]{1,0:T(8,128)(2,1)S(1)}, bf16[288,256]{1,0:T(8,128)(2,1)S(1)}, u32[]{:S(2)}, u32[]{:S(2)}) collective-permute-start(bf16[288,256]{1,0:T(8,128)(2,1)S(1)} %get-tuple-element.425), channel_id=1, source_target_pairs={{0,3},{1,2},{2,1},{3,0},{4,7},{5,6},{6,5},{7,4},{8,11},{9,10},{10,... | collective-permute-start | bytes 442376 | tf_op jit(solution)/shard_map/ppermute | solution.py:44
  87.1 10.9 %collective-permute-start.26 = (bf16[128,1024]{1,0:T(8,128)(2,1)S(1)}, bf16[128,1024]{1,0:T(8,128)(2,1)S(1)}, u32[]{:S(2)}, u32[]{:S(2)}) collective-permute-start(bf16[128,1024]{1,0:T(8,128)(2,1)S(1)} %bitcast.102), channel_id=1, source_target_pairs={{0,8},{8,16},{16,24},{24,28},{28,20},{20,12},{12,4},{4,0},{1,9},{9... | collective-permute-start | bytes 786440 | tf_op jit(solution)/shard_map/ppermute | solution.py:329
  87.4 10.6 %collective-permute-start.25 = (bf16[128,1024]{1,0:T(8,128)(2,1)S(1)}, bf16[128,1024]{1,0:T(8,128)(2,1)S(1)}, u32[]{:S(2)}, u32[]{:S(2)}) collective-permute-start(bf16[128,1024]{1,0:T(8,128)(2,1)S(1)} %bitcast.103), channel_id=1, source_target_pairs={{0,4},{8,0},{16,8},{24,16},{28,24},{20,28},{12,20},{4,12},{1,5},{9... | collective-permute-start | bytes 786440 | tf_op jit(solution)/shard_map/ppermute | solution.py:329
  89.2 7.7 %collective-permute-start.27 = (bf16[72,1024]{1,0:T(8,128)(2,1)S(1)}, bf16[72,1024]{1,0:T(8,128)(2,1)S(1)}, u32[]{:S(2)}, u32[]{:S(2)}) collective-permute-start(bf16[72,1024]{1,0:T(8,128)(2,1)S(1)} %get-tuple-element.451), channel_id=1, source_target_pairs={{0,1},{1,0},{2,3},{3,2},{4,5},{5,4},{6,7},{7,6},{8,9},{9,8},{10,11... | collective-permute-start | bytes 442376 | tf_op jit(solution)/shard_map/ppermute | solution.py:44
  89.4 7.5 %collective-permute-start.28 = (bf16[72,1024]{1,0:T(8,128)(2,1)S(1)}, bf16[72,1024]{1,0:T(8,128)(2,1)S(1)}, u32[]{:S(2)}, u32[]{:S(2)}) collective-permute-start(bf16[72,1024]{1,0:T(8,128)(2,1)S(1)} %get-tuple-element.452), channel_id=1, source_target_pairs={{0,2},{1,3},{2,0},{3,1},{4,6},{5,7},{6,4},{7,5},{8,10},{9,11},{10,... | collective-permute-start | bytes 442376 | tf_op jit(solution)/shard_map/ppermute | solution.py:44
  90.0 8.0 %collective-permute-start.29 = (bf16[72,1024]{1,0:T(8,128)(2,1)S(1)}, bf16[72,1024]{1,0:T(8,128)(2,1)S(1)}, u32[]{:S(2)}, u32[]{:S(2)}) collective-permute-start(bf16[72,1024]{1,0:T(8,128)(2,1)S(1)} %get-tuple-element.453), channel_id=1, source_target_pairs={{0,3},{1,2},{2,1},{3,0},{4,7},{5,6},{6,5},{7,4},{8,11},{9,10},{10,... | collective-permute-start | bytes 442376 | tf_op jit(solution)/shard_map/ppermute | solution.py:44
  100.3 8.6 %collective-permute-start.31 = (bf16[128,1024]{1,0:T(8,128)(2,1)S(1)}, bf16[128,1024]{1,0:T(8,128)(2,1)S(1)}, u32[]{:S(2)}, u32[]{:S(2)}) collective-permute-start(bf16[128,1024]{1,0:T(8,128)(2,1)S(1)} %collective-permute-done.25.refs_1_), channel_id=1, source_target_pairs={{0,4},{8,0},{16,8},{24,16},{28,24},{20,28},{12,20},{4,12},{1,5},{9... | collective-permute-start | bytes 786440 | tf_op jit(solution)/shard_map/ppermute | solution.py:329
  101.3 8.3 %collective-permute-start.32 = (bf16[128,1024]{1,0:T(8,128)(2,1)S(1)}, bf16[128,1024]{1,0:T(8,128)(2,1)S(1)}, u32[]{:S(2)}, u32[]{:S(2)}) collective-permute-start(bf16[128,1024]{1,0:T(8,128)(2,1)S(1)} %collective-permute-done.26.refs_7_), channel_id=1, source_target_pairs={{0,8},{8,16},{16,24},{24,28},{28,20},{20,12},{12,4},{4,0},{1,9},{9... | collective-permute-start | bytes 786440 | tf_op jit(solution)/shard_map/ppermute | solution.py:329
  102.4 16.2 %collective-permute-start.34 = (bf16[288,1024]{1,0:T(8,128)(2,1)S(1)}, bf16[288,1024]{1,0:T(8,128)(2,1)S(1)}, u32[]{:S(2)}, u32[]{:S(2)}) collective-permute-start(bf16[288,1024]{1,0:T(8,128)(2,1)S(1)} %add_convert_fusion), channel_id=1, source_target_pairs={{0,2},{1,3},{2,0},{3,1},{4,6},{5,7},{6,4},{7,5},{8,10},{9,11},{10,... | collective-permute-start | bytes 1769480 | tf_op jit(solution)/shard_map/ppermute | solution.py:44
  109.6 9.0 %collective-permute-start.33 = (bf16[288,1024]{1,0:T(8,128)(2,1)S(1)}, bf16[288,1024]{1,0:T(8,128)(2,1)S(1)}, u32[]{:S(2)}, u32[]{:S(2)}) collective-permute-start(bf16[288,1024]{1,0:T(8,128)(2,1)S(1)} %get-tuple-element.473), channel_id=1, source_target_pairs={{0,1},{1,0},{2,3},{3,2},{4,5},{5,4},{6,7},{7,6},{8,9},{9,8},{10,11... | collective-permute-start | bytes 1769480 | tf_op jit(solution)/shard_map/ppermute | solution.py:44
  109.6 8.7 %collective-permute-start.35 = (bf16[128,1024]{1,0:T(8,128)(2,1)S(1)}, bf16[128,1024]{1,0:T(8,128)(2,1)S(1)}, u32[]{:S(2)}, u32[]{:S(2)}) collective-permute-start(bf16[128,1024]{1,0:T(8,128)(2,1)S(1)} %collective-permute-done.31.refs_2_), channel_id=1, source_target_pairs={{0,4},{8,0},{16,8},{24,16},{28,24},{20,28},{12,20},{4,12},{1,5},{9... | collective-permute-start | bytes 786440 | tf_op jit(solution)/shard_map/ppermute | solution.py:329
  110.1 8.4 %collective-permute-start.36 = (bf16[128,1024]{1,0:T(8,128)(2,1)S(1)}, bf16[128,1024]{1,0:T(8,128)(2,1)S(1)}, u32[]{:S(2)}, u32[]{:S(2)}) collective-permute-start(bf16[128,1024]{1,0:T(8,128)(2,1)S(1)} %collective-permute-done.32.refs_6_), channel_id=1, source_target_pairs={{0,8},{8,16},{16,24},{24,28},{28,20},{20,12},{12,4},{4,0},{1,9},{9... | collective-permute-start | bytes 786440 | tf_op jit(solution)/shard_map/ppermute | solution.py:329
  120.9 7.6 %collective-permute-start.38 = (bf16[72,1024]{1,0:T(8,128)(2,1)S(1)}, bf16[72,1024]{1,0:T(8,128)(2,1)S(1)}, u32[]{:S(2)}, u32[]{:S(2)}) collective-permute-start(bf16[72,1024]{1,0:T(8,128)(2,1)S(1)} %get-tuple-element.500.p0), channel_id=1, source_target_pairs={{0,1},{1,0},{2,3},{3,2},{4,5},{5,4},{6,7},{7,6},{8,9},{9,8},{10,11... | collective-permute-start | bytes 442376 | tf_op jit(solution)/shard_map/ppermute | solution.py:44
  121.0 7.5 %collective-permute-start.37 = (bf16[72,1024]{1,0:T(8,128)(2,1)S(1)}, bf16[72,1024]{1,0:T(8,128)(2,1)S(1)}, u32[]{:S(2)}, u32[]{:S(2)}) collective-permute-start(bf16[72,1024]{1,0:T(8,128)(2,1)S(1)} %get-tuple-element.500.p0), channel_id=1, source_target_pairs={{0,2},{1,3},{2,0},{3,1},{4,6},{5,7},{6,4},{7,5},{8,10},{9,11},{10,... | collective-permute-start | bytes 442376 | tf_op jit(solution)/shard_map/ppermute | solution.py:44
  134.7 6.0 %collective-permute-start.43 = (bf16[72,1024]{1,0:T(8,128)(2,1)S(1)}, bf16[72,1024]{1,0:T(8,128)(2,1)S(1)}, u32[]{:S(2)}, u32[]{:S(2)}) collective-permute-start(bf16[72,1024]{1,0:T(8,128)(2,1)S(1)} %fusion.14), channel_id=1, source_target_pairs={{0,2},{1,3},{2,0},{3,1},{4,6},{5,7},{6,4},{7,5},{8,10},{9,11},{10,... | collective-permute-start | bytes 442376 | tf_op jit(solution)/shard_map/ppermute | solution.py:44
  147.4 7.2 %collective-permute-start.48 = (bf16[144,1024]{1,0:T(8,128)(2,1)S(1)}, bf16[144,1024]{1,0:T(8,128)(2,1)S(1)}, u32[]{:S(2)}, u32[]{:S(2)}) collective-permute-start(bf16[144,1024]{1,0:T(8,128)(2,1)S(1)} %pad_maximum_fusion), channel_id=1, source_target_pairs={{0,8},{8,16},{16,24},{24,28},{28,20},{20,12},{12,4},{4,0},{1,9},{9... | collective-permute-start | bytes 884744 | tf_op jit(solution)/shard_map/ppermute | solution.py:329
  148.6 6.9 %collective-permute-start.50 = (bf16[144,1024]{1,0:T(8,128)(2,1)S(1)}, bf16[144,1024]{1,0:T(8,128)(2,1)S(1)}, u32[]{:S(2)}, u32[]{:S(2)}) collective-permute-start(bf16[144,1024]{1,0:T(8,128)(2,1)S(1)} %pad_maximum_fusion.1), channel_id=1, source_target_pairs={{0,4},{8,0},{16,8},{24,16},{28,24},{20,28},{12,20},{4,12},{1,5},{9... | collective-permute-start | bytes 884744 | tf_op jit(solution)/shard_map/ppermute | solution.py:329
  149.6 10.4 %collective-permute-start.47 = (bf16[288,1024]{1,0:T(8,128)(2,1)S(1)}, bf16[288,1024]{1,0:T(8,128)(2,1)S(1)}, u32[]{:S(2)}, u32[]{:S(2)}) collective-permute-start(bf16[288,1024]{1,0:T(8,128)(2,1)S(1)} %get-tuple-element.574.g0), channel_id=1, source_target_pairs={{0,1},{1,0},{2,3},{3,2},{4,5},{5,4},{6,7},{7,6},{8,9},{9,8},{10,11... | collective-permute-start | bytes 1769480 | tf_op jit(solution)/shard_map/ppermute | solution.py:44
  149.6 16.4 %collective-permute-start.46 = (bf16[288,1024]{1,0:T(8,128)(2,1)S(1)}, bf16[288,1024]{1,0:T(8,128)(2,1)S(1)}, u32[]{:S(2)}, u32[]{:S(2)}) collective-permute-start(bf16[288,1024]{1,0:T(8,128)(2,1)S(1)} %get-tuple-element.574.g0), channel_id=1, source_target_pairs={{0,2},{1,3},{2,0},{3,1},{4,6},{5,7},{6,4},{7,5},{8,10},{9,11},{10,... | collective-permute-start | bytes 1769480 | tf_op jit(solution)/shard_map/ppermute | solution.py:44
  155.8 10.2 %collective-permute-start.51 = (bf16[144,1024]{1,0:T(8,128)(2,1)S(1)}, bf16[144,1024]{1,0:T(8,128)(2,1)S(1)}, u32[]{:S(2)}, u32[]{:S(2)}) collective-permute-start(bf16[144,1024]{1,0:T(8,128)(2,1)S(1)} %get-tuple-element.710), channel_id=1, source_target_pairs={{0,4},{8,0},{16,8},{24,16},{28,24},{20,28},{12,20},{4,12},{1,5},{9... | collective-permute-start | bytes 884744 | tf_op jit(solution)/shard_map/ppermute | solution.py:329
  156.7 9.2 %collective-permute-start.49 = (bf16[144,1024]{1,0:T(8,128)(2,1)S(1)}, bf16[144,1024]{1,0:T(8,128)(2,1)S(1)}, u32[]{:S(2)}, u32[]{:S(2)}) collective-permute-start(bf16[144,1024]{1,0:T(8,128)(2,1)S(1)} %get-tuple-element.711), channel_id=1, source_target_pairs={{0,8},{8,16},{16,24},{24,28},{28,20},{20,12},{12,4},{4,0},{1,9},{9... | collective-permute-start | bytes 884744 | tf_op jit(solution)/shard_map/ppermute | solution.py:329
  166.8 9.0 %collective-permute-start.56 = (bf16[144,1024]{1,0:T(8,128)(2,1)S(1)}, bf16[144,1024]{1,0:T(8,128)(2,1)S(1)}, u32[]{:S(2)}, u32[]{:S(2)}) collective-permute-start(bf16[144,1024]{1,0:T(8,128)(2,1)S(1)} %get-tuple-element.708), channel_id=1, source_target_pairs={{0,4},{8,0},{16,8},{24,16},{28,24},{20,28},{12,20},{4,12},{1,5},{9... | collective-permute-start | bytes 884744 | tf_op jit(solution)/shard_map/ppermute | solution.py:329
  167.7 8.7 %collective-permute-start.55 = (bf16[144,1024]{1,0:T(8,128)(2,1)S(1)}, bf16[144,1024]{1,0:T(8,128)(2,1)S(1)}, u32[]{:S(2)}, u32[]{:S(2)}) collective-permute-start(bf16[144,1024]{1,0:T(8,128)(2,1)S(1)} %get-tuple-element.709), channel_id=1, source_target_pairs={{0,8},{8,16},{16,24},{24,28},{28,20},{20,12},{12,4},{4,0},{1,9},{9... | collective-permute-start | bytes 884744 | tf_op jit(solution)/shard_map/ppermute | solution.py:329
  169.5 8.3 %collective-permute-start.54 = (bf16[4,32,1024]{2,1,0:T(8,128)(2,1)S(1)}, bf16[4,32,1024]{2,1,0:T(8,128)(2,1)S(1)}, u32[]{:S(2)}, u32[]{:S(2)}) collective-permute-start(bf16[4,32,1024]{2,1,0:T(8,128)(2,1)S(1)} %get-tuple-element.565), channel_id=1, source_target_pairs={{0,2},{1,3},{2,0},{3,1},{4,6},{5,7},{6,4},{7,5},{8,10},{9,11},{10,... | collective-permute-start | bytes 786440 | tf_op jit(solution)/shard_map/ppermute | solution.py:44
  177.9 9.7 %collective-permute-start.57 = (bf16[5,32,1024]{2,1,0:T(8,128)(2,1)S(1)}, bf16[5,32,1024]{2,1,0:T(8,128)(2,1)S(1)}, u32[]{:S(2)}, u32[]{:S(2)}) collective-permute-start(bf16[5,32,1024]{2,1,0:T(8,128)(2,1)S(1)} %get-tuple-element.572), channel_id=1, source_target_pairs={{0,8},{8,16},{16,24},{24,28},{28,20},{20,12},{12,4},{4,0},{1,9},{9... | collective-permute-start | bytes 983048 | tf_op jit(solution)/shard_map/ppermute | solution.py:329
  178.5 9.1 %collective-permute-start.58 = (bf16[5,32,1024]{2,1,0:T(8,128)(2,1)S(1)}, bf16[5,32,1024]{2,1,0:T(8,128)(2,1)S(1)}, u32[]{:S(2)}, u32[]{:S(2)}) collective-permute-start(bf16[5,32,1024]{2,1,0:T(8,128)(2,1)S(1)} %get-tuple-element.573), channel_id=1, source_target_pairs={{0,4},{8,0},{16,8},{24,16},{28,24},{20,28},{12,20},{4,12},{1,5},{9... | collective-permute-start | bytes 983048 | tf_op jit(solution)/shard_map/ppermute | solution.py:329
  179.9 7.6 %collective-permute-start.59 = (bf16[4,32,1024]{2,1,0:T(8,128)(2,1)S(1)}, bf16[4,32,1024]{2,1,0:T(8,128)(2,1)S(1)}, u32[]{:S(2)}, u32[]{:S(2)}) collective-permute-start(bf16[4,32,1024]{2,1,0:T(8,128)(2,1)S(1)} %get-tuple-element.582), channel_id=1, source_target_pairs={{0,2},{1,3},{2,0},{3,1},{4,6},{5,7},{6,4},{7,5},{8,10},{9,11},{10,... | collective-permute-start | bytes 786440 | tf_op jit(solution)/shard_map/ppermute | solution.py:44
  187.7 11.3 %collective-permute-start.61 = (bf16[5,32,1024]{2,1,0:T(8,128)(2,1)S(1)}, bf16[5,32,1024]{2,1,0:T(8,128)(2,1)S(1)}, u32[]{:S(2)}, u32[]{:S(2)}) collective-permute-start(bf16[5,32,1024]{2,1,0:T(8,128)(2,1)S(1)} %add_convert_fusion.9), channel_id=1, source_target_pairs={{0,4},{8,0},{16,8},{24,16},{28,24},{20,28},{12,20},{4,12},{1,5},{9... | collective-permute-start | bytes 983048 | tf_op jit(solution)/shard_map/ppermute | solution.py:329
  188.8 10.2 %collective-permute-start.60 = (bf16[5,32,1024]{2,1,0:T(8,128)(2,1)S(1)}, bf16[5,32,1024]{2,1,0:T(8,128)(2,1)S(1)}, u32[]{:S(2)}, u32[]{:S(2)}) collective-permute-start(bf16[5,32,1024]{2,1,0:T(8,128)(2,1)S(1)} %add_convert_fusion.10), channel_id=1, source_target_pairs={{0,8},{8,16},{16,24},{24,28},{28,20},{20,12},{12,4},{4,0},{1,9},{9... | collective-permute-start | bytes 983048 | tf_op jit(solution)/shard_map/ppermute | solution.py:329
  189.9 6.6 %collective-permute-start.63 = (bf16[288,256]{1,0:T(8,128)(2,1)S(1)}, bf16[288,256]{1,0:T(8,128)(2,1)S(1)}, u32[]{:S(2)}, u32[]{:S(2)}) collective-permute-start(bf16[288,256]{1,0:T(8,128)(2,1)S(1)} %get-tuple-element.602), channel_id=1, source_target_pairs={{0,2},{1,3},{2,0},{3,1},{4,6},{5,7},{6,4},{7,5},{8,10},{9,11},{10,... | collective-permute-start | bytes 442376 | tf_op jit(solution)/shard_map/ppermute | solution.py:44
  191.0 8.0 %collective-permute-start.64 = (bf16[288,256]{1,0:T(8,128)(2,1)S(1)}, bf16[288,256]{1,0:T(8,128)(2,1)S(1)}, u32[]{:S(2)}, u32[]{:S(2)}) collective-permute-start(bf16[288,256]{1,0:T(8,128)(2,1)S(1)} %get-tuple-element.603), channel_id=1, source_target_pairs={{0,3},{1,2},{2,1},{3,0},{4,7},{5,6},{6,5},{7,4},{8,11},{9,10},{10,... | collective-permute-start | bytes 442376 | tf_op jit(solution)/shard_map/ppermute | solution.py:44
  199.0 9.8 %collective-permute-start.65 = (bf16[5,32,1024]{2,1,0:T(8,128)(2,1)S(1)}, bf16[5,32,1024]{2,1,0:T(8,128)(2,1)S(1)}, u32[]{:S(2)}, u32[]{:S(2)}) collective-permute-start(bf16[5,32,1024]{2,1,0:T(8,128)(2,1)S(1)} %get-tuple-element.607), channel_id=1, source_target_pairs={{0,8},{8,16},{16,24},{24,28},{28,20},{20,12},{12,4},{4,0},{1,9},{9... | collective-permute-start | bytes 983048 | tf_op jit(solution)/shard_map/ppermute | solution.py:329
  200.0 9.5 %collective-permute-start.66 = (bf16[5,32,1024]{2,1,0:T(8,128)(2,1)S(1)}, bf16[5,32,1024]{2,1,0:T(8,128)(2,1)S(1)}, u32[]{:S(2)}, u32[]{:S(2)}) collective-permute-start(bf16[5,32,1024]{2,1,0:T(8,128)(2,1)S(1)} %get-tuple-element.608), channel_id=1, source_target_pairs={{0,4},{8,0},{16,8},{24,16},{28,24},{20,28},{12,20},{4,12},{1,5},{9... | collective-permute-start | bytes 983048 | tf_op jit(solution)/shard_map/ppermute | solution.py:329
  210.6 9.3 %collective-permute-start.67 = (bf16[5,32,1024]{2,1,0:T(8,128)(2,1)S(1)}, bf16[5,32,1024]{2,1,0:T(8,128)(2,1)S(1)}, u32[]{:S(2)}, u32[]{:S(2)}) collective-permute-start(bf16[5,32,1024]{2,1,0:T(8,128)(2,1)S(1)} %add_convert_fusion.8), channel_id=1, source_target_pairs={{0,8},{8,16},{16,24},{24,28},{28,20},{20,12},{12,4},{4,0},{1,9},{9... | collective-permute-start | bytes 983048 | tf_op jit(solution)/shard_map/ppermute | solution.py:329
  211.0 9.1 %collective-permute-start.68 = (bf16[5,32,1024]{2,1,0:T(8,128)(2,1)S(1)}, bf16[5,32,1024]{2,1,0:T(8,128)(2,1)S(1)}, u32[]{:S(2)}, u32[]{:S(2)}) collective-permute-start(bf16[5,32,1024]{2,1,0:T(8,128)(2,1)S(1)} %add_convert_fusion.7), channel_id=1, source_target_pairs={{0,4},{8,0},{16,8},{24,16},{28,24},{20,28},{12,20},{4,12},{1,5},{9... | collective-permute-start | bytes 983048 | tf_op jit(solution)/shard_map/ppermute | solution.py:329
  212.9 6.2 %collective-permute-start.72 = (bf16[72,1024]{1,0:T(8,128)(2,1)S(1)}, bf16[72,1024]{1,0:T(8,128)(2,1)S(1)}, u32[]{:S(2)}, u32[]{:S(2)}) collective-permute-start(bf16[72,1024]{1,0:T(8,128)(2,1)S(1)} %get-tuple-element.635), channel_id=1, source_target_pairs={{0,3},{1,2},{2,1},{3,0},{4,7},{5,6},{6,5},{7,4},{8,11},{9,10},{10,... | collective-permute-start | bytes 442376 | tf_op jit(solution)/shard_map/ppermute | solution.py:44
  220.1 8.8 %collective-permute-start.73 = (bf16[5,32,1024]{2,1,0:T(8,128)(2,1)S(1)}, bf16[5,32,1024]{2,1,0:T(8,128)(2,1)S(1)}, u32[]{:S(2)}, u32[]{:S(2)}) collective-permute-start(bf16[5,32,1024]{2,1,0:T(8,128)(2,1)S(1)} %add_convert_fusion.6), channel_id=1, source_target_pairs={{0,8},{8,16},{16,24},{24,28},{28,20},{20,12},{12,4},{4,0},{1,9},{9... | collective-permute-start | bytes 983048 | tf_op jit(solution)/shard_map/ppermute | solution.py:329
  220.4 8.5 %collective-permute-start.74 = (bf16[5,32,1024]{2,1,0:T(8,128)(2,1)S(1)}, bf16[5,32,1024]{2,1,0:T(8,128)(2,1)S(1)}, u32[]{:S(2)}, u32[]{:S(2)}) collective-permute-start(bf16[5,32,1024]{2,1,0:T(8,128)(2,1)S(1)} %add_convert_fusion.5), channel_id=1, source_target_pairs={{0,4},{8,0},{16,8},{24,16},{28,24},{20,28},{12,20},{4,12},{1,5},{9... | collective-permute-start | bytes 983048 | tf_op jit(solution)/shard_map/ppermute | solution.py:329
  222.1 8.2 %collective-permute-start.75 = (bf16[4,40,1024]{2,1,0:T(8,128)(2,1)S(1)}, bf16[4,40,1024]{2,1,0:T(8,128)(2,1)S(1)}, u32[]{:S(2)}, u32[]{:S(2)}) collective-permute-start(bf16[4,40,1024]{2,1,0:T(8,128)(2,1)S(1)} %get-tuple-element.640), channel_id=1, source_target_pairs={{0,2},{1,3},{2,0},{3,1},{4,6},{5,7},{6,4},{7,5},{8,10},{9,11},{10,... | collective-permute-start | bytes 983048 | tf_op jit(solution)/shard_map/ppermute | solution.py:44
  230.4 7.0 %collective-permute-start.81 = (bf16[40,1024]{1,0:T(8,128)(2,1)S(1)}, bf16[40,1024]{1,0:T(8,128)(2,1)S(1)}, u32[]{:S(2)}, u32[]{:S(2)}) collective-permute-start(bf16[40,1024]{1,0:T(8,128)(2,1)S(1)} %get-tuple-element.720), channel_id=1, source_target_pairs={{0,16},{8,24},{16,28},{24,20},{28,12},{20,4},{12,0},{4,8},{1,17},{... | collective-permute-start | bytes 245768 | tf_op jit(solution)/shard_map/ppermute | solution.py:329
  231.1 10.9 %collective-permute-start.76 = (bf16[5,32,1024]{2,1,0:T(8,128)(2,1)S(1)}, bf16[5,32,1024]{2,1,0:T(8,128)(2,1)S(1)}, u32[]{:S(2)}, u32[]{:S(2)}) collective-permute-start(bf16[5,32,1024]{2,1,0:T(8,128)(2,1)S(1)} %add_convert_fusion.4), channel_id=1, source_target_pairs={{0,8},{8,16},{16,24},{24,28},{28,20},{20,12},{12,4},{4,0},{1,9},{9... | collective-permute-start | bytes 983048 | tf_op jit(solution)/shard_map/ppermute | solution.py:329
  232.7 9.2 %collective-permute-start.77 = (bf16[5,32,1024]{2,1,0:T(8,128)(2,1)S(1)}, bf16[5,32,1024]{2,1,0:T(8,128)(2,1)S(1)}, u32[]{:S(2)}, u32[]{:S(2)}) collective-permute-start(bf16[5,32,1024]{2,1,0:T(8,128)(2,1)S(1)} %add_convert_fusion.2), channel_id=1, source_target_pairs={{0,4},{8,0},{16,8},{24,16},{28,24},{20,28},{12,20},{4,12},{1,5},{9... | collective-permute-start | bytes 983048 | tf_op jit(solution)/shard_map/ppermute | solution.py:329
  233.2 8.7 %collective-permute-start.78 = (bf16[4,40,1024]{2,1,0:T(8,128)(2,1)S(1)}, bf16[4,40,1024]{2,1,0:T(8,128)(2,1)S(1)}, u32[]{:S(2)}, u32[]{:S(2)}) collective-permute-start(bf16[4,40,1024]{2,1,0:T(8,128)(2,1)S(1)} %get-tuple-element.649), channel_id=1, source_target_pairs={{0,2},{1,3},{2,0},{3,1},{4,6},{5,7},{6,4},{7,5},{8,10},{9,11},{10,... | collective-permute-start | bytes 983048 | tf_op jit(solution)/shard_map/ppermute | solution.py:44
  242.7 8.4 %collective-permute-start.85 = (bf16[40,1024]{1,0:T(8,128)(2,1)}, bf16[40,1024]{1,0:T(8,128)(2,1)}, u32[]{:S(2)}, u32[]{:S(2)}) collective-permute-start(bf16[40,1024]{1,0:T(8,128)(2,1)} %fusion.17), channel_id=1, source_target_pairs={{0,4},{8,0},{16,8},{24,16},{28,24},{20,28},{12,20},{4,12},{1,5},{9... | collective-permute-start | bytes 245768 | tf_op jit(solution)/shard_map/ppermute | solution.py:329
  246.1 8.7 %collective-permute-start.83 = (bf16[5,32,1024]{2,1,0:T(8,128)(2,1)}, bf16[5,32,1024]{2,1,0:T(8,128)(2,1)S(1)}, u32[]{:S(2)}, u32[]{:S(2)}) collective-permute-start(bf16[5,32,1024]{2,1,0:T(8,128)(2,1)} %add_convert_fusion.1), channel_id=1, source_target_pairs={{0,4},{8,0},{16,8},{24,16},{28,24},{20,28},{12,20},{4,12},{1,5},{9... | collective-permute-start | bytes 983048 | tf_op jit(solution)/shard_map/ppermute | solution.py:329
  246.7 8.2 %collective-permute-start.82 = (bf16[5,32,1024]{2,1,0:T(8,128)(2,1)S(1)}, bf16[5,32,1024]{2,1,0:T(8,128)(2,1)S(1)}, u32[]{:S(2)}, u32[]{:S(2)}) collective-permute-start(bf16[5,32,1024]{2,1,0:T(8,128)(2,1)S(1)} %add_convert_fusion.3), channel_id=1, source_target_pairs={{0,8},{8,16},{16,24},{24,28},{28,20},{20,12},{12,4},{4,0},{1,9},{9... | collective-permute-start | bytes 983048 | tf_op jit(solution)/shard_map/ppermute | solution.py:329
  248.8 6.0 %collective-permute-start.84 = (bf16[40,1024]{1,0:T(8,128)(2,1)}, bf16[40,1024]{1,0:T(8,128)(2,1)S(1)}, u32[]{:S(2)}, u32[]{:S(2)}) collective-permute-start(bf16[40,1024]{1,0:T(8,128)(2,1)} %fusion.19), channel_id=1, source_target_pairs={{0,8},{8,16},{16,24},{24,28},{28,20},{20,12},{12,4},{4,0},{1,9},{9... | collective-permute-start | bytes 245768 | tf_op jit(solution)/shard_map/ppermute | solution.py:329
  255.8 5.9 %collective-permute-start.87 = (bf16[40,1024]{1,0:T(8,128)(2,1)S(1)}, bf16[40,1024]{1,0:T(8,128)(2,1)S(1)}, u32[]{:S(2)}, u32[]{:S(2)}) collective-permute-start(bf16[40,1024]{1,0:T(8,128)(2,1)S(1)} %get-tuple-element.718), channel_id=1, source_target_pairs={{0,4},{8,0},{16,8},{24,16},{28,24},{20,28},{12,20},{4,12},{1,5},{9... | collective-permute-start | bytes 245768 | tf_op jit(solution)/shard_map/ppermute | solution.py:329
  (31 other events, 206.5 us)
